TPU v7x, 32 devices: a whole 2x2x4 slice. The times are simulated.
32 devices in a mesh: ctx: 16 (over z, x, core), wt: 2 (over y).
Axes of the slice: x: 2, y: 2, z: 4, core: 2. Of those that a mesh axis runs over, the one named last changes fastest.
Arguments:
- content: bfloat16 [2, 2, 1024, 768], P('wt', None, 'ctx'), may hold values from -6 to 6
- query_stream: bfloat16 [2, 384, 768], P('wt', 'ctx'), may hold values from -6 to 6
- token_order: int32 [2, 2048], P('wt'), may hold values from 0 to 2047, each once within a row
- targets: int32 [2, 384], P('wt'), may hold values from 1 to 2047, as said below
- query_weight: bfloat16 [768, 768], P(None, 'wt'), may hold values from -0.21875 to 0.21875
- key_weight: bfloat16 [768, 768], P(None, 'wt'), may hold values from -0.21875 to 0.21875
- value_weight: bfloat16 [768, 768], P(None, 'wt'), may hold values from -0.21875 to 0.21875
- output_weight: bfloat16 [768, 768], P(None, 'wt'), may hold values from -1.75 to 1.75
- query_bias: bfloat16 [768], P('wt'), may hold values from -3 to 3
- value_bias: bfloat16 [768], P('wt'), may hold values from -2 to 2
- output_bias: bfloat16 [768], P('wt'), may hold values from -3 to 3
- bias_table: bfloat16 [32, 12], P('wt'), may hold values from -4 to 4
- first_gain: bfloat16 [768], P('wt'), may hold values from 0.099609375 to 1.8984375
- first_shift: bfloat16 [768], P('wt'), may hold values from -2 to 2
- inner_weight: bfloat16 [768, 3072], P(None, 'wt'), may hold values from -0.21875 to 0.21875
- inner_bias: bfloat16 [3072], P('wt'), may hold values from -3 to 3
- outer_weight: bfloat16 [3072, 768], P(None, 'wt'), may hold values from -0.109375 to 0.109375
- outer_bias: bfloat16 [768], P('wt'), may hold values from -3 to 3
- second_gain: bfloat16 [768], P('wt'), may hold values from 0.099609375 to 1.8984375
- second_shift: bfloat16 [768], P('wt'), may hold values from -2 to 2
- content_cotangent: bfloat16 [2, 2, 1024, 768], P('wt', None, 'ctx'), may hold values from -6 to 6
- query_cotangent: bfloat16 [2, 384, 768], P('wt', 'ctx'), may hold values from -6 to 6
Outputs:
- content_result: bfloat16 [2, 2, 1024, 768], P('wt', None, 'ctx')
- query_result: bfloat16 [2, 384, 768], P('wt', 'ctx')
- content_gradient: float32 [2, 2, 1024, 768], P('wt', None, 'ctx')
- query_gradient: float32 [2, 384, 768], P('wt', 'ctx')
- query_weight_gradient: float32 [768, 768], P(None, 'wt')
- key_weight_gradient: float32 [768, 768], P(None, 'wt')
- value_weight_gradient: float32 [768, 768], P(None, 'wt')
- output_weight_gradient: float32 [768, 768], P(None, 'wt')
- query_bias_gradient: float32 [768], P('wt')
- value_bias_gradient: float32 [768], P('wt')
- output_bias_gradient: float32 [768], P('wt')
- bias_table_gradient: float32 [32, 12], P('wt')
- first_gain_gradient: float32 [768], P('wt')
- first_shift_gradient: float32 [768], P('wt')
- inner_weight_gradient: float32 [768, 3072], P(None, 'wt')
- inner_bias_gradient: float32 [3072], P('wt')
- outer_weight_gradient: float32 [3072, 768], P(None, 'wt')
- outer_bias_gradient: float32 [768], P('wt')
- second_gain_gradient: float32 [768], P('wt')
- second_shift_gradient: float32 [768], P('wt')
Inputs may be any that keep to these rules, and one draw needn't show every extreme that they name: `token_order`: each row is a permutation of the initial positions 0 to 2047. `targets`: places of the predicted tokens in the permuted order, all different within a sequence.
All inputs are finite; a program needn't handle non-finite values.
Results may differ from a plain program's by a relative error of at most 0.015.
The roundings to bfloat16 on the way count: a program that leaves them out, or rounds other values in their place, can miss the bound.
Values may be sent and summed in bfloat16 or wider, within the bound.
No kernel may reach another device: no remote copies, remote signals or barrier semaphores. Data moves between devices by JAX's collectives and lax.ppermute only.
A program may use at most 256 MiB of HBM per device.

v0:
```python
import functools

import jax
import jax.numpy as jnp
from jax import lax
from jax.experimental import pallas as pl
from jax.experimental.layout import Layout, with_layout_constraint
from jax.experimental.pallas import tpu as pltpu
from jax.sharding import PartitionSpec as P

BF16 = jnp.bfloat16
F32 = jnp.float32
FAR_EDGES = (12, 16, 23, 32, 46, 64, 91)
NEGATIVE = -1e30
TILE = 256
ROWS = 640
GROUP = 16


def layer_norm(hidden_rows, gain_row, shift_row):
    average = jnp.mean(hidden_rows, axis=-1, keepdims=True)
    centered = hidden_rows - average
    variance = jnp.mean(centered * centered, axis=-1, keepdims=True)
    return centered * lax.rsqrt(variance + 1e-05) * gain_row + shift_row


def norm_of_sum(residual, branch_value, gain_row, shift_row):
    return layer_norm(residual + branch_value, gain_row, shift_row)


def gelu_exact(values):
    return jax.nn.gelu(values, approximate=False)


def dot(left, right):
    return jnp.dot(left, right, preferred_element_type=F32)


def contract_rows(left, right):
    return lax.dot_general(left, right, (((0,), (0,)), ((), ())), preferred_element_type=F32)


def times_transpose(left, right):
    return lax.dot_general(left, right, (((1,), (1,)), ((), ())), preferred_element_type=F32)


def transpose_low(block):
    return block.astype(F32).T.astype(BF16)


def tile_branches(branch_index, process):
    for branch in range(4):
        pl.when(branch_index == branch)(functools.partial(process, 128 * branch))


def forward_kernel(call, count, heads, *refs):
    place_ref, query_ref, kv_ref, anchor_ref, row_ref, table_ref = refs[:6]
    refs = refs[6:]
    if call == 1:
        max_in, sum_in, mixed_in = refs[4:7]
        refs = refs[7:]
    exp_ref, bucket_ref, low_ref, max_ref, run_max, run_sum, mixed_t_ref = refs[:7]
    refs = refs[7:]
    if call == 1:
        mixed_ref, total_ref = refs[:2]
        refs = refs[2:]
    query_z, prob_ref, scale_ref = refs
    step = pl.program_id(0)
    branch_index = step // count
    tile_index = branch_index * (2 * count) + call * count + step % count

    @pl.when(step == 0)
    def _():
        query_t = transpose_low(query_ref[...])
        part = lax.broadcasted_iota(jnp.int32, (256, ROWS), 0) // 64
        for head in range(heads):
            query_z[head] = jnp.where(part == head, query_t.astype(F32), 0.0).astype(BF16)
        if call == 0:
            run_max[...] = jnp.full(run_max.shape, NEGATIVE, F32)
            run_sum[...] = jnp.zeros(run_sum.shape, F32)
            mixed_t_ref[...] = jnp.zeros(mixed_t_ref.shape, F32)
        else:
            run_max[...] = max_in[...]
            run_sum[...] = sum_in[...]
            mixed_t_ref[...] = mixed_in[...]

    place_sign = jnp.where(branch_index < 2, 1, -1)
    keys_values = kv_ref[...].reshape(TILE, 384)
    value_t = transpose_low(keys_values[:, 128:384])

    def process(offset):
        chunks = (ROWS - offset) // 128
        for head in range(heads):
            exp_ref[head, :, offset:] = dot(keys_values[:, 0:256], query_z[head, :, offset:])

        def bias_group(group, tops):
            start = pl.multiple_of(group * GROUP, GROUP)
            keys = anchor_ref[pl.ds(start, GROUP), :]
            row = start % 64 + lax.broadcasted_iota(jnp.int32, (GROUP, 128), 0)
            place = place_ref[tile_index * (TILE // 64) + start // 64] + place_sign * row
            new_tops = []
            for chunk in range(chunks):
                lanes = slice(offset + chunk * 128, offset + chunk * 128 + 128)
                relative = keys - row_ref[0:1, lanes]
                magnitude = jnp.abs(relative)
                bucket = jnp.minimum(magnitude, 8)
                for edge in FAR_EDGES:
                    bucket = bucket + jnp.where(magnitude >= edge, 1, 0)
                bucket = bucket + jnp.where(relative > 0, 16, 0)
                bucket_ref[pl.ds(start, GROUP), lanes] = bucket.astype(F32).astype(BF16)
                low_ref[pl.ds(start, GROUP), lanes] = (bucket & 3).astype(F32).astype(BF16)
                allowed = place < row_ref[1:2, lanes]
                for head in range(heads):
                    table = jnp.broadcast_to(table_ref[head : head + 1, :], (8, 128))
                    bias = jnp.concatenate(
                        [
                            jnp.take_along_axis(table, bucket[0:8], axis=1),
                            jnp.take_along_axis(table, bucket[8:16], axis=1),
                        ],
                        axis=0,
                    )
                    scores = exp_ref[head, pl.ds(start, GROUP), lanes] + bias
                    scores = jnp.where(allowed, scores, NEGATIVE)
                    exp_ref[head, pl.ds(start, GROUP), lanes] = scores
                    top = tops[chunk * heads + head]
                    new_tops.append(jnp.maximum(top, jnp.maximum(scores[0:8], scores[8:16])))
            return tuple(new_tops)

        tops = lax.fori_loop(
            0,
            TILE // GROUP,
            bias_group,
            tuple(jnp.full((8, 128), NEGATIVE, F32) for _ in range(chunks * heads)),
            unroll=2,
        )
        for chunk in range(chunks):
            lanes = slice(offset + chunk * 128, offset + chunk * 128 + 128)
            for head in range(heads):
                top = jnp.max(tops[chunk * heads + head], axis=0, keepdims=True)
                old = run_max[head : head + 1, lanes]
                new = jnp.maximum(old, top)
                scale_ref[head : head + 1, lanes] = jnp.exp(old - new)
                run_max[head : head + 1, lanes] = new
        max_ref[0] = run_max[...]

        def exp_group(group, sums):
            start = pl.multiple_of(group * GROUP, GROUP)
            new_sums = []
            for chunk in range(chunks):
                lanes = slice(offset + chunk * 128, offset + chunk * 128 + 128)
                for head in range(heads):
                    terms = jnp.exp(
                        exp_ref[head, pl.ds(start, GROUP), lanes] - run_max[head : head + 1, lanes]
                    )
                    exp_ref[head, pl.ds(start, GROUP), lanes] = terms
                    prob_ref[head, pl.ds(start, GROUP), lanes] = terms.astype(BF16)
                    new_sums.append(sums[chunk * heads + head] + (terms[0:8] + terms[8:16]))
            return tuple(new_sums)

        sums = lax.fori_loop(
            0,
            TILE // GROUP,
            exp_group,
            tuple(jnp.zeros((8, 128), F32) for _ in range(chunks * heads)),
        )
        for chunk in range(chunks):
            lanes = slice(offset + chunk * 128, offset + chunk * 128 + 128)
            for head in range(heads):
                run_sum[head : head + 1, lanes] = run_sum[head : head + 1, lanes] * scale_ref[
                    head : head + 1, lanes
                ] + jnp.sum(sums[chunk * heads + head], axis=0, keepdims=True)
        for head in range(heads):
            rows = slice(64 * head, 64 * head + 64)
            mixed_t_ref[rows, offset:] = mixed_t_ref[rows, offset:] * scale_ref[
                head : head + 1, offset:
            ] + dot(value_t[64 + 64 * head : 128 + 64 * head], prob_ref[head, :, offset:])

    tile_branches(branch_index, process)

    if call == 1:

        @pl.when(step == 4 * count - 1)
        def _():
            for head in range(heads):
                rows = slice(64 * head, 64 * head + 64)
                mixed_t_ref[rows, :] = mixed_t_ref[rows, :] / run_sum[head : head + 1, :]
                total_ref[head : head + 1, :] = run_max[head : head + 1, :] + jnp.log(
                    run_sum[head : head + 1, :]
                )
            mixed_ref[...] = mixed_t_ref[...].T.astype(BF16)


def attention_forward(
    call, query256, keys_values, key_anchor, block_places, row_info, tables, previous, heads
):
    count = keys_values.shape[0] // 2
    tiles = 8 * count
    total_keys = tiles * TILE

    def tile_of(s):
        return (s // count) * (2 * count) + call * count + s % count

    def whole(shape):
        return pl.BlockSpec(shape, lambda s, p: (0,) * len(shape))

    in_specs = [
        whole((ROWS, 256)),
        pl.BlockSpec((2, 2, 64, 384), lambda s, p: (s % count, s // count, 0, 0)),
        pl.BlockSpec((TILE, 128), lambda s, p: (tile_of(s), 0)),
        whole((8, ROWS)),
        whole((8, 128)),
    ]
    out_specs = [
        pl.BlockSpec((heads, TILE, ROWS), lambda s, p: (0, tile_of(s), 0)),
        pl.BlockSpec((TILE, ROWS), lambda s, p: (tile_of(s), 0)),
        pl.BlockSpec((TILE, ROWS), lambda s, p: (tile_of(s), 0)),
        pl.BlockSpec((1, 8, ROWS), lambda s, p: (tile_of(s), 0, 0)),
        whole((8, ROWS)),
        whole((8, ROWS)),
        whole((192, ROWS)),
    ]
    out_shape = [
        jax.ShapeDtypeStruct((heads, total_keys, ROWS), F32),
        jax.ShapeDtypeStruct((total_keys, ROWS), BF16),
        jax.ShapeDtypeStruct((total_keys, ROWS), BF16),
        jax.ShapeDtypeStruct((tiles, 8, ROWS), F32),
        jax.ShapeDtypeStruct((8, ROWS), F32),
        jax.ShapeDtypeStruct((8, ROWS), F32),
        jax.ShapeDtypeStruct((192, ROWS), F32),
    ]
    aliases = {}
    if call == 1:
        in_specs += [pl.BlockSpec(memory_space=pl.ANY)] * 4
        in_specs += [whole((8, ROWS)), whole((8, ROWS)), whole((192, ROWS))]
        out_specs += [whole((ROWS, 192)), whole((8, ROWS))]
        out_shape += [
            jax.ShapeDtypeStruct((ROWS, 192), BF16),
            jax.ShapeDtypeStruct((8, ROWS), F32),
        ]
        aliases = {6: 0, 7: 1, 8: 2, 9: 3}
    return pl.pallas_call(
        functools.partial(forward_kernel, call, count, heads),
        grid_spec=pltpu.PrefetchScalarGridSpec(
            num_scalar_prefetch=1,
            grid=(4 * count,),
            in_specs=in_specs,
            out_specs=out_specs,
            scratch_shapes=[
                pltpu.VMEM((heads, 256, ROWS), BF16),
                pltpu.VMEM((heads, TILE, ROWS), BF16),
                pltpu.VMEM((8, ROWS), F32),
            ],
        ),
        out_shape=out_shape,
        input_output_aliases=aliases,
        compiler_params=pltpu.CompilerParams(
            dimension_semantics=("arbitrary",), vmem_limit_bytes=32 << 20
        ),
        cost_estimate=pl.CostEstimate(
            flops=14 << 30, bytes_accessed=12 << 20, transcendentals=2 << 20
        ),
        name="attention_forward",
    )(block_places, query256, keys_values, key_anchor, row_info, tables, *previous)


def backward_kernel(branch, heads, *refs):
    refs = list(refs)
    if branch > 0:
        del refs[11]
    backward_tile(branch, heads, *refs)


def backward_tile(
    branch,
    heads,
    exp_ref,
    bucket_ref,
    low_ref,
    max_ref,
    total_ref,
    query_ref,
    grad_ref,
    mixed_t_ref,
    kv_ref,
    dquery_in,
    dtable_in,
    dquery_ref,
    dtable_ref,
    dkv_ref,
    grad_z,
    query_n,
    grad_n,
    dprob_ref,
    dscore_ref,
    prob_ref,
    high_hot,
    low_parts,
    delta_ref,
    scale_ref,
):
    tile_index = pl.program_id(0)
    offset = 128 * branch
    chunks = (ROWS - offset) // 128

    @pl.when(tile_index == 0)
    def _():
        grad_t = grad_ref[offset:, :].astype(F32).T
        part = lax.broadcasted_iota(jnp.int32, (256, ROWS - offset), 0) // 64
        lane_part = lax.broadcasted_iota(jnp.int32, (ROWS - offset, 256), 1) // 64
        for head in range(heads):
            grad_z[head, :, offset:] = jnp.where(part == head + 1, grad_t, 0.0).astype(BF16)
            query_n[head, offset:, :] = jnp.where(
                lane_part == head, query_ref[offset:, :].astype(F32), 0.0
            ).astype(BF16)
            grad_n[head, offset:, :] = jnp.where(
                lane_part == head + 1, grad_ref[offset:, :].astype(F32), 0.0
            ).astype(BF16)
            delta_ref[head : head + 1, offset:] = jnp.sum(
                grad_t[64 + 64 * head : 128 + 64 * head]
                * mixed_t_ref[64 * head : 64 * head + 64, offset:],
                axis=0,
                keepdims=True,
            )
        if branch == 0:
            dquery_ref[...] = jnp.zeros(dquery_ref.shape, F32)
            dtable_ref[...] = jnp.zeros(dtable_ref.shape, F32)
        else:
            dquery_ref[...] = dquery_in[...]
            dtable_ref[...] = dtable_in[...]

    keys_values = kv_ref[...].reshape(TILE, 384)
    key_t = transpose_low(keys_values[:, 0:256])
    for head in range(heads):
        dprob_ref[head, :, offset:] = dot(keys_values[:, 128:384], grad_z[head, :, offset:])
        scale_ref[head : head + 1, offset:] = jnp.exp(
            max_ref[0, head : head + 1, offset:] - total_ref[head : head + 1, offset:]
        )

    def build(group, slot):
        start = pl.multiple_of(group * GROUP, GROUP)
        one = jnp.ones((GROUP, 128), BF16)
        zero = jnp.zeros((GROUP, 128), BF16)
        for chunk in range(chunks):
            lanes = slice(offset + chunk * 128, offset + chunk * 128 + 128)
            bucket = bucket_ref[pl.ds(start, GROUP), lanes]
            low = low_ref[pl.ds(start, GROUP), lanes]
            for high in range(8):
                hot = jnp.where(bucket >= jnp.asarray(4 * high, BF16), one, zero)
                high_hot[slot, GROUP * high : GROUP * high + GROUP, lanes] = hot
            matches = [low == jnp.asarray(value, BF16) for value in range(4)]
            for head in range(heads):
                prob = (
                    exp_ref[head, pl.ds(start, GROUP), lanes] * scale_ref[head : head + 1, lanes]
                )
                dscore = prob * (
                    dprob_ref[head, pl.ds(start, GROUP), lanes]
                    - delta_ref[head : head + 1, lanes]
                )
                dscore_low = dscore.astype(BF16)
                prob_ref[head, pl.ds(start, GROUP), lanes] = prob.astype(BF16)
                dscore_ref[head, pl.ds(start, GROUP), lanes] = dscore_low
                for value in range(4):
                    row = GROUP * (value * heads + head)
                    low_parts[slot, row : row + GROUP, lanes] = jnp.where(
                        matches[value], dscore_low, zero
                    )

    def product(slot):
        return times_transpose(high_hot[slot, :, offset:], low_parts[slot, :, offset:])

    groups = TILE // GROUP
    build(0, 0)
    build(1, 1)

    def step(index, carry):
        even = product(0) + product(1)
        build(4 * index + 2, 2)
        build(4 * index + 3, 3)
        odd = product(2) + product(3)
        following = jnp.minimum(4 * index + 4, groups - 2)
        build(following, 0)
        build(following + 1, 1)
        dtable_ref[...] = dtable_ref[...] + (even + odd)
        return carry

    lax.fori_loop(0, groups // 4, step, 0)
    dkey = jnp.zeros((TILE, 256), F32)
    dvalue = jnp.zeros((TILE, 256), F32)
    for head in range(heads):
        dkey = dkey + dot(dscore_ref[head, :, offset:], query_n[head, offset:, :])
        dvalue = dvalue + dot(prob_ref[head, :, offset:], grad_n[head, offset:, :])
        rows = slice(64 * head, 64 * head + 64)
        dquery_ref[rows, offset:] = dquery_ref[rows, offset:] + dot(
            key_t[rows], dscore_ref[head, :, offset:]
        )
    dkv_ref[:, :, :, 0:128] = dkey[:, 0:128].reshape(2, 2, 64, 128)
    dkv_ref[:, :, :, 128:256] = (dkey[:, 128:256] + dvalue[:, 0:128]).reshape(2, 2, 64, 128)
    dkv_ref[:, :, :, 256:384] = dvalue[:, 128:256].reshape(2, 2, 64, 128)


def attention_backward(branch, saved, query256, grad256, mixed_t, keys_values, carried, heads):
    exps, buckets, lows, maxima, totals = saved
    members = keys_values.shape[0]
    tiles = members // 2
    first = branch * tiles
    def whole(shape):
        return pl.BlockSpec(shape, lambda t: (0,) * len(shape))

    in_specs = [
        pl.BlockSpec((heads, TILE, ROWS), lambda t: (0, first + t, 0)),
        pl.BlockSpec((TILE, ROWS), lambda t: (first + t, 0)),
        pl.BlockSpec((TILE, ROWS), lambda t: (first + t, 0)),
        pl.BlockSpec((1, 8, ROWS), lambda t: (first + t, 0, 0)),
        whole((8, ROWS)),
        whole((ROWS, 256)),
        whole((ROWS, 256)),
        whole((192, ROWS)),
        pl.BlockSpec((2, 2, 64, 384), lambda t: (t, branch, 0, 0)),
    ]
    if branch == 0:
        carried = (totals, totals)
        in_specs += [whole((8, ROWS)), whole((8, ROWS))]
        aliases = {}
    else:
        in_specs += [
            whole((192, ROWS)),
            whole((128, 64 * heads)),
            pl.BlockSpec(memory_space=pl.ANY),
        ]
        aliases = {11: 2}
    return pl.pallas_call(
        functools.partial(backward_kernel, branch, heads),
        grid=(tiles,),
        in_specs=in_specs,
        out_specs=[
            whole((192, ROWS)),
            whole((128, 64 * heads)),
            pl.BlockSpec((2, 2, 64, 384), lambda t: (t, branch, 0, 0)),
        ],
        out_shape=[
            jax.ShapeDtypeStruct((192, ROWS), F32),
            jax.ShapeDtypeStruct((128, 64 * heads), F32),
            jax.ShapeDtypeStruct((members, 8, 64, 384), F32),
        ],
        input_output_aliases=aliases,
        scratch_shapes=[
            pltpu.VMEM((heads, 256, ROWS), BF16),
            pltpu.VMEM((heads, ROWS, 256), BF16),
            pltpu.VMEM((heads, ROWS, 256), BF16),
            pltpu.VMEM((heads, TILE, ROWS), F32),
            pltpu.VMEM((heads, TILE, ROWS), BF16),
            pltpu.VMEM((heads, TILE, ROWS), BF16),
            pltpu.VMEM((4, 128, ROWS), BF16),
            pltpu.VMEM((4, 64 * heads, ROWS), BF16),
            pltpu.VMEM((8, ROWS), F32),
            pltpu.VMEM((8, ROWS), F32),
        ],
        compiler_params=pltpu.CompilerParams(
            dimension_semantics=("arbitrary",), vmem_limit_bytes=58 << 20
        ),
        cost_estimate=pl.CostEstimate(
            flops=8 << 30, bytes_accessed=6 << 20, transcendentals=1 << 18
        ),
        name="attention_backward",
    )(exps, buckets, lows, maxima, totals, query256, grad256, mixed_t, keys_values, *carried)


def arrange_kernel(half_rows, query_rows, plane_ref, *refs):
    block_refs, out_ref, rows_ref = refs[:4], refs[4], refs[5]
    rows_ref[...] = jnp.zeros(rows_ref.shape, F32)
    for distance in range(4):
        plane = plane_ref[0] ^ distance
        block = block_refs[distance][...].astype(F32)
        start = pl.multiple_of(plane * half_rows, half_rows)
        rows_ref[pl.ds(start, half_rows), 64:256] = block[:half_rows, 0:192]
        start = pl.multiple_of((7 - plane) * half_rows, half_rows)
        rows_ref[pl.ds(start, half_rows), 64:256] = block[:half_rows, 192:384]
        start = pl.multiple_of(8 * half_rows + plane * query_rows, 8)
        rows_ref[pl.ds(start, query_rows), 64:256] = block[half_rows:, 0:192]
    out_ref[...] = rows_ref[...].astype(BF16)


def arrange_rows(blocks, plane, half_rows, query_rows):
    return pl.pallas_call(
        functools.partial(arrange_kernel, half_rows, query_rows),
        in_specs=[pl.BlockSpec(memory_space=pltpu.SMEM)]
        + [pl.BlockSpec(memory_space=pltpu.VMEM)] * 4,
        out_specs=pl.BlockSpec(memory_space=pltpu.VMEM),
        out_shape=jax.ShapeDtypeStruct((ROWS, 256), BF16),
        scratch_shapes=[pltpu.VMEM((ROWS, 256), F32)],
        name="arrange_rows",
    )(plane[None], *blocks)


def widen_kernel(group, order_ref, near_ref, far_ref, *out_refs):
    step = pl.program_id(0) ^ (order_ref[0] // group)
    half_steps = pl.num_programs(0) // 2
    inner = order_ref[0] % group

    def from_pieces(pieces_ref):
        rows = pieces_ref.shape[-2]
        for k in range(group):
            start = 0
            for out_ref in out_refs:
                columns = out_ref.shape[-1]
                lanes = slice(start, start + columns)
                if len(pieces_ref.shape) == 4:
                    for s in range(2):
                        block = pieces_ref[k ^ inner, s ^ order_ref[1], :, lanes]
                        out_ref[s, k * rows : (k + 1) * rows, :] = block.astype(F32)
                else:
                    block = pieces_ref[k ^ inner, :, lanes]
                    out_ref[k * rows : (k + 1) * rows, :] = block.astype(F32)
                start += columns

    pl.when(step < half_steps)(lambda: from_pieces(near_ref))
    pl.when(step >= half_steps)(lambda: from_pieces(far_ref))


def widen_rows(near, far, order, columns):
    half, rows, width = near.shape[0], near.shape[-2], near.shape[-1]
    sides = near.shape[1:-2]
    group = min(4, half)
    if rows % 16 != 0:
        pieces = jnp.concatenate([near, far], axis=0)
        position = jnp.arange(2 * half, dtype=jnp.int32) ^ order[0]
        whole = jnp.take(pieces, position, axis=0).astype(F32)
        if sides:
            whole = jnp.swapaxes(jnp.where(order[1] == 1, whole[:, ::-1], whole), 0, 1)
        whole = whole.reshape(sides + (2 * half * rows, width))
        ends = [sum(columns[: i + 1]) for i in range(len(columns))]
        return [whole[..., end - c : end] for end, c in zip(ends, columns)]
    zeros = (0,) * (len(sides) + 2)
    half_steps = half // group

    def piece_map(part):
        def index(r, o):
            order_step = o[0] // group
            first = jnp.where(order_step >= half_steps, 1 - part, part) * half_steps
            inside = jnp.clip(r, first, first + half_steps - 1)
            return ((inside ^ order_step) % half_steps,) + zeros

        return index

    def out_map(r, o):
        return (0,) * len(sides) + (r, 0)

    return pl.pallas_call(
        functools.partial(widen_kernel, group),
        grid_spec=pltpu.PrefetchScalarGridSpec(
            num_scalar_prefetch=1,
            grid=(2 * half_steps,),
            in_specs=[pl.BlockSpec((group,) + near.shape[1:], piece_map(part)) for part in range(2)],
            out_specs=[pl.BlockSpec(sides + (group * rows, c), out_map) for c in columns],
        ),
        out_shape=[jax.ShapeDtypeStruct(sides + (2 * half * rows, c), F32) for c in columns],
        compiler_params=pltpu.CompilerParams(
            dimension_semantics=("arbitrary",), vmem_limit_bytes=24 << 20
        ),
        cost_estimate=pl.CostEstimate(
            flops=0, bytes_accessed=6 * near.size * 2, transcendentals=0
        ),
        name="widen_rows",
    )(order, near, far)


def widen_heads_kernel(order_ref, pieces_ref, *out_refs):
    odd = order_ref[1] == 1
    first, second = pieces_ref[0, 0], pieces_ref[0, 1]
    low = jnp.where(odd, second.astype(F32), first.astype(F32))
    high = jnp.where(odd, first.astype(F32), second.astype(F32))
    size = low.shape[1] // 3
    for i, out_ref in enumerate(out_refs):
        lanes = slice(i * size, (i + 1) * size)
        out_ref[...] = jnp.concatenate([low[:, lanes], high[:, lanes]], axis=1)


def widen_heads(pieces, order, odd):
    count, _, rows, width = pieces.shape
    columns = 2 * width // 3
    return pl.pallas_call(
        widen_heads_kernel,
        grid_spec=pltpu.PrefetchScalarGridSpec(
            num_scalar_prefetch=1,
            grid=(count,),
            in_specs=[pl.BlockSpec((1, 2, rows, width), lambda r, o: (r ^ o[0], 0, 0, 0))],
            out_specs=[pl.BlockSpec((rows, columns), lambda r, o: (r, 0))] * 3,
        ),
        out_shape=[jax.ShapeDtypeStruct((count * rows, columns), F32)] * 3,
        compiler_params=pltpu.CompilerParams(dimension_semantics=("arbitrary",)),
        cost_estimate=pl.CostEstimate(
            flops=0, bytes_accessed=12 * count * rows * width, transcendentals=0
        ),
        name="widen_heads",
    )(jnp.stack([order, odd]), pieces)


def pack_kernel(*refs):
    out_ref = refs[-1]
    rows = [ref[...].reshape(1, -1).astype(F32) for ref in refs[:8]]
    out_ref[...] = jnp.zeros(out_ref.shape, BF16)
    out_ref[0:8, :] = jnp.concatenate(rows, axis=0).astype(BF16)
    table = refs[8][...].astype(F32)
    lanes = jnp.zeros((table.shape[0], 128 - table.shape[1]), F32)
    out_ref[16:32, 0:128] = jnp.concatenate([table, lanes], axis=1).astype(BF16)


def pack_vectors(vectors, table):
    vmem = pl.BlockSpec(memory_space=pltpu.VMEM)
    return pl.pallas_call(
        pack_kernel,
        in_specs=[vmem] * 9,
        out_specs=vmem,
        out_shape=jax.ShapeDtypeStruct((32, vectors[0].shape[0]), BF16),
        name="pack_vectors",
    )(*vectors, table)


def unpack_kernel(heads, where_ref, own_ref, other_ref, full_ref, bias_ref, table_ref, turned_ref):
    side = where_ref[0] == 1
    own, other = own_ref[...].astype(F32), other_ref[...].astype(F32)
    low, high = jnp.where(side, other, own), jnp.where(side, own, other)
    full = jnp.concatenate([low[0:8], high[0:8]], axis=1)
    full_ref[...] = full
    both = jnp.concatenate([low[16:32, 0:128], high[16:32, 0:128]], axis=0)
    square = jnp.concatenate([both, jnp.zeros((96, 128), F32)], axis=0)
    turned_ref[...] = square.T
    bias_ref[...] = jnp.zeros(bias_ref.shape, F32)
    table_ref[...] = jnp.zeros(table_ref.shape, F32)
    for plane in range(4):

        @pl.when(where_ref[1] == plane)
        def _(plane=plane):
            lanes = slice(192 * plane, 192 * plane + 192)
            bias_ref[0:1, 0:192] = full[0:1, lanes]
            bias_ref[1:2, 192:384] = full[1:2, lanes]
            table_ref[0:heads, :] = turned_ref[heads * plane : heads * plane + heads, :]


def unpack_vectors(own, other, side, plane, heads):
    vmem = pl.BlockSpec(memory_space=pltpu.VMEM)
    half = own.shape[1]
    return pl.pallas_call(
        functools.partial(unpack_kernel, heads),
        in_specs=[pl.BlockSpec(memory_space=pltpu.SMEM)] + [vmem] * 2,
        out_specs=[vmem] * 3,
        out_shape=[
            jax.ShapeDtypeStruct((8, 2 * half), F32),
            jax.ShapeDtypeStruct((8, half), F32),
            jax.ShapeDtypeStruct((8, 128), F32),
        ],
        scratch_shapes=[pltpu.VMEM((128, 128), F32)],
        name="unpack_vectors",
    )(jnp.stack([side, plane]), own, other)


def after(value, *earlier):
    return lax.optimization_barrier((value,) + earlier)[0]


def row_major(value):
    return with_layout_constraint(value, Layout(major_to_minor=tuple(range(value.ndim))))


class Chain:
    def __init__(self, state, stages):
        self.state, self.stages = state, stages
        self.leave()

    def leave(self):
        if self.stages:
            self.sent, self.kept = self.stages[0][0](self.state)
            self.arrived = self.stages[0][1](self.sent)

    def advance(self, token):
        kept = jax.tree.map(lambda leaf: after(leaf, token), self.kept)
        self.state = self.stages[0][2](kept, self.arrived)
        self.stages = self.stages[1:]
        self.leave()
        return self.sent if self.stages else jax.tree.leaves(self.state)[0]

    def drain(self, token):
        while self.stages:
            token = self.advance(token)
        return token


def reverse_bits(value, count):
    result = jnp.zeros_like(value)
    bit, mirrored = 1, count // 2
    while bit < count:
        result = result + jnp.where((value & bit) != 0, mirrored, 0)
        bit, mirrored = bit * 2, mirrored // 2
    return result


def body(
    content,
    query_stream,
    token_order,
    targets,
    query_weight,
    key_weight,
    value_weight,
    output_weight,
    query_bias,
    value_bias,
    output_bias,
    bias_table,
    first_gain,
    first_shift,
    inner_weight,
    inner_bias,
    outer_weight,
    outer_bias,
    second_gain,
    second_shift,
    content_cotangent,
    query_cotangent,
):
    ctx = lax.axis_size("ctx")
    index = lax.axis_index("ctx")
    side = lax.axis_index("wt")
    members = ctx // 4
    plane = index // members
    member = index % members
    half_rows = content.shape[2]
    tok_rows = 2 * half_rows
    query_rows = query_stream.shape[1]
    rows_dev = tok_rows + query_rows
    width = content.shape[3]
    heads = bias_table.shape[1]
    my_heads = heads // 4
    head_width = my_heads * (width // heads)
    half_width = width // 2
    seq_length = tok_rows * ctx
    half_length = seq_length // 2
    order_row = token_order[0]
    target_row = targets[0]
    core_bit = (index & 1) == 1

    def swap(value, bit):
        return lax.ppermute(value, "ctx", [(i, i ^ bit) for i in range(ctx)])

    def swap_side(value):
        return lax.ppermute(value, "wt", [(0, 1), (1, 0)])

    def order_two(flag, mine, other, axis):
        low = jnp.where(flag, other, mine)
        high = jnp.where(flag, mine, other)
        return jnp.concatenate([low, high], axis=axis)

    def half_of_core(value):
        rows = value.shape[0] // 2
        return lax.dynamic_slice_in_dim(value, (index & 1) * rows, rows, 0)

    def both_cores(arrived):
        return order_two(core_bit, arrived, swap(arrived, 1), 0)

    def by_distance(blocks):
        flag = (plane & 1) == 1
        blocks = [jnp.where(flag, blocks[d ^ 1], blocks[d]) for d in range(4)]
        flag = (plane & 2) == 2
        return [jnp.where(flag, blocks[d ^ 2], blocks[d]) for d in range(4)]

    def exchange_planes(blocks):
        sent = by_distance(blocks)
        arrived = [sent[0]] + [swap(sent[d], d * members) for d in range(1, 4)]
        return by_distance(arrived)

    def pack_rows(rows):
        top = jnp.concatenate([rows[:half_rows], rows[half_rows:tok_rows]], axis=1)
        bottom = jnp.concatenate([rows[tok_rows:], jnp.zeros_like(rows[tok_rows:])], axis=1)
        return jnp.concatenate([top, bottom], axis=0)

    def unpack_rows(packed):
        return jnp.concatenate(
            [
                packed[:half_rows, :head_width],
                packed[:half_rows, head_width:],
                packed[half_rows:, :head_width],
            ],
            axis=0,
        )

    def plane_rows(blocks):
        pad = ROWS - 4 * rows_dev
        return jnp.concatenate(
            [blocks[d][:half_rows] for d in range(4)]
            + [blocks[3 - d][half_rows:tok_rows] for d in range(4)]
            + [blocks[d][tok_rows:] for d in range(4)]
            + [jnp.zeros((pad, blocks[0].shape[1]), blocks[0].dtype)],
            axis=0,
        )

    def split_rows(rows):
        blocks = []
        for d in range(4):
            parts = [
                rows[d * half_rows : (d + 1) * half_rows],
                rows[(7 - d) * half_rows : (8 - d) * half_rows],
            ]
            if rows.shape[0] > 4 * tok_rows:
                start = 4 * tok_rows + d * query_rows
                parts.append(rows[start : start + query_rows])
            blocks.append(jnp.concatenate(parts, axis=0))
        return blocks

    local_content = content[0].reshape(tok_rows, width)
    stacked = jnp.concatenate([local_content, query_stream[0]], axis=0)
    arrived_rows = [stacked] + [swap(stacked, d * members) for d in range(1, 4)]
    owner = plane // 2
    odd_plane = (plane & 1) == 1
    side_flag = side == 1
    shards = [query_weight, key_weight, value_weight]
    near_own = jnp.concatenate(
        [jnp.where(odd_plane, s[:, head_width:], s[:, :head_width]) for s in shards], axis=1
    )
    near_sent = half_of_core(near_own)
    near_other = both_cores(swap_side(near_sent))
    vectors = [
        query_bias,
        value_bias,
        output_bias,
        first_gain,
        first_shift,
        outer_bias,
        second_gain,
        second_shift,
    ]
    own_vectors = pack_vectors(vectors, bias_table)
    other_vectors = swap_side(own_vectors)
    full_vectors, head_bias, tables = unpack_vectors(
        own_vectors, other_vectors, side, plane, my_heads
    )
    (
        full_output_bias,
        full_first_gain,
        full_first_shift,
        full_outer_bias,
        full_second_gain,
        full_second_shift,
    ) = [full_vectors[i : i + 1] for i in range(2, 8)]
    buckets = 2 * bias_table.shape[0]

    places = jnp.arange(half_length, dtype=jnp.int32)
    key_place = jnp.concatenate(
        [places, (seq_length - 1 - places).reshape(4, -1)[::-1].reshape(-1)]
    )
    key_anchor = jnp.concatenate(
        [
            order_row[:half_length],
            order_row[half_length:][::-1].reshape(4, -1)[::-1].reshape(-1),
        ]
    )

    def of_member(array, count):
        return lax.dynamic_index_in_dim(
            array.reshape(-1, members, count), member, 1, keepdims=False
        ).reshape(-1)

    def by_member_distance(array):
        pieces = [array.reshape(8, members, -1)]
        bit = members // 2
        while bit >= 1:
            flag = (member & bit) != 0
            split = []
            for piece in pieces:
                size = piece.shape[1] // 2
                low, high = piece[:, :size], piece[:, size:]
                split.append(jnp.where(flag, high, low))
                split.append(jnp.where(flag, low, high))
            pieces = split
            bit //= 2
        return jnp.concatenate(pieces, axis=1)

    plane_targets = of_member(target_row, query_rows)
    target_anchor = jnp.sum(
        jnp.where(
            jnp.arange(seq_length, dtype=jnp.int32)[:, None] == plane_targets[None],
            order_row[:, None],
            0,
        ),
        axis=0,
    )
    pad_rows = ROWS - 4 * rows_dev
    row_anchor = jnp.concatenate(
        [of_member(key_anchor, half_rows), target_anchor, jnp.zeros((pad_rows,), jnp.int32)]
    )
    row_limit = jnp.concatenate(
        [
            of_member(key_place, half_rows) + 1,
            plane_targets,
            jnp.ones((pad_rows,), jnp.int32),
        ]
    )
    row_info = jnp.concatenate(
        [row_anchor[None], row_limit[None], jnp.zeros((6, ROWS), jnp.int32)], axis=0
    )

    def by_tile(array):
        parts = by_member_distance(array).reshape(4, 2, members // 2, 2, -1)
        return jnp.transpose(parts, (0, 2, 3, 1, 4)).reshape(-1)

    near_anchor = by_tile(key_anchor)
    key_anchor_wide = jnp.broadcast_to(near_anchor[:, None], (seq_length, 128))
    block_places = by_tile(key_place.reshape(-1, half_rows)[:, 0])
    head_weights = jnp.where(side == owner, near_own, near_other)
    plane_x = plane_rows(by_distance(arrived_rows))
    plane_kv = (
        dot(plane_x[: 4 * tok_rows], head_weights[:, head_width:]) + head_bias[1:2]
    ).astype(BF16)
    first_kv = plane_kv.reshape(1, 8, half_rows, 2 * head_width)
    far_kv = swap(first_kv, members // 2)
    bit = 1
    near_members = first_kv
    while bit < members // 2:
        near_members = jnp.concatenate([near_members, swap(near_members, bit)], axis=0)
        bit *= 2
    query_weights = jnp.pad(head_weights[:, :head_width], ((0, 0), (0, 256 - head_width)))
    query256 = ((dot(plane_x, query_weights) + head_bias[0:1, :256]) * 0.125).astype(BF16)

    output_early, outer_early, rest_own = lax.optimization_barrier(
        (
            output_weight,
            outer_weight,
            jnp.concatenate(
                [
                    jnp.where(odd_plane, s[:, :head_width], s[:, head_width:])
                    for s in lax.optimization_barrier(tuple(shards) + (plane_kv,))[:3]
                ],
                axis=1,
            ),
            query256,
        )
    )[:3]
    hidden_half = outer_weight.shape[0] // 2

    outer_sent = lax.dynamic_slice_in_dim(outer_early, (1 - side) * hidden_half, hidden_half, 0)
    output_arrived = swap_side(half_of_core(output_early))
    outer_arrived_half = swap_side(half_of_core(outer_sent))
    rest_arrived = swap_side(half_of_core(rest_own))

    forward_info = (key_anchor_wide, block_places, row_info, tables)
    first_half = attention_forward(0, query256, near_members, *forward_info, (), my_heads)
    far_members = far_kv
    bit = 1
    while bit < members // 2:
        far_members = jnp.concatenate([far_members, swap(far_members, bit)], axis=0)
        bit *= 2
    exps, bucket_ids, bucket_lows, maxima, _, _, mixed_t, mixed_plane, totals = attention_forward(
        1, query256, far_members, *forward_info, first_half, my_heads
    )
    keys_values = jnp.concatenate([near_members, far_members], axis=0)

    full_output = order_two(side_flag, output_weight, both_cores(after(output_arrived, mixed_plane)), 1)
    outer_kept = lax.dynamic_slice_in_dim(outer_weight, side * hidden_half, hidden_half, 0)
    outer_rows = order_two(side_flag, outer_kept, both_cores(after(outer_arrived_half, mixed_plane)), 1)
    rest_other = both_cores(after(rest_arrived, mixed_plane))
    full_qkv = []
    for i in range(3):
        lanes = slice(i * head_width, (i + 1) * head_width)
        other = order_two(odd_plane, near_other[:, lanes], rest_other[:, lanes], 1)
        full_qkv.append(order_two(side_flag, shards[i], other, 1))

    mixed_blocks = exchange_planes([pack_rows(block) for block in split_rows(mixed_plane)])
    mixed = jnp.concatenate([unpack_rows(block) for block in mixed_blocks], axis=1)
    branch = dot(mixed, full_output) + full_output_bias
    first_norm, first_back = jax.vjp(
        norm_of_sum, stacked.astype(F32), branch, full_first_gain, full_first_shift
    )
    first_low = first_norm.astype(BF16)
    both_first = jnp.concatenate([first_low, swap_side(first_low)], axis=0)
    inner_value = dot(both_first, inner_weight) + inner_bias.astype(F32)
    hidden_value, gelu_back = jax.vjp(gelu_exact, inner_value)
    hidden_low = hidden_value.astype(BF16)
    outer_part = dot(hidden_low, outer_rows)
    outer_arrived = swap_side(outer_part[rows_dev:].astype(BF16))
    outer_value = outer_part[:rows_dev] + outer_arrived.astype(F32) + full_outer_bias
    final_norm, second_back = jax.vjp(
        norm_of_sum, first_norm, outer_value, full_second_gain, full_second_shift
    )
    content_result = final_norm[:tok_rows].reshape(1, 2, half_rows, width).astype(BF16)
    query_result = final_norm[tok_rows:].reshape(1, query_rows, width).astype(BF16)
    cotangent = jnp.concatenate(
        [content_cotangent[0].reshape(tok_rows, width), query_cotangent[0]], axis=0
    )
    rest_grad, outer_grad, second_gain_grad, second_shift_grad = second_back(cotangent.astype(F32))
    outer_low = outer_grad.astype(BF16)
    both_outer = jnp.concatenate([outer_low, swap_side(outer_low)], axis=0)
    (inner_grad,) = gelu_back(times_transpose(both_outer, outer_rows))
    inner_low = inner_grad.astype(BF16)
    first_part = times_transpose(inner_low, inner_weight)
    first_arrived = swap_side(first_part[rows_dev:].astype(BF16))
    first_grad = rest_grad + (first_part[:rows_dev] + first_arrived.astype(F32))
    row_grad, branch_grad, first_gain_grad, first_shift_grad = first_back(first_grad)
    branch_low = branch_grad.astype(BF16)
    mixed_low = times_transpose(branch_low, full_output).astype(BF16)

    def to(bit):
        return lambda value: swap(value, bit)

    def leave_half(bit):
        def leave(parts):
            rows = parts[0].shape[0] // 2
            upper = jnp.where((index & bit) != 0, 1, 0)
            sent = [
                lax.dynamic_slice_in_dim(part, (1 - upper) * rows, rows, 0).astype(BF16)
                for part in parts
            ]
            return jnp.concatenate(sent, axis=1), parts

        return leave

    def add_half(bit):
        def add(parts, arrived):
            rows = parts[0].shape[0] // 2
            upper = jnp.where((index & bit) != 0, 1, 0)
            kept = [lax.dynamic_slice_in_dim(part, upper * rows, rows, 0) for part in parts]
            return [jnp.concatenate(kept, axis=1) + arrived.astype(F32)]

        return add

    def keep_all(state):
        return state, state

    def append(kept, arrived):
        return jnp.concatenate([kept, arrived], axis=0)

    bits = []
    bit = 1
    while bit < ctx:
        bits.append(bit)
        bit *= 2
    sum_stages = [(leave_half(bit), to(bit), add_half(bit)) for bit in bits]
    gather_stages = [(keep_all, to(bit), append) for bit in bits[::-1]]

    def leave_columns(parts):
        piece = parts[0].astype(BF16)
        left, right = piece[:, :half_width], piece[:, half_width:]
        return jnp.where(side_flag, left, right), jnp.where(side_flag, right, left)

    def pair_sides(kept, arrived):
        return jnp.stack([kept, arrived], axis=0)[None]

    def start_gather(parts):
        state = parts[0].astype(BF16)[None]
        return state, state

    outer_chain = Chain(
        [contract_rows(hidden_low, both_outer)],
        sum_stages + [(leave_columns, swap_side, pair_sides)] + gather_stages[:-1],
    )

    other_mixed = swap_side(mixed)
    branch_left, branch_right = branch_low[:, :half_width], branch_low[:, half_width:]
    branch_kept = jnp.where(side_flag, branch_right, branch_left)
    inner_part = contract_rows(both_first, inner_low)
    branch_arrived = swap_side(jnp.where(side_flag, branch_left, branch_right))
    output_part = contract_rows(mixed, branch_kept) + contract_rows(other_mixed, branch_arrived)
    joined_chain = Chain(
        [inner_part, output_part],
        sum_stages + [(start_gather, to(bits[-1]), append)] + gather_stages[1:-1],
    )

    token = outer_chain.advance(branch_low)
    grad_sent = by_distance(
        [
            pack_rows(mixed_low[:, d * head_width : (d + 1) * head_width])
            for d in range(4)
        ]
    )
    grad_sent = lax.optimization_barrier(tuple(grad_sent) + (token,))[:4]
    grad_blocks = [grad_sent[0]] + [swap(grad_sent[d], d * members) for d in range(1, 4)]
    grad256 = arrange_rows(grad_blocks, plane, half_rows, query_rows)
    saved = (exps, bucket_ids, bucket_lows, maxima, totals)
    carried = None
    for call in range(4):
        if call == 0:
            token = outer_chain.advance(grad256)
            token = joined_chain.advance(token)
            grad256 = after(grad256, token)
        else:
            token = outer_chain.advance(carried[0])
            if call > 1:
                token = joined_chain.advance(token)
            carried = (after(carried[0], token),) + carried[1:]
        carried = tuple(
            attention_backward(
                call, saved, query256, grad256, mixed_t, keys_values, carried, my_heads
            )
        )
    dquery_t, table_part, dkv = carried
    query_scaled = dquery_t.T.astype(BF16) * 0.125

    member_bits = [bit for bit in bits if bit < members]

    def leave_members(state):
        pairs = state.reshape((-1, 2) + state.shape[1:])
        return row_major(pairs[:, 1].astype(BF16)), state

    def add_members(state, arrived):
        pairs = state.reshape((-1, 2) + state.shape[1:])
        return row_major(pairs[:, 0] + arrived.astype(F32))

    kv_chain = Chain(
        dkv,
        [(leave_members, to(bit), add_members) for bit in member_bits],
    )
    token = joined_chain.advance(kv_chain.sent)
    token = kv_chain.advance(token)
    token = outer_chain.advance(token)
    token = joined_chain.advance(token)
    token = kv_chain.drain(token)
    kv_low = kv_chain.state.reshape(4 * tok_rows, 2 * head_width).astype(BF16)

    low_parts = jnp.concatenate(
        [query_scaled, jnp.pad(kv_low, ((0, ROWS - 4 * tok_rows), (0, 0)))], axis=1
    )

    def leave_same(parts):
        return parts[0].astype(BF16), parts

    def add_side(kept, arrived):
        return (kept[0] + arrived.astype(F32)).astype(BF16)

    def choose_owner(kept, arrived):
        return jnp.where(owner == side, kept, arrived)[None]

    def append_plane(kept, arrived):
        return jnp.concatenate([kept, arrived], axis=0)[None]

    heads_chain = Chain(
        [contract_rows(plane_x, low_parts)],
        sum_stages[: len(member_bits)]
        + [
            (leave_same, swap_side, add_side),
            (keep_all, to(2 * members), choose_owner),
            (keep_all, to(members), append_plane),
        ]
        + [(keep_all, to(bit), append) for bit in member_bits[::-1]],
    )

    sent_blocks = [
        jnp.concatenate([pack_rows(query_block), kv_block], axis=0)
        for query_block, kv_block in zip(split_rows(query_scaled), split_rows(kv_low))
    ]
    sent_distance = by_distance(sent_blocks)
    sent_distance = lax.optimization_barrier(tuple(sent_distance) + (heads_chain.sent,))[:4]
    got_distance = [sent_distance[0]] + [
        swap(sent_distance[d], d * members) for d in range(1, 4)
    ]
    full_query, full_key, full_value = full_qkv

    blocks = table_part.reshape(8, GROUP, 4, my_heads, GROUP)
    same = jnp.eye(GROUP, dtype=F32)[None, :, None, None, :]
    table_cumulative = jnp.sum(blocks * same, axis=(1, 4))
    table_grad = table_cumulative - jnp.concatenate(
        [table_cumulative[1:], jnp.zeros_like(table_cumulative[:1])], axis=0
    )
    table_grad = table_grad.reshape(buckets, my_heads)

    def at_plane(values, axis):
        return jnp.concatenate(
            [jnp.where(plane == d, values, jnp.zeros_like(values)) for d in range(4)], axis=axis
        )

    inner_bias_part = jnp.sum(inner_low.astype(F32), axis=0)
    inner_bias_zero = jnp.zeros_like(inner_bias_part)
    late_small = jnp.concatenate(
        [
            at_plane(jnp.sum(query_scaled.astype(F32), axis=0), 0),
            at_plane(jnp.sum(kv_low[:, head_width:].astype(F32), axis=0), 0),
            jnp.sum(branch_low.astype(F32), axis=0),
            first_gain_grad.reshape(-1),
            first_shift_grad.reshape(-1),
            jnp.sum(outer_low.astype(F32), axis=0),
            second_gain_grad.reshape(-1),
            second_shift_grad.reshape(-1),
            jnp.where(side_flag, inner_bias_zero, inner_bias_part),
            jnp.where(side_flag, inner_bias_part, inner_bias_zero),
            at_plane(table_grad, 1).reshape(-1),
        ]
    )
    late_length = late_small.shape[0]
    late_small = jnp.pad(late_small, (0, -late_length % 1024)).reshape(-1, 128)

    def add_plain(kept, arrived):
        return kept + arrived

    late_chain = Chain(
        after(late_small, heads_chain.sent),
        [(keep_all, to(bit), add_plain) for bit in bits] + [(keep_all, swap_side, add_plain)],
    )

    token = heads_chain.advance(late_chain.sent)
    token = late_chain.advance(token)
    token = joined_chain.advance(token)
    token = heads_chain.advance(token)
    token = outer_chain.advance(token)
    token = late_chain.advance(token)
    token = heads_chain.advance(token)
    got_distance = lax.optimization_barrier(tuple(got_distance) + (token,))[:4]
    got_blocks = by_distance(got_distance)
    packed_rows = half_rows + query_rows
    own_query = jnp.concatenate([unpack_rows(b[:packed_rows]) for b in got_blocks], axis=1)
    own_key = jnp.concatenate([b[packed_rows:, :head_width] for b in got_blocks], axis=1)
    own_value = jnp.concatenate([b[packed_rows:, head_width:] for b in got_blocks], axis=1)
    input_grad = row_grad + times_transpose(own_query, full_query)
    content_extra = times_transpose(own_key, full_key) + times_transpose(own_value, full_value)
    content_gradient = (input_grad[:tok_rows] + content_extra).reshape(1, 2, half_rows, width)
    query_gradient = input_grad[tok_rows:].reshape(1, query_rows, width)
    token = joined_chain.advance(content_gradient)
    token = late_chain.advance(token)
    token = heads_chain.advance(token)
    token = outer_chain.advance(token)
    token = late_chain.advance(token)
    token = heads_chain.advance(token)
    token = late_chain.drain(token)
    token = outer_chain.drain(token)
    outer_near, outer_far = outer_chain.state, swap(outer_chain.state, 1)
    token = joined_chain.drain(token)
    token = heads_chain.drain(token)
    row_order = jnp.stack([reverse_bits(index, ctx), side])
    joined_pieces = joined_chain.state
    outer_weight_grad = widen_rows(
        outer_near, outer_far, row_order, (half_width,)
    )[0].reshape(2 * hidden_half, half_width)
    inner_weight_grad, output_weight_grad = widen_rows(
        joined_pieces, swap(joined_pieces, 1), row_order, (hidden_half, half_width)
    )
    qkv_grads = widen_heads(heads_chain.state, reverse_bits(member, members), plane & 1)

    late_small = late_chain.state.reshape(-1)[:late_length]
    table_start = 8 * width + 2 * hidden_half
    table_all = late_small[table_start:].reshape(2, buckets // 2, heads)
    bias_table_grad = jnp.where(side_flag, table_all[1], table_all[0])

    def my_half(start, size):
        low = late_small[start : start + size]
        return jnp.where(side_flag, late_small[start + size : start + 2 * size], low)

    mine = [my_half(i * width, half_width) for i in range(8)]
    inner_bias_grad = my_half(8 * width, hidden_half)

    return (
        content_result,
        query_result,
        content_gradient,
        query_gradient,
        qkv_grads[0],
        qkv_grads[1],
        qkv_grads[2],
        output_weight_grad,
        mine[0],
        mine[1],
        mine[2],
        bias_table_grad,
        mine[3],
        mine[4],
        inner_weight_grad,
        inner_bias_grad,
        outer_weight_grad,
        mine[5],
        mine[6],
        mine[7],
    )


def solution(mesh):
    return jax.shard_map(
        body,
        mesh=mesh,
        in_specs=(
            P("wt", None, "ctx", None),
            P("wt", "ctx", None),
            P("wt", None),
            P("wt", None),
            P(None, "wt"),
            P(None, "wt"),
            P(None, "wt"),
            P(None, "wt"),
            P("wt"),
            P("wt"),
            P("wt"),
            P("wt", None),
            P("wt"),
            P("wt"),
            P(None, "wt"),
            P("wt"),
            P(None, "wt"),
            P("wt"),
            P("wt"),
            P("wt"),
            P("wt", None, "ctx", None),
            P("wt", "ctx", None),
        ),
        out_specs=(
            P("wt", None, "ctx", None),
            P("wt", "ctx", None),
            P("wt", None, "ctx", None),
            P("wt", "ctx", None),
            P(None, "wt"),
            P(None, "wt"),
            P(None, "wt"),
            P(None, "wt"),
            P("wt"),
            P("wt"),
            P("wt"),
            P("wt", None),
            P("wt"),
            P("wt"),
            P(None, "wt"),
            P("wt"),
            P(None, "wt"),
            P("wt"),
            P("wt"),
            P("wt"),
        ),
        check_vma=False,
    )
```

profile of v0, /device:TPU:0, one launch (start us, length us, event | category | flops | bytes accessed | tf_op | source)
XLA Modules:
  0.0 323.2 jit_solution(6715909424680550595)
XLA Ops:
  0.7 1.8 pad_maximum_fusion.32
  2.5 4.0 %collective-permute-start.1 = (bf16[152,768]{1,0:T(8,128)(2,1)}, bf16[152,768]{1,0:T(8,128)(2,1)}, u32[]{:S(2)}, u32[]{:S(2)}) collective-permute-start(bf16[152,768]{1,0:T(8,128)(2,1)} %pad_maximum_fusion.32), channel_id=1, source_target_pairs={{0,16},{2,18},{4,20},{6,22},{8,24},{10,26},{12,28},{14,30},{16,0},... | collective-permute-start | bytes 700424 | tf_op jit(solution)/shard_map/ppermute | solution.py:743
  21.6 2.0 unpack_vectors.1
  29.1 2.0 collective-permute-done.4
  40.2 4.5 %collective-permute-done.6 = bf16[1,8,64,384]{3,2,1,0:T(8,128)(2,1)S(1)} collective-permute-done((bf16[1,8,64,384]{3,2,1,0:T(8,128)(2,1)S(1)}, bf16[1,8,64,384]{3,2,1,0:T(8,128)(2,1)S(1)}, u32[]{:S(2)}, u32[]{:S(2)}) %collective-permute-start.6) | collective-permute-done | bytes 393248 | tf_op jit(solution)/shard_map/ppermute | solution.py:743
  45.2 12.6 %attention_forward.2 = (f32[3,2048,640]{2,1,0:T(8,128)}, bf16[2048,640]{1,0:T(8,128)(2,1)S(1)}, bf16[2048,640]{1,0:T(8,128)(2,1)S(1)}, f32[8,8,640]{2,1,0:T(8,12...) custom-call(s32[32]{0:T(128)S(1)} %reshape.276.refs_0_, ...), custom_call_target="tpu_custom_call" | custom-call | flops 15032385536 | bytes 12582912 | tf_op jit(solution)/shard_map/attention_forward/pallas_call | solution.py:241
  57.9 12.9 %attention_forward.3 = (f32[3,2048,640]{2,1,0:T(8,128)}, bf16[2048,640]{1,0:T(8,128)(2,1)S(1)}, bf16[2048,640]{1,0:T(8,128)(2,1)S(1)}, f32[8,8,640]{2,1,0:T(8,12...) custom-call(s32[32]{0:T(128)S(1)} %reshape.276.refs_0_, ...), custom_call_target="tpu_custom_call", output_to_operand_aliasing={{0}: (6, {}), {1}: (7, {}), {2}: (8, {}), {3}: (9, {})} | custom-call | flops 15032385536 | bytes 12582912 | tf_op jit(solution)/shard_map/attention_forward/pallas_call | solution.py:241
  72.5 3.0 collective-permute-start.10
  79.9 2.5 collective-permute-done.9
  89.1 6.7 %collective-permute-done.14 = bf16[152,768]{1,0:T(8,128)(2,1)S(1)} collective-permute-done((bf16[152,768]{1,0:T(8,128)(2,1)S(1)}, bf16[152,768]{1,0:T(8,128)(2,1)S(1)}, u32[]{:S(2)}, u32[]{:S(2)}) %collective-permute-start.14) | collective-permute-done | bytes 233504 | tf_op jit(solution)/shard_map/ppermute | solution.py:746
  95.8 4.6 %multiply_convert_fusion = (bf16[304,1536]{1,0:T(8,128)(2,1)S(1)}, f32[304,1536]{1,0:T(8,128)S(1)}, f32[304,1536]{1,0:T(8,128)S(1)}) fusion(f32[1536]{0:T(1024)S(1)} %convert_element_type.199, bf16[768,1536]{1,0:T(8,128)(2,1)S(1)} %copy-done, bf16[152,768]{1,0:T(8,128)(2,1)S(1)} %collective-permute-done.14, bf16[152,768]{1,0:T(8,128)(2,1)S(1)} %fusion.57), kind=kOutput, calls=%fused_computation.11 | convolution fusion | flops 748978176 | bytes 7501824 | tf_op jit(solution)/shard_map/dot_general | solution.py:36
  102.0 1.8 collective-permute-start.17
  105.2 3.6 %collective-permute-done.17 = bf16[152,768]{1,0:T(8,128)(2,1)S(1)} collective-permute-done((bf16[152,768]{1,0:T(8,128)(2,1)S(1)}, bf16[152,768]{1,0:T(8,128)(2,1)S(1)}, u32[]{:S(2)}, u32[]{:S(2)}) %collective-permute-start.17) | collective-permute-done | bytes 233504 | tf_op jit(solution)/shard_map/ppermute | solution.py:746
  111.8 1.7 collective-permute-start.18
  114.9 2.9 collective-permute-done.18
  120.5 1.8 collective-permute-start.19
  129.7 1.8 collective-permute-start.26
  131.6 3.0 collective-permute-done.26
  140.8 2.5 collective-permute-start.22
  145.1 4.3 %collective-permute-done.22.refs_2_ = bf16[88,384]{1,0:T(8,128)(2,1)S(1)} collective-permute-done((bf16[88,384]{1,0:T(8,128)(2,1)S(1)}, bf16[88,384]{1,0:T(8,128)(2,1)S(1)}, u32[]{:S(2)}, u32[]{:S(2)}) %collective-permute-start.22) | collective-permute-done | bytes 67616 | tf_op jit(solution)/shard_map/ppermute | solution.py:743
  150.1 1.9 arrange_rows.1.refs_6_
  156.2 1.8 constant_dynamic-slice_fusion.3
  158.1 1.7 maximum_add_fusion
  161.4 13.0 %attention_backward.4 = (f32[192,640]{1,0:T(8,128)}, f32[128,192]{1,0:T(8,128)}, f32[4,8,64,384]{3,2,1,0:T(8,128)}) custom-call(f32[3,2048,640]{2,1,0:T(8,128)} %get-tuple-element.128.refs_0_, bf16[2048,640]{1,0:T(8,128)(2,1)} %copy-done.4, bf16[2048,640]{1,0:T(8,128)(2,1)} %copy-done.5, f32[8,8,640]{2,1,0:T(8,128)} %copy-done.7, f32[8,640]{1,0:T(8,128)} %copy-done.8, ...), custom_call_target="tpu_custom_call" | custom-call | flops 8589934592 | bytes 6291456 | tf_op jit(solution)/shard_map/attention_backward/pallas_call | solution.py:431
  175.5 2.5 collective-permute-start.29
  178.1 11.2 %attention_backward.5 = (f32[192,640]{1,0:T(8,128)}, f32[128,192]{1,0:T(8,128)}, f32[4,8,64,384]{3,2,1,0:T(8,128)}) custom-call(f32[3,2048,640]{2,1,0:T(8,128)} %get-tuple-element.128.refs_0_, bf16[2048,640]{1,0:T(8,128)(2,1)} %copy-done.4, bf16[2048,640]{1,0:T(8,128)(2,1)} %copy-done.5, f32[8,8,640]{2,1,0:T(8,128)} %copy-done.7, ...), custom_call_target="tpu_custom_call", output_to_operand_aliasing={{2}: (11, {})} | custom-call | flops 8589934592 | bytes 6291456 | tf_op jit(solution)/shard_map/attention_backward/pallas_call | solution.py:431
  192.3 9.7 %attention_backward.6 = (f32[192,640]{1,0:T(8,128)}, f32[128,192]{1,0:T(8,128)}, f32[4,8,64,384]{3,2,1,0:T(8,128)}) custom-call(f32[3,2048,640]{2,1,0:T(8,128)} %get-tuple-element.128.refs_0_, bf16[2048,640]{1,0:T(8,128)(2,1)} %copy-done.4, bf16[2048,640]{1,0:T(8,128)(2,1)} %copy-done.5, f32[8,8,640]{2,1,0:T(8,128)} %copy-done.7, ...), custom_call_target="tpu_custom_call", output_to_operand_aliasing={{2}: (11, {})} | custom-call | flops 8589934592 | bytes 6291456 | tf_op jit(solution)/shard_map/attention_backward/pallas_call | solution.py:431
  202.1 2.0 collective-permute-start.35
  205.9 7.8 %attention_backward.7 = (f32[192,640]{1,0:T(8,128)}, f32[128,192]{1,0:T(8,128)}, f32[4,8,64,384]{3,2,1,0:T(8,128)}) custom-call(f32[3,2048,640]{2,1,0:T(8,128)} %get-tuple-element.128.refs_0_, bf16[2048,640]{1,0:T(8,128)(2,1)} %copy-done.4, bf16[2048,640]{1,0:T(8,128)(2,1)} %copy-done.5, f32[8,8,640]{2,1,0:T(8,128)} %copy-done.7, ...), custom_call_target="tpu_custom_call", output_to_operand_aliasing={{2}: (11, {})} | custom-call | flops 8589934592 | bytes 6291456 | tf_op jit(solution)/shard_map/attention_backward/pallas_call | solution.py:431
  213.7 2.1 convert.21
  220.6 2.0 collective-permute-start.36
  222.7 1.9 convert_bitcast_fusion
  228.0 4.0 %collective-permute-done.36 = bf16[1,48,1920]{2,1,0:T(8,128)(2,1)S(1)} collective-permute-done((bf16[1,48,1920]{2,1,0:T(8,128)(2,1)S(1)}, bf16[1,48,1920]{2,1,0:T(8,128)(2,1)S(1)}, u32[]{:S(2)}, u32[]{:S(2)}) %collective-permute-start.36) | collective-permute-done | bytes 184352 | tf_op jit(solution)/shard_map/ppermute | solution.py:743
  232.2 3.2 collective-permute-done.37
  242.1 2.0 copy.149
  244.1 2.2 collective-permute-start.39
  247.6 1.8 collective-permute-start.40
  251.0 5.5 %collective-permute-done.44 = bf16[192,576]{1,0:T(8,128)(2,1)S(1)} collective-permute-done((bf16[192,576]{1,0:T(8,128)(2,1)S(1)}, bf16[192,576]{1,0:T(8,128)(2,1)S(1)}, u32[]{:S(2)}, u32[]{:S(2)}) %collective-permute-start.44) | collective-permute-done | bytes 221216 | tf_op jit(solution)/shard_map/ppermute | solution.py:743
  259.6 2.7 collective-permute-done.46
  265.5 3.2 %collective-permute-start.52 = (bf16[192,576]{1,0:T(8,128)(2,1)S(1)}, bf16[192,576]{1,0:T(8,128)(2,1)S(1)}, u32[]{:S(2)}, u32[]{:S(2)}) collective-permute-start(bf16[192,576]{1,0:T(8,128)(2,1)S(1)} %add_convert_fusion.1), channel_id=1, source_target_pairs={{0,16},{2,18},{4,20},{6,22},{8,24},{10,26},{12,28},{14,30},{16,0},... | collective-permute-start | bytes 663560 | tf_op jit(solution)/shard_map/ppermute | solution.py:743
  271.9 9.8 %collective-permute-done.50 = bf16[4,48,1920]{2,1,0:T(8,128)(2,1)S(1)} collective-permute-done((bf16[4,48,1920]{2,1,0:T(8,128)(2,1)S(1)}, bf16[4,48,1920]{2,1,0:T(8,128)(2,1)S(1)}, u32[]{:S(2)}, u32[]{:S(2)}) %collective-permute-start.50) | collective-permute-done | bytes 737312 | tf_op jit(solution)/shard_map/ppermute | solution.py:743
  282.0 3.2 collective-permute-start.54
  285.3 6.1 %collective-permute-done.53 = bf16[4,2,96,384]{3,2,1,0:T(8,128)(2,1)S(1)} collective-permute-done((bf16[4,2,96,384]{3,2,1,0:T(8,128)(2,1)S(1)}, bf16[4,2,96,384]{3,2,1,0:T(8,128)(2,1)S(1)}, u32[]{:S(2)}, u32[]{:S(2)}) %collective-permute-start.53) | collective-permute-done | bytes 589856 | tf_op jit(solution)/shard_map/ppermute | solution.py:743
  297.6 3.4 %collective-permute-done.57 = bf16[1,2,192,576]{3,2,1,0:T(8,128)(2,1)S(1)} collective-permute-done((bf16[1,2,192,576]{3,2,1,0:T(8,128)(2,1)S(1)}, bf16[1,2,192,576]{3,2,1,0:T(8,128)(2,1)S(1)}, u32[]{:S(2)}, u32[]{:S(2)}) %collective-permute-start.57) | collective-permute-done | bytes 442400 | tf_op jit(solution)/shard_map/ppermute | solution.py:743
  304.4 5.1 %widen_rows.3 = f32[2,1536,384]{2,1,0:T(8,128)} custom-call(s32[2]{0:T(128)S(1)} %pad_add_fusion.7.order_ref, bf16[8,2,96,384]{3,2,1,0:T(8,128)(2,1)S(1)} %constant_dynamic-update-slice_fusion.16.near_ref, bf16[8,2,96,384]{3,2,1,0:T(8,128)(2,1)} %collective-permute-done.60.far_ref), custom_call_target="tpu_custom_call" | custom-call | bytes 7077888 | tf_op jit(solution)/shard_map/widen_rows/pallas_call | solution.py:548
  309.5 5.5 %widen_rows.2 = (f32[768,1536]{1,0:T(8,128)}, f32[768,384]{1,0:T(8,128)}) custom-call(s32[2]{0:T(128)S(1)} %pad_add_fusion.7.order_ref, bf16[8,48,1920]{2,1,0:T(8,128)(2,1)S(1)} %constant_dynamic-update-slice_fusion.14.near_ref, bf16[8,48,1920]{2,1,0:T(8,128)(2,1)} %collective-permute-done.59.far_ref), custom_call_target="tpu_custom_call" | custom-call | bytes 8847360 | tf_op jit(solution)/shard_map/widen_rows/pallas_call | solution.py:548
  315.0 3.2 pad_maximum_fusion.1.pieces_ref
  318.2 4.8 %widen_heads.1 = (f32[768,384]{1,0:T(8,128)}, f32[768,384]{1,0:T(8,128)}, f32[768,384]{1,0:T(8,128)}) custom-call(s32[2]{0:T(128)} %pad_add_fusion.6.order_ref, bf16[4,2,192,576]{3,2,1,0:T(8,128)(2,1)} %pad_maximum_fusion.1.pieces_ref), custom_call_target="tpu_custom_call" | custom-call | bytes 5308416 | tf_op jit(solution)/shard_map/widen_heads/pallas_call | solution.py:581
  (474 shorter events, 116.6 us)
Async XLA Ops:
  2.5 23.5 %collective-permute-start.1 = (bf16[152,768]{1,0:T(8,128)(2,1)}, bf16[152,768]{1,0:T(8,128)(2,1)}, u32[]{:S(2)}, u32[]{:S(2)}) collective-permute-start(bf16[152,768]{1,0:T(8,128)(2,1)} %pad_maximum_fusion.32), channel_id=1, source_target_pairs={{0,16},{2,18},{4,20},{6,22},{8,24},{10,26},{12,28},{14,30},{16,0},... | collective-permute-start | bytes 700424 | tf_op jit(solution)/shard_map/ppermute | solution.py:743
  6.5 19.5 %collective-permute-start = (bf16[152,768]{1,0:T(8,128)(2,1)}, bf16[152,768]{1,0:T(8,128)(2,1)}, u32[]{:S(2)}, u32[]{:S(2)}) collective-permute-start(bf16[152,768]{1,0:T(8,128)(2,1)} %pad_maximum_fusion.32), channel_id=1, source_target_pairs={{0,24},{2,26},{4,28},{6,30},{8,16},{10,18},{12,20},{14,22},{16,8},... | collective-permute-start | bytes 700424 | tf_op jit(solution)/shard_map/ppermute | solution.py:743
  7.9 18.2 %collective-permute-start.2 = (bf16[152,768]{1,0:T(8,128)(2,1)}, bf16[152,768]{1,0:T(8,128)(2,1)}, u32[]{:S(2)}, u32[]{:S(2)}) collective-permute-start(bf16[152,768]{1,0:T(8,128)(2,1)} %pad_maximum_fusion.32), channel_id=1, source_target_pairs={{0,8},{2,10},{4,12},{6,14},{8,0},{10,2},{12,4},{14,6},{16,24},{18,... | collective-permute-start | bytes 700424 | tf_op jit(solution)/shard_map/ppermute | solution.py:743
  9.6 11.4 %collective-permute-start.5 = (bf16[32,384]{1,0:T(8,128)(2,1)}, bf16[32,384]{1,0:T(8,128)(2,1)S(1)}, u32[]{:S(2)}, u32[]{:S(2)}) collective-permute-start(bf16[32,384]{1,0:T(8,128)(2,1)} %pack_vectors.1.own_ref), channel_id=1, source_target_pairs={{0,1},{1,0},{2,3},{3,2},{4,5},{5,4},{6,7},{7,6},{8,9},{9,8},{10,11... | collective-permute-start | bytes 73736 | tf_op jit(solution)/shard_map/ppermute | solution.py:746
  16.6 12.4 %collective-permute-start.3 = (bf16[384,576]{1,0:T(8,128)(2,1)}, bf16[384,576]{1,0:T(8,128)(2,1)}, u32[]{:S(2)}, u32[]{:S(2)}) collective-permute-start(bf16[384,576]{1,0:T(8,128)(2,1)} %constant_dynamic-slice_fusion.8), channel_id=1, source_target_pairs={{0,1},{1,0},{2,3},{3,2},{4,5},{5,4},{6,7},{7,6},{8,9},{9,8},{10,11... | collective-permute-start | bytes 1327112 | tf_op jit(solution)/shard_map/ppermute | solution.py:746
  33.5 11.2 %collective-permute-start.6 = (bf16[1,8,64,384]{3,2,1,0:T(8,128)(2,1)S(1)}, bf16[1,8,64,384]{3,2,1,0:T(8,128)(2,1)S(1)}, u32[]{:S(2)}, u32[]{:S(2)}) collective-permute-start(bf16[1,8,64,384]{3,2,1,0:T(8,128)(2,1)S(1)} %bitcast.138), channel_id=1, source_target_pairs={{0,4},{2,6},{4,0},{6,2},{8,12},{10,14},{12,8},{14,10},{16,20},{18,... | collective-permute-start | bytes 1179656 | tf_op jit(solution)/shard_map/ppermute | solution.py:743
  35.1 9.7 %collective-permute-start.8 = (bf16[1,8,64,384]{3,2,1,0:T(8,128)(2,1)S(1)}, bf16[1,8,64,384]{3,2,1,0:T(8,128)(2,1)S(1)}, u32[]{:S(2)}, u32[]{:S(2)}) collective-permute-start(bf16[1,8,64,384]{3,2,1,0:T(8,128)(2,1)S(1)} %bitcast.139), channel_id=1, source_target_pairs={{0,2},{2,0},{4,6},{6,4},{8,10},{10,8},{12,14},{14,12},{16,18},{18,... | collective-permute-start | bytes 1179656 | tf_op jit(solution)/shard_map/ppermute | solution.py:743
  36.7 40.0 %collective-permute-start.12 = (bf16[384,384]{1,0:T(8,128)(2,1)S(1)}, bf16[384,384]{1,0:T(8,128)(2,1)S(1)}, u32[]{:S(2)}, u32[]{:S(2)}) collective-permute-start(bf16[384,384]{1,0:T(8,128)(2,1)S(1)} %constant_dynamic-slice_fusion.5), channel_id=1, source_target_pairs={{0,1},{1,0},{2,3},{3,2},{4,5},{5,4},{6,7},{7,6},{8,9},{9,8},{10,11... | collective-permute-start | bytes 884744 | tf_op jit(solution)/shard_map/ppermute | solution.py:746
  38.0 40.2 %collective-permute-start.15 = (bf16[768,384]{1,0:T(8,128)(2,1)S(1)}, bf16[768,384]{1,0:T(8,128)(2,1)S(1)}, u32[]{:S(2)}, u32[]{:S(2)}) collective-permute-start(bf16[768,384]{1,0:T(8,128)(2,1)S(1)} %constant_dynamic-slice_fusion.4), channel_id=1, source_target_pairs={{0,1},{1,0},{2,3},{3,2},{4,5},{5,4},{6,7},{7,6},{8,9},{9,8},{10,11... | collective-permute-start | bytes 1769480 | tf_op jit(solution)/shard_map/ppermute | solution.py:746
  39.0 39.2 %collective-permute-start.48 = (bf16[384,576]{1,0:T(8,128)(2,1)S(1)}, bf16[384,576]{1,0:T(8,128)(2,1)S(1)}, u32[]{:S(2)}, u32[]{:S(2)}) collective-permute-start(bf16[384,576]{1,0:T(8,128)(2,1)S(1)} %constant_dynamic-slice_fusion), channel_id=1, source_target_pairs={{0,1},{1,0},{2,3},{3,2},{4,5},{5,4},{6,7},{7,6},{8,9},{9,8},{10,11... | collective-permute-start | bytes 1327112 | tf_op jit(solution)/shard_map/ppermute | solution.py:746
  44.7 13.1 %collective-permute-start.7 = (bf16[1,8,64,384]{3,2,1,0:T(8,128)(2,1)S(1)}, bf16[1,8,64,384]{3,2,1,0:T(8,128)(2,1)S(1)}, u32[]{:S(2)}, u32[]{:S(2)}) collective-permute-start(bf16[1,8,64,384]{3,2,1,0:T(8,128)(2,1)S(1)} %collective-permute-done.6), channel_id=1, source_target_pairs={{0,2},{2,0},{4,6},{6,4},{8,10},{10,8},{12,14},{14,12},{16,18},{18,... | collective-permute-start | bytes 1179656 | tf_op jit(solution)/shard_map/ppermute | solution.py:743
  72.5 7.5 %collective-permute-start.10 = (bf16[88,384]{1,0:T(8,128)(2,1)S(1)}, bf16[88,384]{1,0:T(8,128)(2,1)S(1)}, u32[]{:S(2)}, u32[]{:S(2)}) collective-permute-start(bf16[88,384]{1,0:T(8,128)(2,1)S(1)} %broadcast_select_fusion.73), channel_id=1, source_target_pairs={{0,16},{2,18},{4,20},{6,22},{8,24},{10,26},{12,28},{14,30},{16,0},... | collective-permute-start | bytes 202760 | tf_op jit(solution)/shard_map/ppermute | solution.py:743
  75.6 6.8 %collective-permute-start.9 = (bf16[88,384]{1,0:T(8,128)(2,1)S(1)}, bf16[88,384]{1,0:T(8,128)(2,1)S(1)}, u32[]{:S(2)}, u32[]{:S(2)}) collective-permute-start(bf16[88,384]{1,0:T(8,128)(2,1)S(1)} %broadcast_select_fusion.74), channel_id=1, source_target_pairs={{0,24},{2,26},{4,28},{6,30},{8,16},{10,18},{12,20},{14,22},{16,8},... | collective-permute-start | bytes 202760 | tf_op jit(solution)/shard_map/ppermute | solution.py:743
  78.3 22.1 %collective-permute-start.16 = (bf16[768,384]{1,0:T(8,128)(2,1)S(1)}, bf16[768,384]{1,0:T(8,128)(2,1)S(1)}, u32[]{:S(2)}, u32[]{:S(2)}) collective-permute-start(bf16[768,384]{1,0:T(8,128)(2,1)S(1)} %collective-permute-done.15), channel_id=1, source_target_pairs={{0,2},{2,0},{4,6},{6,4},{8,10},{10,8},{12,14},{14,12},{16,18},{18,... | collective-permute-start | bytes 1769480 | tf_op jit(solution)/shard_map/ppermute | solution.py:743
  79.9 6.9 %collective-permute-start.49 = (bf16[384,576]{1,0:T(8,128)(2,1)S(1)}, bf16[384,576]{1,0:T(8,128)(2,1)S(1)}, u32[]{:S(2)}, u32[]{:S(2)}) collective-permute-start(bf16[384,576]{1,0:T(8,128)(2,1)S(1)} %collective-permute-done.48), channel_id=1, source_target_pairs={{0,2},{2,0},{4,6},{6,4},{8,10},{10,8},{12,14},{14,12},{16,18},{18,... | collective-permute-start | bytes 1327112 | tf_op jit(solution)/shard_map/ppermute | solution.py:743
  83.4 48.2 %collective-permute-start.25 = (bf16[152,768]{1,0:T(8,128)(2,1)S(1)}, bf16[152,768]{1,0:T(8,128)(2,1)S(1)}, u32[]{:S(2)}, u32[]{:S(2)}) collective-permute-start(bf16[152,768]{1,0:T(8,128)(2,1)S(1)} %maximum_maximum_fusion), channel_id=1, source_target_pairs={{0,1},{1,0},{2,3},{3,2},{4,5},{5,4},{6,7},{7,6},{8,9},{9,8},{10,11... | collective-permute-start | bytes 700424 | tf_op jit(solution)/shard_map/ppermute | solution.py:746
  86.2 9.6 %collective-permute-start.14 = (bf16[152,768]{1,0:T(8,128)(2,1)S(1)}, bf16[152,768]{1,0:T(8,128)(2,1)S(1)}, u32[]{:S(2)}, u32[]{:S(2)}) collective-permute-start(bf16[152,768]{1,0:T(8,128)(2,1)S(1)} %fusion.57), channel_id=1, source_target_pairs={{0,1},{1,0},{2,3},{3,2},{4,5},{5,4},{6,7},{7,6},{8,9},{9,8},{10,11... | collective-permute-start | bytes 700424 | tf_op jit(solution)/shard_map/ppermute | solution.py:746
  123.8 12.5 %collective-permute-start.20 = (bf16[768,768]{1,0:T(8,128)(2,1)S(1)}, bf16[768,768]{1,0:T(8,128)(2,1)S(1)}, u32[]{:S(2)}, u32[]{:S(2)}) collective-permute-start(bf16[768,768]{1,0:T(8,128)(2,1)S(1)} %dynamic-slice_convert_fusion.1), channel_id=1, source_target_pairs={{0,2},{2,0},{4,6},{6,4},{8,10},{10,8},{12,14},{14,12},{16,18},{18,... | collective-permute-start | bytes 3538952 | tf_op jit(solution)/shard_map/ppermute | solution.py:743
  136.3 21.8 %collective-permute-start.27 = (bf16[384,1920]{1,0:T(8,128)(2,1)}, bf16[384,1920]{1,0:T(8,128)(2,1)}, u32[]{:S(2)}, u32[]{:S(2)}) collective-permute-start(bf16[384,1920]{1,0:T(8,128)(2,1)} %pad_maximum_fusion.7), channel_id=1, source_target_pairs={{0,2},{2,0},{4,6},{6,4},{8,10},{10,8},{12,14},{14,12},{16,18},{18,... | collective-permute-start | bytes 4423688 | tf_op jit(solution)/shard_map/ppermute | solution.py:743
  137.5 16.1 %collective-permute-start.24 = (bf16[384,768]{1,0:T(8,128)(2,1)}, bf16[384,768]{1,0:T(8,128)(2,1)}, u32[]{:S(2)}, u32[]{:S(2)}) collective-permute-start(bf16[384,768]{1,0:T(8,128)(2,1)} %dynamic-slice_convert_fusion.3), channel_id=1, source_target_pairs={{0,4},{2,6},{4,0},{6,2},{8,12},{10,14},{12,8},{14,10},{16,20},{18,... | collective-permute-start | bytes 1769480 | tf_op jit(solution)/shard_map/ppermute | solution.py:743
  140.8 8.7 %collective-permute-start.22 = (bf16[88,384]{1,0:T(8,128)(2,1)S(1)}, bf16[88,384]{1,0:T(8,128)(2,1)S(1)}, u32[]{:S(2)}, u32[]{:S(2)}) collective-permute-start(bf16[88,384]{1,0:T(8,128)(2,1)S(1)} %broadcast_select_fusion.64), channel_id=1, source_target_pairs={{0,16},{2,18},{4,20},{6,22},{8,24},{10,26},{12,28},{14,30},{16,0},... | collective-permute-start | bytes 202760 | tf_op jit(solution)/shard_map/ppermute | solution.py:743
  143.2 6.8 %collective-permute-start.23 = (bf16[88,384]{1,0:T(8,128)(2,1)S(1)}, bf16[88,384]{1,0:T(8,128)(2,1)}, u32[]{:S(2)}, u32[]{:S(2)}) collective-permute-start(bf16[88,384]{1,0:T(8,128)(2,1)S(1)} %broadcast_select_fusion.63), channel_id=1, source_target_pairs={{0,24},{2,26},{4,28},{6,30},{8,16},{10,18},{12,20},{14,22},{16,8},... | collective-permute-start | bytes 202760 | tf_op jit(solution)/shard_map/ppermute | solution.py:743
  155.5 18.9 %collective-permute-start.28 = (bf16[192,768]{1,0:T(8,128)(2,1)}, bf16[192,768]{1,0:T(8,128)(2,1)}, u32[]{:S(2)}, u32[]{:S(2)}) collective-permute-start(bf16[192,768]{1,0:T(8,128)(2,1)} %dynamic-slice_convert_fusion.6), channel_id=1, source_target_pairs={{0,8},{2,10},{4,12},{6,14},{8,0},{10,2},{12,4},{14,6},{16,24},{18,... | collective-permute-start | bytes 884744 | tf_op jit(solution)/shard_map/ppermute | solution.py:743
  159.9 30.8 %collective-permute-start.30 = (bf16[192,1920]{1,0:T(8,128)(2,1)S(1)}, bf16[192,1920]{1,0:T(8,128)(2,1)}, u32[]{:S(2)}, u32[]{:S(2)}) collective-permute-start(bf16[192,1920]{1,0:T(8,128)(2,1)S(1)} %dynamic-slice_convert_fusion.2), channel_id=1, source_target_pairs={{0,4},{2,6},{4,0},{6,2},{8,12},{10,14},{12,8},{14,10},{16,20},{18,... | collective-permute-start | bytes 2211848 | tf_op jit(solution)/shard_map/ppermute | solution.py:743
  175.5 13.7 %collective-permute-start.29 = (bf16[96,768]{1,0:T(8,128)(2,1)S(1)}, bf16[96,768]{1,0:T(8,128)(2,1)S(1)}, u32[]{:S(2)}, u32[]{:S(2)}) collective-permute-start(bf16[96,768]{1,0:T(8,128)(2,1)S(1)} %dynamic-slice_convert_fusion.9), channel_id=1, source_target_pairs={{0,16},{2,18},{4,20},{6,22},{8,24},{10,26},{12,28},{14,30},{16,0},... | collective-permute-start | bytes 442376 | tf_op jit(solution)/shard_map/ppermute | solution.py:743
  189.3 12.7 %collective-permute-start.31 = (bf16[96,384]{1,0:T(8,128)(2,1)S(1)}, bf16[96,384]{1,0:T(8,128)(2,1)S(1)}, u32[]{:S(2)}, u32[]{:S(2)}) collective-permute-start(bf16[96,384]{1,0:T(8,128)(2,1)S(1)} %get-tuple-element.341), channel_id=1, source_target_pairs={{0,1},{1,0},{2,3},{3,2},{4,5},{5,4},{6,7},{7,6},{8,9},{9,8},{10,11... | collective-permute-start | bytes 221192 | tf_op jit(solution)/shard_map/ppermute | solution.py:746
  192.0 12.2 %collective-permute-start.32 = (bf16[96,1920]{1,0:T(8,128)(2,1)S(1)}, bf16[96,1920]{1,0:T(8,128)(2,1)S(1)}, u32[]{:S(2)}, u32[]{:S(2)}) collective-permute-start(bf16[96,1920]{1,0:T(8,128)(2,1)S(1)} %dynamic-slice_convert_fusion.4), channel_id=1, source_target_pairs={{0,8},{2,10},{4,12},{6,14},{8,0},{10,2},{12,4},{14,6},{16,24},{18,... | collective-permute-start | bytes 1105928 | tf_op jit(solution)/shard_map/ppermute | solution.py:743
  202.1 23.8 %collective-permute-start.35 = (bf16[1,2,96,384]{3,2,1,0:T(8,128)(2,1)S(1)}, bf16[1,2,96,384]{3,2,1,0:T(8,128)(2,1)}, u32[]{:S(2)}, u32[]{:S(2)}) collective-permute-start(bf16[1,2,96,384]{3,2,1,0:T(8,128)(2,1)S(1)} %maximum_bitcast_fusion.1), channel_id=1, source_target_pairs={{0,16},{2,18},{4,20},{6,22},{8,24},{10,26},{12,28},{14,30},{16,0},... | collective-permute-start | bytes 442376 | tf_op jit(solution)/shard_map/ppermute | solution.py:743
  204.9 15.6 %collective-permute-start.33 = (bf16[48,1920]{1,0:T(8,128)(2,1)}, bf16[48,1920]{1,0:T(8,128)(2,1)S(1)}, u32[]{:S(2)}, u32[]{:S(2)}) collective-permute-start(bf16[48,1920]{1,0:T(8,128)(2,1)} %dynamic-slice_convert_fusion.8), channel_id=1, source_target_pairs={{0,16},{2,18},{4,20},{6,22},{8,24},{10,26},{12,28},{14,30},{16,0},... | collective-permute-start | bytes 552968 | tf_op jit(solution)/shard_map/ppermute | solution.py:743
  220.6 11.4 %collective-permute-start.36 = (bf16[1,48,1920]{2,1,0:T(8,128)(2,1)S(1)}, bf16[1,48,1920]{2,1,0:T(8,128)(2,1)S(1)}, u32[]{:S(2)}, u32[]{:S(2)}) collective-permute-start(bf16[1,48,1920]{2,1,0:T(8,128)(2,1)S(1)} %fusion.99), channel_id=1, source_target_pairs={{0,16},{2,18},{4,20},{6,22},{8,24},{10,26},{12,28},{14,30},{16,0},... | collective-permute-start | bytes 552968 | tf_op jit(solution)/shard_map/ppermute | solution.py:743
  224.6 10.7 %collective-permute-start.37 = (bf16[1,8,64,384]{3,2,1,0:T(8,128)(2,1)S(1)}, bf16[1,8,64,384]{3,2,1,0:T(8,128)(2,1)S(1)}, u32[]{:S(2)}, u32[]{:S(2)}) collective-permute-start(bf16[1,8,64,384]{3,2,1,0:T(8,128)(2,1)S(1)} %slice_bitcast_fusion.3), channel_id=1, source_target_pairs={{0,4},{2,6},{4,0},{6,2},{8,12},{10,14},{12,8},{14,10},{16,20},{18,... | collective-permute-start | bytes 1179656 | tf_op jit(solution)/shard_map/ppermute | solution.py:743
  227.5 30.4 %collective-permute-start.45 = (bf16[2,2,96,384]{3,2,1,0:T(8,128)(2,1)}, bf16[2,2,96,384]{3,2,1,0:T(8,128)(2,1)}, u32[]{:S(2)}, u32[]{:S(2)}) collective-permute-start(bf16[2,2,96,384]{3,2,1,0:T(8,128)(2,1)} %constant_dynamic-update-slice_fusion.6), channel_id=1, source_target_pairs={{0,8},{2,10},{4,12},{6,14},{8,0},{10,2},{12,4},{14,6},{16,24},{18,... | collective-permute-start | bytes 884744 | tf_op jit(solution)/shard_map/ppermute | solution.py:743
  232.1 17.3 %collective-permute-start.43 = (bf16[2,48,1920]{2,1,0:T(8,128)(2,1)S(1)}, bf16[2,48,1920]{2,1,0:T(8,128)(2,1)}, u32[]{:S(2)}, u32[]{:S(2)}) collective-permute-start(bf16[2,48,1920]{2,1,0:T(8,128)(2,1)S(1)} %constant_dynamic-update-slice_fusion.8), channel_id=1, source_target_pairs={{0,8},{2,10},{4,12},{6,14},{8,0},{10,2},{12,4},{14,6},{16,24},{18,... | collective-permute-start | bytes 1105928 | tf_op jit(solution)/shard_map/ppermute | solution.py:743
  239.1 8.4 %collective-permute-start.42 = (f32[80,128]{1,0:T(8,128)S(1)}, f32[80,128]{1,0:T(8,128)S(1)}, u32[]{:S(2)}, u32[]{:S(2)}) collective-permute-start(f32[80,128]{1,0:T(8,128)S(1)} %pad_bitcast_fusion), channel_id=1, source_target_pairs={{0,2},{2,0},{4,6},{6,4},{8,10},{10,8},{12,14},{14,12},{16,18},{18,... | collective-permute-start | bytes 122888 | tf_op jit(solution)/shard_map/ppermute | solution.py:743
  241.5 21.5 %collective-permute-start.38 = (bf16[216,384]{1,0:T(8,128)(2,1)}, bf16[216,384]{1,0:T(8,128)(2,1)S(1)}, u32[]{:S(2)}, u32[]{:S(2)}) collective-permute-start(bf16[216,384]{1,0:T(8,128)(2,1)} %broadcast_select_fusion.46), channel_id=1, source_target_pairs={{0,8},{2,10},{4,12},{6,14},{8,0},{10,2},{12,4},{14,6},{16,24},{18,... | collective-permute-start | bytes 497672 | tf_op jit(solution)/shard_map/ppermute | solution.py:743
  244.1 20.5 %collective-permute-start.39 = (bf16[216,384]{1,0:T(8,128)(2,1)}, bf16[216,384]{1,0:T(8,128)(2,1)S(1)}, u32[]{:S(2)}, u32[]{:S(2)}) collective-permute-start(bf16[216,384]{1,0:T(8,128)(2,1)} %broadcast_select_fusion.45), channel_id=1, source_target_pairs={{0,16},{2,18},{4,20},{6,22},{8,24},{10,26},{12,28},{14,30},{16,0},... | collective-permute-start | bytes 497672 | tf_op jit(solution)/shard_map/ppermute | solution.py:743
  247.6 17.0 %collective-permute-start.40 = (bf16[216,384]{1,0:T(8,128)(2,1)S(1)}, bf16[216,384]{1,0:T(8,128)(2,1)S(1)}, u32[]{:S(2)}, u32[]{:S(2)}) collective-permute-start(bf16[216,384]{1,0:T(8,128)(2,1)S(1)} %broadcast_select_fusion.44), channel_id=1, source_target_pairs={{0,24},{2,26},{4,28},{6,30},{8,16},{10,18},{12,20},{14,22},{16,8},... | collective-permute-start | bytes 497672 | tf_op jit(solution)/shard_map/ppermute | solution.py:743
  249.4 7.1 %collective-permute-start.44 = (bf16[192,576]{1,0:T(8,128)(2,1)S(1)}, bf16[192,576]{1,0:T(8,128)(2,1)S(1)}, u32[]{:S(2)}, u32[]{:S(2)}) collective-permute-start(bf16[192,576]{1,0:T(8,128)(2,1)S(1)} %dynamic-slice_convert_fusion.7), channel_id=1, source_target_pairs={{0,4},{2,6},{4,0},{6,2},{8,12},{10,14},{12,8},{14,10},{16,20},{18,... | collective-permute-start | bytes 663560 | tf_op jit(solution)/shard_map/ppermute | solution.py:743
  262.3 19.4 %collective-permute-start.50 = (bf16[4,48,1920]{2,1,0:T(8,128)(2,1)S(1)}, bf16[4,48,1920]{2,1,0:T(8,128)(2,1)S(1)}, u32[]{:S(2)}, u32[]{:S(2)}) collective-permute-start(bf16[4,48,1920]{2,1,0:T(8,128)(2,1)S(1)} %constant_dynamic-update-slice_fusion.10), channel_id=1, source_target_pairs={{0,4},{2,6},{4,0},{6,2},{8,12},{10,14},{12,8},{14,10},{16,20},{18,... | collective-permute-start | bytes 2211848 | tf_op jit(solution)/shard_map/ppermute | solution.py:743
  262.9 18.9 %collective-permute-start.51 = (f32[80,128]{1,0:T(8,128)S(1)}, f32[80,128]{1,0:T(8,128)S(1)}, u32[]{:S(2)}, u32[]{:S(2)}) collective-permute-start(f32[80,128]{1,0:T(8,128)S(1)} %add.373), channel_id=1, source_target_pairs={{0,8},{2,10},{4,12},{6,14},{8,0},{10,2},{12,4},{14,6},{16,24},{18,... | collective-permute-start | bytes 122888 | tf_op jit(solution)/shard_map/ppermute | solution.py:743
  263.0 28.3 %collective-permute-start.53 = (bf16[4,2,96,384]{3,2,1,0:T(8,128)(2,1)S(1)}, bf16[4,2,96,384]{3,2,1,0:T(8,128)(2,1)S(1)}, u32[]{:S(2)}, u32[]{:S(2)}) collective-permute-start(bf16[4,2,96,384]{3,2,1,0:T(8,128)(2,1)S(1)} %constant_dynamic-update-slice_fusion.12), channel_id=1, source_target_pairs={{0,4},{2,6},{4,0},{6,2},{8,12},{10,14},{12,8},{14,10},{16,20},{18,... | collective-permute-start | bytes 1769480 | tf_op jit(solution)/shard_map/ppermute | solution.py:743
  265.5 16.4 %collective-permute-start.52 = (bf16[192,576]{1,0:T(8,128)(2,1)S(1)}, bf16[192,576]{1,0:T(8,128)(2,1)S(1)}, u32[]{:S(2)}, u32[]{:S(2)}) collective-permute-start(bf16[192,576]{1,0:T(8,128)(2,1)S(1)} %add_convert_fusion.1), channel_id=1, source_target_pairs={{0,16},{2,18},{4,20},{6,22},{8,24},{10,26},{12,28},{14,30},{16,0},... | collective-permute-start | bytes 663560 | tf_op jit(solution)/shard_map/ppermute | solution.py:743
  281.9 9.5 %collective-permute-start.55 = (bf16[1,192,576]{2,1,0:T(8,128)(2,1)S(1)}, bf16[1,192,576]{2,1,0:T(8,128)(2,1)S(1)}, u32[]{:S(2)}, u32[]{:S(2)}) collective-permute-start(bf16[1,192,576]{2,1,0:T(8,128)(2,1)S(1)} %select_bitcast_fusion), channel_id=1, source_target_pairs={{0,8},{2,10},{4,12},{6,14},{8,0},{10,2},{12,4},{14,6},{16,24},{18,... | collective-permute-start | bytes 663560 | tf_op jit(solution)/shard_map/ppermute | solution.py:743
  282.0 9.4 %collective-permute-start.54 = (f32[80,128]{1,0:T(8,128)S(1)}, f32[80,128]{1,0:T(8,128)S(1)}, u32[]{:S(2)}, u32[]{:S(2)}) collective-permute-start(f32[80,128]{1,0:T(8,128)S(1)} %add.379), channel_id=1, source_target_pairs={{0,16},{2,18},{4,20},{6,22},{8,24},{10,26},{12,28},{14,30},{16,0},... | collective-permute-start | bytes 122888 | tf_op jit(solution)/shard_map/ppermute | solution.py:743
  285.2 24.3 %collective-permute-start.59 = (bf16[8,48,1920]{2,1,0:T(8,128)(2,1)S(1)}, bf16[8,48,1920]{2,1,0:T(8,128)(2,1)}, u32[]{:S(2)}, u32[]{:S(2)}) collective-permute-start(bf16[8,48,1920]{2,1,0:T(8,128)(2,1)S(1)} %constant_dynamic-update-slice_fusion.14.near_ref), channel_id=1, source_target_pairs={{0,2},{2,0},{4,6},{6,4},{8,10},{10,8},{12,14},{14,12},{16,18},{18,... | collective-permute-start | bytes 4423688 | tf_op jit(solution)/shard_map/ppermute | solution.py:743
  291.6 9.5 %collective-permute-start.57 = (bf16[1,2,192,576]{3,2,1,0:T(8,128)(2,1)S(1)}, bf16[1,2,192,576]{3,2,1,0:T(8,128)(2,1)S(1)}, u32[]{:S(2)}, u32[]{:S(2)}) collective-permute-start(bf16[1,2,192,576]{3,2,1,0:T(8,128)(2,1)S(1)} %maximum_bitcast_fusion), channel_id=1, source_target_pairs={{0,4},{2,6},{4,0},{6,2},{8,12},{10,14},{12,8},{14,10},{16,20},{18,... | collective-permute-start | bytes 1327112 | tf_op jit(solution)/shard_map/ppermute | solution.py:743
  294.5 9.9 %collective-permute-start.60 = (bf16[8,2,96,384]{3,2,1,0:T(8,128)(2,1)S(1)}, bf16[8,2,96,384]{3,2,1,0:T(8,128)(2,1)}, u32[]{:S(2)}, u32[]{:S(2)}) collective-permute-start(bf16[8,2,96,384]{3,2,1,0:T(8,128)(2,1)S(1)} %constant_dynamic-update-slice_fusion.16.near_ref), channel_id=1, source_target_pairs={{0,2},{2,0},{4,6},{6,4},{8,10},{10,8},{12,14},{14,12},{16,18},{18,... | collective-permute-start | bytes 3538952 | tf_op jit(solution)/shard_map/ppermute | solution.py:743
  301.8 13.1 %collective-permute-start.58 = (bf16[2,2,192,576]{3,2,1,0:T(8,128)(2,1)}, bf16[2,2,192,576]{3,2,1,0:T(8,128)(2,1)}, u32[]{:S(2)}, u32[]{:S(2)}) collective-permute-start(bf16[2,2,192,576]{3,2,1,0:T(8,128)(2,1)} %constant_dynamic-update-slice_fusion.18), channel_id=1, source_target_pairs={{0,2},{2,0},{4,6},{6,4},{8,10},{10,8},{12,14},{14,12},{16,18},{18,... | collective-permute-start | bytes 2654216 | tf_op jit(solution)/shard_map/ppermute | solution.py:743
  (74 other events, 420.1 us)
where the time goes:
time: 327 us; the launch traced here: 323 us
  Pallas kernels  88 us (27%)
  waiting for transfers between devices  70.8 us (22%)
  starting transfers between devices  62.2 us (19%)
  other arithmetic  48.9 us (15%)
  local copies, waits for them, and re-layouts  33.2 us (10%)
  matrix products  17.4 us (5%)
    ppermute x47, waiting for transfers between devices, swap(): return lax.ppermute(value, 'ctx', [(i, i ^ bit) for i in range(ctx)])  51.1 us
    ppermute x47, starting transfers between devices, swap(): return lax.ppermute(value, 'ctx', [(i, i ^ bit) for i in range(ctx)])  44.7 us
    pallas_call x4, Pallas kernels, attention_backward(): pl.pallas_call(functools.partial(backward_kernel, branch, heads), grid=(t...  41.8 us
    pallas_call x2, Pallas kernels, attention_forward(): pl.pallas_call(functools.partial(forward_kernel, call, count, heads), gri...  25.5 us
    ppermute x14, waiting for transfers between devices, swap_side(): return lax.ppermute(value, 'wt', [(0, 1), (1, 0)])  19.7 us
    ppermute x14, starting transfers between devices, swap_side(): return lax.ppermute(value, 'wt', [(0, 1), (1, 0)])  17.5 us
    pallas_call x2, Pallas kernels, widen_rows(): pl.pallas_call(functools.partial(widen_kernel, group), grid_spec=pltpu.Pr...  10.5 us
    unnamed x140, local copies, waits for them, and re-layouts  9.82 us
  transfers between devices with their start and end apart: 61, of which 21 were waited for; matrix products, arithmetic and copies ran while one was open for 27% of the time, Pallas kernels for 26%

commit v1 on v0

--- a/solution.py
+++ b/solution.py
@@ -15,6 +15,8 @@
 TILE = 256
 ROWS = 640
 GROUP = 16
+GAPS = ['O', 'OJ', 'O', 'OJ', 'OJ']
+TAIL = 'KJOK|HLHJOHXLJHLOHLBLHAC'
 
 
 def layer_norm(hidden_rows, gain_row, shift_row):
@@ -266,7 +268,7 @@
 def backward_kernel(branch, heads, *refs):
     refs = list(refs)
     if branch > 0:
-        del refs[11]
+        del refs[11:13]
     backward_tile(branch, heads, *refs)
 
 
@@ -286,7 +288,8 @@
     dtable_in,
     dquery_ref,
     dtable_ref,
-    dkv_ref,
+    kept_ref,
+    sent_ref,
     grad_z,
     query_n,
     grad_n,
@@ -393,9 +396,12 @@
         dquery_ref[rows, offset:] = dquery_ref[rows, offset:] + dot(
             key_t[rows], dscore_ref[head, :, offset:]
         )
-    dkv_ref[:, :, :, 0:128] = dkey[:, 0:128].reshape(2, 2, 64, 128)
-    dkv_ref[:, :, :, 128:256] = (dkey[:, 128:256] + dvalue[:, 0:128]).reshape(2, 2, 64, 128)
-    dkv_ref[:, :, :, 256:384] = dvalue[:, 128:256].reshape(2, 2, 64, 128)
+    shape = (1, 2, 64, 128)
+    parts = (dkey[:, 0:128], dkey[:, 128:256] + dvalue[:, 0:128], dvalue[:, 128:256])
+    for i, value in enumerate(parts):
+        lanes = slice(128 * i, 128 * i + 128)
+        kept_ref[:, :, :, lanes] = value[:128].reshape(shape)
+        sent_ref[:, :, :, lanes] = value[128:].astype(BF16).reshape(shape)
 
 
 def attention_backward(branch, saved, query256, grad256, mixed_t, keys_values, carried, heads):
@@ -426,8 +432,9 @@
             whole((192, ROWS)),
             whole((128, 64 * heads)),
             pl.BlockSpec(memory_space=pl.ANY),
+            pl.BlockSpec(memory_space=pl.ANY),
         ]
-        aliases = {11: 2}
+        aliases = {11: 2, 12: 3}
     return pl.pallas_call(
         functools.partial(backward_kernel, branch, heads),
         grid=(tiles,),
@@ -435,12 +442,14 @@
         out_specs=[
             whole((192, ROWS)),
             whole((128, 64 * heads)),
-            pl.BlockSpec((2, 2, 64, 384), lambda t: (t, branch, 0, 0)),
+            pl.BlockSpec((1, 2, 64, 384), lambda t: (t, branch, 0, 0)),
+            pl.BlockSpec((1, 2, 64, 384), lambda t: (t, branch, 0, 0)),
         ],
         out_shape=[
             jax.ShapeDtypeStruct((192, ROWS), F32),
             jax.ShapeDtypeStruct((128, 64 * heads), F32),
-            jax.ShapeDtypeStruct((members, 8, 64, 384), F32),
+            jax.ShapeDtypeStruct((tiles, 8, 64, 384), F32),
+            jax.ShapeDtypeStruct((tiles, 8, 64, 384), BF16),
         ],
         input_output_aliases=aliases,
         scratch_shapes=[
@@ -564,26 +573,41 @@
     )(order, near, far)
 
 
-def widen_heads_kernel(order_ref, pieces_ref, *out_refs):
-    odd = order_ref[1] == 1
-    first, second = pieces_ref[0, 0], pieces_ref[0, 1]
-    low = jnp.where(odd, second.astype(F32), first.astype(F32))
-    high = jnp.where(odd, first.astype(F32), second.astype(F32))
-    size = low.shape[1] // 3
-    for i, out_ref in enumerate(out_refs):
-        lanes = slice(i * size, (i + 1) * size)
-        out_ref[...] = jnp.concatenate([low[:, lanes], high[:, lanes]], axis=1)
-
-
-def widen_heads(pieces, order, odd):
-    count, _, rows, width = pieces.shape
+def widen_heads_kernel(count, order_ref, near_ref, far_ref, *out_refs):
+    def from_pieces(pieces_ref):
+        odd = order_ref[1] == 1
+        first, second = pieces_ref[0, 0].astype(F32), pieces_ref[0, 1].astype(F32)
+        low = jnp.where(odd, second, first)
+        high = jnp.where(odd, first, second)
+        size = low.shape[1] // 3
+        for i, out_ref in enumerate(out_refs):
+            lanes = slice(i * size, (i + 1) * size)
+            out_ref[...] = jnp.concatenate([low[:, lanes], high[:, lanes]], axis=1)
+
+    near = (pl.program_id(0) ^ order_ref[0]) < count // 2
+    pl.when(near)(lambda: from_pieces(near_ref))
+    pl.when(jnp.logical_not(near))(lambda: from_pieces(far_ref))
+
+
+def widen_heads(near, far, order, odd):
+    half, _, rows, width = near.shape
+    count = 2 * half
     columns = 2 * width // 3
+
+    def piece(part):
+        def index(r, o):
+            first = jnp.where(o[0] >= half, 1 - part, part) * half
+            inside = jnp.clip(r, first, first + half - 1)
+            return ((inside ^ o[0]) % half, 0, 0, 0)
+
+        return index
+
     return pl.pallas_call(
-        widen_heads_kernel,
+        functools.partial(widen_heads_kernel, count),
         grid_spec=pltpu.PrefetchScalarGridSpec(
             num_scalar_prefetch=1,
             grid=(count,),
-            in_specs=[pl.BlockSpec((1, 2, rows, width), lambda r, o: (r ^ o[0], 0, 0, 0))],
+            in_specs=[pl.BlockSpec((1, 2, rows, width), piece(part)) for part in range(2)],
             out_specs=[pl.BlockSpec((rows, columns), lambda r, o: (r, 0))] * 3,
         ),
         out_shape=[jax.ShapeDtypeStruct((count * rows, columns), F32)] * 3,
@@ -592,7 +616,7 @@
             flops=0, bytes_accessed=12 * count * rows * width, transcendentals=0
         ),
         name="widen_heads",
-    )(jnp.stack([order, odd]), pieces)
+    )(jnp.stack([order, odd]), near, far)
 
 
 def pack_kernel(*refs):
@@ -652,6 +676,70 @@
         scratch_shapes=[pltpu.VMEM((128, 128), F32)],
         name="unpack_vectors",
     )(jnp.stack([side, plane]), own, other)
+
+
+def finish_kernel(half_rows, query_rows, where_ref, dquery_ref, kv_ref, kv_far_ref, x_ref, *refs):
+    block_refs, sent_ref, kept_ref, sums_ref, query_ref, value_ref, low_ref = (
+        refs[:4],
+        *refs[4:],
+    )
+    keys = 8 * half_rows
+    value_ref[...] = kv_ref[...] + kv_far_ref[...].astype(F32)
+    query = dquery_ref[...].T.astype(BF16).astype(F32) * 0.125
+    query_ref[...] = query
+    low_ref[...] = jnp.zeros(low_ref.shape, BF16)
+    low_ref[:, 0:192] = query.astype(BF16)
+    low_ref[0:keys, 192:576] = value_ref[...].astype(BF16)
+    plane = where_ref[0]
+    for distance in range(4):
+        other = plane ^ distance
+        block_ref = block_refs[distance]
+        first = pl.multiple_of(other * half_rows, half_rows)
+        second = pl.multiple_of((7 - other) * half_rows, half_rows)
+        third = pl.multiple_of(keys + other * query_rows, 8)
+        rows = half_rows + query_rows
+        block_ref[0:half_rows, 0:192] = query_ref[pl.ds(first, half_rows), :].astype(BF16)
+        block_ref[0:half_rows, 192:384] = query_ref[pl.ds(second, half_rows), :].astype(BF16)
+        tail = query_ref[pl.ds(third, query_rows), :]
+        tail = jnp.concatenate([tail, jnp.zeros_like(tail)], axis=1)
+        content = jnp.concatenate(
+            [value_ref[pl.ds(first, half_rows), :], value_ref[pl.ds(second, half_rows), :]], axis=0
+        )
+        block_ref[half_rows:, :] = jnp.concatenate([tail, content], axis=0).astype(BF16)
+    width = x_ref.shape[1] // 2
+    for target_ref, flip in ((sent_ref, 1), (kept_ref, 0)):
+        start = pl.multiple_of((where_ref[1] ^ flip) * width, width)
+        product = contract_rows(x_ref[:, pl.ds(start, width)], low_ref[...])
+        target_ref[...] = product.astype(target_ref.dtype)
+    rounded = low_ref[...].astype(F32)
+    sums_ref[...] = jnp.zeros(sums_ref.shape, F32)
+    sums_ref[0:1, :] = jnp.sum(rounded, axis=0, keepdims=True)
+
+
+def finish_heads(dquery_t, kv, kv_far, plane_x, plane, core, half_rows, query_rows):
+    keys = 8 * half_rows
+    block_rows = half_rows + query_rows + 2 * half_rows
+    width = plane_x.shape[1] // 2
+    vmem = pl.BlockSpec(memory_space=pltpu.VMEM)
+    return pl.pallas_call(
+        functools.partial(finish_kernel, half_rows, query_rows),
+        in_specs=[pl.BlockSpec(memory_space=pltpu.SMEM)] + [vmem] * 4,
+        out_specs=[vmem] * 7,
+        out_shape=[jax.ShapeDtypeStruct((block_rows, 384), BF16)] * 4
+        + [
+            jax.ShapeDtypeStruct((width, 576), BF16),
+            jax.ShapeDtypeStruct((width, 576), F32),
+            jax.ShapeDtypeStruct((8, 576), F32),
+        ],
+        scratch_shapes=[
+            pltpu.VMEM((ROWS, 192), F32),
+            pltpu.VMEM((keys, 384), F32),
+            pltpu.VMEM((ROWS, 576), BF16),
+        ],
+        compiler_params=pltpu.CompilerParams(vmem_limit_bytes=32 << 20),
+        cost_estimate=pl.CostEstimate(flops=1 << 30, bytes_accessed=6 << 20, transcendentals=0),
+        name="finish_heads",
+    )(jnp.stack([plane, core]), dquery_t, kv, kv_far, plane_x)
 
 
 def after(value, *earlier):
@@ -1017,7 +1105,7 @@
             rows = parts[0].shape[0] // 2
             upper = jnp.where((index & bit) != 0, 1, 0)
             kept = [lax.dynamic_slice_in_dim(part, upper * rows, rows, 0) for part in parts]
-            return [jnp.concatenate(kept, axis=1) + arrived.astype(F32)]
+            return [(kept[0].astype(F32) + arrived.astype(F32)).astype(kept[0].dtype)]
 
         return add
 
@@ -1047,76 +1135,101 @@
         state = parts[0].astype(BF16)[None]
         return state, state
 
+    core_half = index & 1
+
+    def halves(left, right):
+        size = left.shape[1] // 2
+        parts = []
+        for half in (1 - core_half, core_half):
+            columns = lax.dynamic_slice_in_dim(left, half * size, size, 1)
+            parts.append(contract_rows(columns, right).astype(BF16))
+        return parts
+
+    def add_pair(kept, arrived):
+        return [(kept.astype(F32) + arrived.astype(F32)).astype(BF16)]
+
+    first_stage = (lambda state: state, to(1), add_pair)
     outer_chain = Chain(
-        [contract_rows(hidden_low, both_outer)],
-        sum_stages + [(leave_columns, swap_side, pair_sides)] + gather_stages[:-1],
-    )
-
-    other_mixed = swap_side(mixed)
+        halves(hidden_low, both_outer),
+        [first_stage] + sum_stages[1:] + [(leave_columns, swap_side, pair_sides)] + gather_stages[:-1],
+    )
+
+    other_mixed = swap_side(after(mixed, inner_low))
     branch_left, branch_right = branch_low[:, :half_width], branch_low[:, half_width:]
     branch_kept = jnp.where(side_flag, branch_right, branch_left)
-    inner_part = contract_rows(both_first, inner_low)
-    branch_arrived = swap_side(jnp.where(side_flag, branch_left, branch_right))
-    output_part = contract_rows(mixed, branch_kept) + contract_rows(other_mixed, branch_arrived)
+    inner_halves = halves(both_first, inner_low)
+    branch_arrived = swap_side(after(jnp.where(side_flag, branch_left, branch_right), mixed_low))
+    both_mixed = jnp.concatenate([mixed, other_mixed], axis=0)
+    both_branch = jnp.concatenate([branch_kept, branch_arrived], axis=0)
+    output_halves = halves(both_mixed, both_branch)
     joined_chain = Chain(
-        [inner_part, output_part],
-        sum_stages + [(start_gather, to(bits[-1]), append)] + gather_stages[1:-1],
-    )
-
-    token = outer_chain.advance(branch_low)
+        [
+            jnp.concatenate([inner, output], axis=1)
+            for inner, output in zip(inner_halves, output_halves)
+        ],
+        [first_stage] + sum_stages[1:] + [(start_gather, to(bits[-1]), append)] + gather_stages[1:-1],
+    )
+
+    chains = {"O": outer_chain, "J": joined_chain}
+
+    def run(order, token):
+        for name in order:
+            chain = chains.get(name)
+            if chain is not None and chain.stages:
+                token = chain.advance(token)
+        return token
+
     grad_sent = by_distance(
         [
             pack_rows(mixed_low[:, d * head_width : (d + 1) * head_width])
             for d in range(4)
         ]
     )
-    grad_sent = lax.optimization_barrier(tuple(grad_sent) + (token,))[:4]
     grad_blocks = [grad_sent[0]] + [swap(grad_sent[d], d * members) for d in range(1, 4)]
+    token = run(GAPS[0], grad_sent[1])
+    grad_blocks = lax.optimization_barrier(tuple(grad_blocks) + (token, joined_chain.sent))[:4]
     grad256 = arrange_rows(grad_blocks, plane, half_rows, query_rows)
     saved = (exps, bucket_ids, bucket_lows, maxima, totals)
     carried = None
     for call in range(4):
         if call == 0:
-            token = outer_chain.advance(grad256)
-            token = joined_chain.advance(token)
+            token = run(GAPS[1], grad256)
             grad256 = after(grad256, token)
         else:
-            token = outer_chain.advance(carried[0])
-            if call > 1:
-                token = joined_chain.advance(token)
+            token = run(GAPS[call + 1], carried[0])
             carried = (after(carried[0], token),) + carried[1:]
         carried = tuple(
             attention_backward(
                 call, saved, query256, grad256, mixed_t, keys_values, carried, my_heads
             )
         )
-    dquery_t, table_part, dkv = carried
-    query_scaled = dquery_t.T.astype(BF16) * 0.125
-
+    dquery_t, table_part, kv_kept, kv_sent = carried
     member_bits = [bit for bit in bits if bit < members]
-
-    def leave_members(state):
-        pairs = state.reshape((-1, 2) + state.shape[1:])
-        return row_major(pairs[:, 1].astype(BF16)), state
-
-    def add_members(state, arrived):
-        pairs = state.reshape((-1, 2) + state.shape[1:])
-        return row_major(pairs[:, 0] + arrived.astype(F32))
-
-    kv_chain = Chain(
-        dkv,
-        [(leave_members, to(bit), add_members) for bit in member_bits],
-    )
-    token = joined_chain.advance(kv_chain.sent)
-    token = kv_chain.advance(token)
-    token = outer_chain.advance(token)
-    token = joined_chain.advance(token)
-    token = kv_chain.drain(token)
-    kv_low = kv_chain.state.reshape(4 * tok_rows, 2 * head_width).astype(BF16)
-
-    low_parts = jnp.concatenate(
-        [query_scaled, jnp.pad(kv_low, ((0, ROWS - 4 * tok_rows), (0, 0)))], axis=1
-    )
+    head_orders = TAIL.split("|")[0].split("K")
+    token = run(head_orders[0], kv_sent)
+    for bit in member_bits:
+        kv_arrived = after(swap(kv_sent, bit), token)
+        if bit < member_bits[-1]:
+            pairs = (-1, 2, 8, half_rows, 2 * head_width)
+            kept, arrived = kv_kept.reshape(pairs), kv_arrived.reshape(pairs)
+            kv_sent = row_major((kept[:, 1] + arrived[:, 1].astype(F32)).astype(BF16))
+            kv_kept = row_major(kept[:, 0] + arrived[:, 0].astype(F32))
+        if bit == 1:
+            token = run(head_orders[1], kv_sent)
+    flat_kv = (8 * half_rows, 2 * head_width)
+    *sent_distance, heads_sent, heads_kept, column_sums = finish_heads(
+        dquery_t,
+        kv_kept.reshape(flat_kv),
+        after(kv_arrived, token).reshape(flat_kv),
+        plane_x,
+        plane,
+        index & 1,
+        half_rows,
+        query_rows,
+    )
+
+    def add_first(kept, arrived):
+        return [kept + arrived.astype(F32)]
 
     def leave_same(parts):
         return parts[0].astype(BF16), parts
@@ -1131,22 +1244,17 @@
         return jnp.concatenate([kept, arrived], axis=0)[None]
 
     heads_chain = Chain(
-        [contract_rows(plane_x, low_parts)],
-        sum_stages[: len(member_bits)]
+        (heads_sent, heads_kept),
+        [(lambda state: state, to(1), add_first)]
+        + sum_stages[1 : len(member_bits)]
         + [
             (leave_same, swap_side, add_side),
             (keep_all, to(2 * members), choose_owner),
             (keep_all, to(members), append_plane),
         ]
-        + [(keep_all, to(bit), append) for bit in member_bits[::-1]],
-    )
-
-    sent_blocks = [
-        jnp.concatenate([pack_rows(query_block), kv_block], axis=0)
-        for query_block, kv_block in zip(split_rows(query_scaled), split_rows(kv_low))
-    ]
-    sent_distance = by_distance(sent_blocks)
-    sent_distance = lax.optimization_barrier(tuple(sent_distance) + (heads_chain.sent,))[:4]
+        + [(keep_all, to(bit), append) for bit in member_bits[:0:-1]],
+    )
+
     got_distance = [sent_distance[0]] + [
         swap(sent_distance[d], d * members) for d in range(1, 4)
     ]
@@ -1169,8 +1277,8 @@
     inner_bias_zero = jnp.zeros_like(inner_bias_part)
     late_small = jnp.concatenate(
         [
-            at_plane(jnp.sum(query_scaled.astype(F32), axis=0), 0),
-            at_plane(jnp.sum(kv_low[:, head_width:].astype(F32), axis=0), 0),
+            at_plane(column_sums[0, :head_width], 0),
+            at_plane(column_sums[0, 2 * head_width :], 0),
             jnp.sum(branch_low.astype(F32), axis=0),
             first_gain_grad.reshape(-1),
             first_shift_grad.reshape(-1),
@@ -1193,43 +1301,46 @@
         [(keep_all, to(bit), add_plain) for bit in bits] + [(keep_all, swap_side, add_plain)],
     )
 
-    token = heads_chain.advance(late_chain.sent)
-    token = late_chain.advance(token)
-    token = joined_chain.advance(token)
-    token = heads_chain.advance(token)
-    token = outer_chain.advance(token)
-    token = late_chain.advance(token)
-    token = heads_chain.advance(token)
-    got_distance = lax.optimization_barrier(tuple(got_distance) + (token,))[:4]
-    got_blocks = by_distance(got_distance)
-    packed_rows = half_rows + query_rows
-    own_query = jnp.concatenate([unpack_rows(b[:packed_rows]) for b in got_blocks], axis=1)
-    own_key = jnp.concatenate([b[packed_rows:, :head_width] for b in got_blocks], axis=1)
-    own_value = jnp.concatenate([b[packed_rows:, head_width:] for b in got_blocks], axis=1)
-    input_grad = row_grad + times_transpose(own_query, full_query)
-    content_extra = times_transpose(own_key, full_key) + times_transpose(own_value, full_value)
-    content_gradient = (input_grad[:tok_rows] + content_extra).reshape(1, 2, half_rows, width)
-    query_gradient = input_grad[tok_rows:].reshape(1, query_rows, width)
-    token = joined_chain.advance(content_gradient)
-    token = late_chain.advance(token)
-    token = heads_chain.advance(token)
-    token = outer_chain.advance(token)
-    token = late_chain.advance(token)
-    token = heads_chain.advance(token)
+    chains["H"], chains["L"] = heads_chain, late_chain
+    token = late_chain.sent
+    row_order = jnp.stack([reverse_bits(index, ctx), side])
+    for name in TAIL.split("|")[1]:
+        if name == "X":
+            arrived = lax.optimization_barrier(tuple(got_distance) + (token,))[:4]
+            got_blocks = by_distance(arrived)
+            packed_rows = half_rows + query_rows
+            own_query = jnp.concatenate([unpack_rows(b[:packed_rows]) for b in got_blocks], axis=1)
+            own_key = jnp.concatenate([b[packed_rows:, :head_width] for b in got_blocks], axis=1)
+            own_value = jnp.concatenate([b[packed_rows:, head_width:] for b in got_blocks], axis=1)
+            input_grad = row_grad + times_transpose(own_query, full_query)
+            content_extra = times_transpose(own_key, full_key)
+            content_extra = content_extra + times_transpose(own_value, full_value)
+            content_gradient = input_grad[:tok_rows] + content_extra
+            content_gradient = content_gradient.reshape(1, 2, half_rows, width)
+            query_gradient = input_grad[tok_rows:].reshape(1, query_rows, width)
+            token = content_gradient
+        elif name in "ABC":
+            chain = {"A": outer_chain, "B": joined_chain, "C": heads_chain}[name]
+            token = chain.drain(token)
+            near = chain.state
+            if name == "A":
+                far = after(swap(near, 1), token)
+                outer_weight_grad = widen_rows(near, far, row_order, (half_width,))[0]
+                outer_weight_grad = outer_weight_grad.reshape(2 * hidden_half, half_width)
+                token = outer_weight_grad
+            elif name == "B":
+                far = after(swap(near, 1), token)
+                inner_weight_grad, output_weight_grad = widen_rows(
+                    near, far, row_order, (hidden_half, half_width)
+                )
+                token = inner_weight_grad
+            else:
+                far = after(swap(near, 1), token)
+                qkv_grads = widen_heads(near, far, reverse_bits(member, members), plane & 1)
+                token = qkv_grads[0]
+        else:
+            token = run(name, token)
     token = late_chain.drain(token)
-    token = outer_chain.drain(token)
-    outer_near, outer_far = outer_chain.state, swap(outer_chain.state, 1)
-    token = joined_chain.drain(token)
-    token = heads_chain.drain(token)
-    row_order = jnp.stack([reverse_bits(index, ctx), side])
-    joined_pieces = joined_chain.state
-    outer_weight_grad = widen_rows(
-        outer_near, outer_far, row_order, (half_width,)
-    )[0].reshape(2 * hidden_half, half_width)
-    inner_weight_grad, output_weight_grad = widen_rows(
-        joined_pieces, swap(joined_pieces, 1), row_order, (hidden_half, half_width)
-    )
-    qkv_grads = widen_heads(heads_chain.state, reverse_bits(member, members), plane & 1)
 
     late_small = late_chain.state.reshape(-1)[:late_length]
     table_start = 8 * width + 2 * hidden_half

time: 327 us -> 323 us (0.988)
  other arithmetic: 48.9 us -> 41.8 us
  waiting for transfers between devices: 70.8 us -> 75.9 us
  local copies, waits for them, and re-layouts: 33.2 us -> 29.2 us
    ppermute x47, waiting for transfers between devices: 51.1 us -> 59.1 us  [swap(): return lax.ppermute(value, 'ctx', [(i, i ^ bit) for i in range(ctx)])]
    convert_element_type x3 -> x8, other arithmetic: 0.15 us -> 6.1 us  [the longest x5 2.74 us: add(): return [(kept[0].astype(F32) + arrived.astype(F32)).astype(kept[0].dtype)]]
    add x7 -> x1, other arithmetic: 6.61 us -> 1.11 us  [add_first(): return [kept + arrived.astype(F32)]]
    pallas_call x1 -> x2, Pallas kernels: 4.8 us -> 7.11 us  [the longest x1 5.05 us: widen_heads(): pl.pallas_call(functools.partial(widen_heads_kernel, count), grid_spec=pl...]
    unnamed x140 -> x139, local copies, waits for them, and re-layouts: 9.82 us -> 7.98 us
  transfers between devices with their start and end apart: 61 -> 61, of which waited for: 21 -> 26; matrix products, arithmetic and copies ran while one was open for 27% -> 21% of each run, Pallas kernels for 26% -> 23%
where the time goes in v1:
time: 323 us; the launch traced here: 320 us
  Pallas kernels  89.8 us (28%)
  waiting for transfers between devices  75.9 us (23%)
  starting transfers between devices  63.7 us (20%)
  other arithmetic  41.8 us (13%)
  local copies, waits for them, and re-layouts  29.2 us (9%)
  matrix products  16.8 us (5%)
    ppermute x47, waiting for transfers between devices, swap(): return lax.ppermute(value, 'ctx', [(i, i ^ bit) for i in range(ctx)])  59.1 us
    ppermute x47, starting transfers between devices, swap(): return lax.ppermute(value, 'ctx', [(i, i ^ bit) for i in range(ctx)])  47 us
    pallas_call x4, Pallas kernels, attention_backward(): pl.pallas_call(functools.partial(backward_kernel, branch, heads), grid=(t...  41.1 us
    pallas_call x2, Pallas kernels, attention_forward(): pl.pallas_call(functools.partial(forward_kernel, call, count, heads), gri...  25.5 us
    ppermute x14, waiting for transfers between devices, swap_side(): return lax.ppermute(value, 'wt', [(0, 1), (1, 0)])  16.8 us
    ppermute x14, starting transfers between devices, swap_side(): return lax.ppermute(value, 'wt', [(0, 1), (1, 0)])  16.6 us
    pallas_call x2, Pallas kernels, widen_rows(): pl.pallas_call(functools.partial(widen_kernel, group), grid_spec=pltpu.Pr...  10.7 us
    unnamed x139, local copies, waits for them, and re-layouts  7.98 us
  transfers between devices with their start and end apart: 61, of which 26 were waited for; matrix products, arithmetic and copies ran while one was open for 21% of the time, Pallas kernels for 23%

profile of v1, /device:TPU:0, one launch (start us, length us, event | category | flops | bytes accessed | tf_op | source)
XLA Modules:
  0.0 319.7 jit_solution(4445112334840825857)
XLA Ops:
  0.7 1.8 pad_maximum_fusion.30
  2.5 4.0 %collective-permute-start.1 = (bf16[152,768]{1,0:T(8,128)(2,1)}, bf16[152,768]{1,0:T(8,128)(2,1)}, u32[]{:S(2)}, u32[]{:S(2)}) collective-permute-start(bf16[152,768]{1,0:T(8,128)(2,1)} %pad_maximum_fusion.30), channel_id=1, source_target_pairs={{0,16},{2,18},{4,20},{6,22},{8,24},{10,26},{12,28},{14,30},{16,0},... | collective-permute-start | bytes 700424 | tf_op jit(solution)/shard_map/ppermute | solution.py:831
  11.1 2.0 slice_select_fusion.7
  21.1 2.0 unpack_vectors.1
  27.1 2.1 collective-permute-done.3
  29.2 2.0 collective-permute-done.4
  40.4 4.5 %collective-permute-done.6 = bf16[1,8,64,384]{3,2,1,0:T(8,128)(2,1)S(1)} collective-permute-done((bf16[1,8,64,384]{3,2,1,0:T(8,128)(2,1)S(1)}, bf16[1,8,64,384]{3,2,1,0:T(8,128)(2,1)S(1)}, u32[]{:S(2)}, u32[]{:S(2)}) %collective-permute-start.6) | collective-permute-done | bytes 393248 | tf_op jit(solution)/shard_map/ppermute | solution.py:831
  45.3 12.6 %attention_forward.2 = (f32[3,2048,640]{2,1,0:T(8,128)}, bf16[2048,640]{1,0:T(8,128)(2,1)S(1)}, bf16[2048,640]{1,0:T(8,128)(2,1)S(1)}, f32[8,8,640]{2,1,0:T(8,12...) custom-call(s32[32]{0:T(128)S(1)} %reshape.332.refs_0_, ...), custom_call_target="tpu_custom_call" | custom-call | flops 15032385536 | bytes 12582912 | tf_op jit(solution)/shard_map/attention_forward/pallas_call | solution.py:243
  58.0 12.9 %attention_forward.3 = (f32[3,2048,640]{2,1,0:T(8,128)}, bf16[2048,640]{1,0:T(8,128)(2,1)S(1)}, bf16[2048,640]{1,0:T(8,128)(2,1)S(1)}, f32[8,8,640]{2,1,0:T(8,12...) custom-call(s32[32]{0:T(128)S(1)} %reshape.332.refs_0_, ...), custom_call_target="tpu_custom_call", output_to_operand_aliasing={{0}: (6, {}), {1}: (7, {}), {2}: (8, {}), {3}: (9, {})} | custom-call | flops 15032385536 | bytes 12582912 | tf_op jit(solution)/shard_map/attention_forward/pallas_call | solution.py:243
  72.6 2.8 collective-permute-start.10
  79.9 2.4 collective-permute-done.9
  88.5 4.0 %collective-permute-done.14 = bf16[152,768]{1,0:T(8,128)(2,1)S(1)} collective-permute-done((bf16[152,768]{1,0:T(8,128)(2,1)S(1)}, bf16[152,768]{1,0:T(8,128)(2,1)S(1)}, u32[]{:S(2)}, u32[]{:S(2)}) %collective-permute-start.14) | collective-permute-done | bytes 233504 | tf_op jit(solution)/shard_map/ppermute | solution.py:834
  92.5 4.6 %multiply_convert_fusion = (bf16[304,1536]{1,0:T(8,128)(2,1)S(1)}, f32[304,1536]{1,0:T(8,128)S(1)}, f32[304,1536]{1,0:T(8,128)S(1)}) fusion(f32[1536]{0:T(1024)S(1)} %copy-done.51, bf16[768,1536]{1,0:T(8,128)(2,1)S(1)} %copy-done, bf16[152,768]{1,0:T(8,128)(2,1)S(1)} %collective-permute-done.14, bf16[152,768]{1,0:T(8,128)(2,1)S(1)} %fusion.50), kind=kOutput, calls=%fused_computation.10 | convolution fusion | flops 748978176 | bytes 7501824 | tf_op jit(solution)/shard_map/dot_general | solution.py:38
  98.7 1.8 collective-permute-start.17
  101.9 3.6 %collective-permute-done.17 = bf16[152,768]{1,0:T(8,128)(2,1)S(1)} collective-permute-done((bf16[152,768]{1,0:T(8,128)(2,1)S(1)}, bf16[152,768]{1,0:T(8,128)(2,1)S(1)}, u32[]{:S(2)}, u32[]{:S(2)}) %collective-permute-start.17) | collective-permute-done | bytes 233504 | tf_op jit(solution)/shard_map/ppermute | solution.py:834
  108.5 1.7 collective-permute-start.18
  111.6 3.0 collective-permute-done.18
  114.6 1.8 convert_reduce_fusion
  117.4 1.8 collective-permute-start.19
  122.9 1.7 collective-permute-done.19
  127.9 2.5 collective-permute-start.25
  130.8 2.4 collective-permute-done.25
  135.5 2.1 collective-permute-start.21
  139.6 1.9 collective-permute-start.22
  144.1 1.9 collective-permute-done.22.refs_3_
  146.0 1.9 arrange_rows.1.refs_6_
  147.9 5.4 %collective-permute-done.26 = bf16[384,768]{1,0:T(8,128)(2,1)} collective-permute-done((bf16[384,768]{1,0:T(8,128)(2,1)S(1)}, bf16[384,768]{1,0:T(8,128)(2,1)}, u32[]{:S(2)}, u32[]{:S(2)}) %collective-permute-start.26) | collective-permute-done | bytes 589856 | tf_op jit(solution)/shard_map/ppermute | solution.py:831
  155.8 1.7 add_convert_fusion
  159.2 13.1 %attention_backward.4 = (f32[192,640]{1,0:T(8,128)}, f32[128,192]{1,0:T(8,128)}, f32[2,8,64,384]{3,2,1,0:T(8,128)}, bf16[2,8,64,384]{3,2,1,0:T(8,128)(2,1)}) custom-call(f32[3,2048,640]{2,1,0:T(8,128)} %get-tuple-element.139.refs_0_, bf16[2048,640]{1,0:T(8,128)(2,1)} %copy-done.7, bf16[2048,640]{1,0:T(8,128)(2,1)} %copy-done.8, f32[8,8,640]{2,1,0:T(8,128)} %copy-done.10, ...), custom_call_target="tpu_custom_call" | custom-call | flops 8589934592 | bytes 6291456 | tf_op jit(solution)/shard_map/attention_backward/pallas_call | solution.py:438
  174.7 10.8 %attention_backward.5 = (f32[192,640]{1,0:T(8,128)}, f32[128,192]{1,0:T(8,128)}, f32[2,8,64,384]{3,2,1,0:T(8,128)}, bf16[2,8,64,384]{3,2,1,0:T(8,128)(2,1)}) custom-call(f32[3,2048,640]{2,1,0:T(8,128)} %get-tuple-element.139.refs_0_, bf16[2048,640]{1,0:T(8,128)(2,1)} %copy-done.7, ...), custom_call_target="tpu_custom_call", output_to_operand_aliasing={{2}: (11, {}), {3}: (12, {})} | custom-call | flops 8589934592 | bytes 6291456 | tf_op jit(solution)/shard_map/attention_backward/pallas_call | solution.py:438
  185.6 2.1 collective-permute-start.31
  188.5 9.6 %attention_backward.6 = (f32[192,640]{1,0:T(8,128)}, f32[128,192]{1,0:T(8,128)}, f32[2,8,64,384]{3,2,1,0:T(8,128)}, bf16[2,8,64,384]{3,2,1,0:T(8,128)(2,1)}) custom-call(f32[3,2048,640]{2,1,0:T(8,128)} %get-tuple-element.139.refs_0_, bf16[2048,640]{1,0:T(8,128)(2,1)} %copy-done.7, ...), custom_call_target="tpu_custom_call", output_to_operand_aliasing={{2}: (11, {}), {3}: (12, {})} | custom-call | flops 8589934592 | bytes 6291456 | tf_op jit(solution)/shard_map/attention_backward/pallas_call | solution.py:438
  199.0 7.7 %attention_backward.7 = (f32[192,640]{1,0:T(8,128)}, f32[128,192]{1,0:T(8,128)}, f32[2,8,64,384]{3,2,1,0:T(8,128)}, bf16[2,8,64,384]{3,2,1,0:T(8,128)(2,1)}) custom-call(f32[3,2048,640]{2,1,0:T(8,128)} %get-tuple-element.139.refs_0_, bf16[2048,640]{1,0:T(8,128)(2,1)} %copy-done.7, ...), custom_call_target="tpu_custom_call", output_to_operand_aliasing={{2}: (11, {}), {3}: (12, {})} | custom-call | flops 8589934592 | bytes 6291456 | tf_op jit(solution)/shard_map/attention_backward/pallas_call | solution.py:438
  218.4 7.3 %collective-permute-done.35 = bf16[48,1920]{1,0:T(8,128)(2,1)} collective-permute-done((bf16[48,1920]{1,0:T(8,128)(2,1)}, bf16[48,1920]{1,0:T(8,128)(2,1)}, u32[]{:S(2)}, u32[]{:S(2)}) %collective-permute-start.35) | collective-permute-done | bytes 184352 | tf_op jit(solution)/shard_map/ppermute | solution.py:831
  229.1 2.1 finish_heads.1
  241.0 2.1 collective-permute-done.42
  244.5 3.9 %collective-permute-done.43 = bf16[1,48,1920]{2,1,0:T(8,128)(2,1)S(1)} collective-permute-done((bf16[1,48,1920]{2,1,0:T(8,128)(2,1)S(1)}, bf16[1,48,1920]{2,1,0:T(8,128)(2,1)S(1)}, u32[]{:S(2)}, u32[]{:S(2)}) %collective-permute-start.43) | collective-permute-done | bytes 184352 | tf_op jit(solution)/shard_map/ppermute | solution.py:831
  248.4 5.4 %collective-permute-done.44 = bf16[2,2,96,384]{3,2,1,0:T(8,128)(2,1)S(1)} collective-permute-done((bf16[2,2,96,384]{3,2,1,0:T(8,128)(2,1)S(1)}, bf16[2,2,96,384]{3,2,1,0:T(8,128)(2,1)S(1)}, u32[]{:S(2)}, u32[]{:S(2)}) %collective-permute-start.44) | collective-permute-done | bytes 294944 | tf_op jit(solution)/shard_map/ppermute | solution.py:831
  257.3 2.5 collective-permute-start.52
  259.8 2.4 collective-permute-done.39
  266.3 2.9 collective-permute-start.51
  269.2 3.8 %collective-permute-done.49 = bf16[2,48,1920]{2,1,0:T(8,128)(2,1)S(1)} collective-permute-done((bf16[2,48,1920]{2,1,0:T(8,128)(2,1)S(1)}, bf16[2,48,1920]{2,1,0:T(8,128)(2,1)S(1)}, u32[]{:S(2)}, u32[]{:S(2)}) %collective-permute-start.49) | collective-permute-done | bytes 368672 | tf_op jit(solution)/shard_map/ppermute | solution.py:831
  275.6 2.8 collective-permute-start.54
  278.7 3.6 %collective-permute-done.53 = bf16[1,192,576]{2,1,0:T(8,128)(2,1)S(1)} collective-permute-done((bf16[1,192,576]{2,1,0:T(8,128)(2,1)S(1)}, bf16[1,192,576]{2,1,0:T(8,128)(2,1)S(1)}, u32[]{:S(2)}, u32[]{:S(2)}) %collective-permute-start.53) | collective-permute-done | bytes 221216 | tf_op jit(solution)/shard_map/ppermute | solution.py:831
  282.4 7.8 %collective-permute-done.55 = bf16[4,48,1920]{2,1,0:T(8,128)(2,1)S(1)} collective-permute-done((bf16[4,48,1920]{2,1,0:T(8,128)(2,1)S(1)}, bf16[4,48,1920]{2,1,0:T(8,128)(2,1)S(1)}, u32[]{:S(2)}, u32[]{:S(2)}) %collective-permute-start.55) | collective-permute-done | bytes 737312 | tf_op jit(solution)/shard_map/ppermute | solution.py:831
  296.2 5.5 %widen_rows.2 = (f32[768,1536]{1,0:T(8,128)}, f32[768,384]{1,0:T(8,128)}) custom-call(s32[2]{0:T(128)S(1)} %pad_add_fusion.8.order_ref, bf16[8,48,1920]{2,1,0:T(8,128)(2,1)S(1)} %constant_dynamic-update-slice_fusion.16.near_ref, bf16[8,48,1920]{2,1,0:T(8,128)(2,1)} %collective-permute-done.56.far_ref), custom_call_target="tpu_custom_call" | custom-call | bytes 8847360 | tf_op jit(solution)/shard_map/widen_rows/pallas_call | solution.py:557
  306.5 5.2 %widen_rows.3 = f32[2,1536,384]{2,1,0:T(8,128)} custom-call(s32[2]{0:T(128)S(1)} %pad_add_fusion.8.order_ref, bf16[8,2,96,384]{3,2,1,0:T(8,128)(2,1)S(1)} %constant_dynamic-update-slice_fusion.14.near_ref, bf16[8,2,96,384]{3,2,1,0:T(8,128)(2,1)} %collective-permute-done.60.far_ref), custom_call_target="tpu_custom_call" | custom-call | bytes 7077888 | tf_op jit(solution)/shard_map/widen_rows/pallas_call | solution.py:557
  314.4 5.0 %widen_heads.1 = (f32[768,384]{1,0:T(8,128)}, f32[768,384]{1,0:T(8,128)}, f32[768,384]{1,0:T(8,128)}) custom-call(s32[2]{0:T(128)} %pad_add_fusion.7.order_ref, bf16[2,2,192,576]{3,2,1,0:T(8,128)(2,1)} %constant_dynamic-update-slice_fusion.18.near_ref, bf16[2,2,192,576]{3,2,1,0:T(8,128)(2,1)} %collective-permute-done.59.far_ref), custom_call_target="tpu_custom_call" | custom-call | bytes 5308416 | tf_op jit(solution)/shard_map/widen_heads/pallas_call | solution.py:605
  (452 shorter events, 118.3 us)
Async XLA Ops:
  2.5 23.0 %collective-permute-start.1 = (bf16[152,768]{1,0:T(8,128)(2,1)}, bf16[152,768]{1,0:T(8,128)(2,1)}, u32[]{:S(2)}, u32[]{:S(2)}) collective-permute-start(bf16[152,768]{1,0:T(8,128)(2,1)} %pad_maximum_fusion.30), channel_id=1, source_target_pairs={{0,16},{2,18},{4,20},{6,22},{8,24},{10,26},{12,28},{14,30},{16,0},... | collective-permute-start | bytes 700424 | tf_op jit(solution)/shard_map/ppermute | solution.py:831
  6.5 18.9 %collective-permute-start = (bf16[152,768]{1,0:T(8,128)(2,1)}, bf16[152,768]{1,0:T(8,128)(2,1)}, u32[]{:S(2)}, u32[]{:S(2)}) collective-permute-start(bf16[152,768]{1,0:T(8,128)(2,1)} %pad_maximum_fusion.30), channel_id=1, source_target_pairs={{0,24},{2,26},{4,28},{6,30},{8,16},{10,18},{12,20},{14,22},{16,8},... | collective-permute-start | bytes 700424 | tf_op jit(solution)/shard_map/ppermute | solution.py:831
  7.9 17.6 %collective-permute-start.2 = (bf16[152,768]{1,0:T(8,128)(2,1)}, bf16[152,768]{1,0:T(8,128)(2,1)}, u32[]{:S(2)}, u32[]{:S(2)}) collective-permute-start(bf16[152,768]{1,0:T(8,128)(2,1)} %pad_maximum_fusion.30), channel_id=1, source_target_pairs={{0,8},{2,10},{4,12},{6,14},{8,0},{10,2},{12,4},{14,6},{16,24},{18,... | collective-permute-start | bytes 700424 | tf_op jit(solution)/shard_map/ppermute | solution.py:831
  9.6 11.5 %collective-permute-start.5 = (bf16[32,384]{1,0:T(8,128)(2,1)}, bf16[32,384]{1,0:T(8,128)(2,1)}, u32[]{:S(2)}, u32[]{:S(2)}) collective-permute-start(bf16[32,384]{1,0:T(8,128)(2,1)} %pack_vectors.1.own_ref), channel_id=1, source_target_pairs={{0,1},{1,0},{2,3},{3,2},{4,5},{5,4},{6,7},{7,6},{8,9},{9,8},{10,11... | collective-permute-start | bytes 73736 | tf_op jit(solution)/shard_map/ppermute | solution.py:834
  16.8 12.4 %collective-permute-start.3 = (bf16[384,576]{1,0:T(8,128)(2,1)}, bf16[384,576]{1,0:T(8,128)(2,1)}, u32[]{:S(2)}, u32[]{:S(2)}) collective-permute-start(bf16[384,576]{1,0:T(8,128)(2,1)} %constant_dynamic-slice_fusion.11), channel_id=1, source_target_pairs={{0,1},{1,0},{2,3},{3,2},{4,5},{5,4},{6,7},{7,6},{8,9},{9,8},{10,11... | collective-permute-start | bytes 1327112 | tf_op jit(solution)/shard_map/ppermute | solution.py:834
  33.6 11.2 %collective-permute-start.6 = (bf16[1,8,64,384]{3,2,1,0:T(8,128)(2,1)S(1)}, bf16[1,8,64,384]{3,2,1,0:T(8,128)(2,1)S(1)}, u32[]{:S(2)}, u32[]{:S(2)}) collective-permute-start(bf16[1,8,64,384]{3,2,1,0:T(8,128)(2,1)S(1)} %bitcast.103), channel_id=1, source_target_pairs={{0,4},{2,6},{4,0},{6,2},{8,12},{10,14},{12,8},{14,10},{16,20},{18,... | collective-permute-start | bytes 1179656 | tf_op jit(solution)/shard_map/ppermute | solution.py:831
  35.2 9.7 %collective-permute-start.8 = (bf16[1,8,64,384]{3,2,1,0:T(8,128)(2,1)S(1)}, bf16[1,8,64,384]{3,2,1,0:T(8,128)(2,1)S(1)}, u32[]{:S(2)}, u32[]{:S(2)}) collective-permute-start(bf16[1,8,64,384]{3,2,1,0:T(8,128)(2,1)S(1)} %bitcast.104), channel_id=1, source_target_pairs={{0,2},{2,0},{4,6},{6,4},{8,10},{10,8},{12,14},{14,12},{16,18},{18,... | collective-permute-start | bytes 1179656 | tf_op jit(solution)/shard_map/ppermute | solution.py:831
  36.8 40.0 %collective-permute-start.12 = (bf16[384,384]{1,0:T(8,128)(2,1)S(1)}, bf16[384,384]{1,0:T(8,128)(2,1)S(1)}, u32[]{:S(2)}, u32[]{:S(2)}) collective-permute-start(bf16[384,384]{1,0:T(8,128)(2,1)S(1)} %constant_dynamic-slice_fusion.8), channel_id=1, source_target_pairs={{0,1},{1,0},{2,3},{3,2},{4,5},{5,4},{6,7},{7,6},{8,9},{9,8},{10,11... | collective-permute-start | bytes 884744 | tf_op jit(solution)/shard_map/ppermute | solution.py:834
  38.2 40.2 %collective-permute-start.15 = (bf16[768,384]{1,0:T(8,128)(2,1)S(1)}, bf16[768,384]{1,0:T(8,128)(2,1)S(1)}, u32[]{:S(2)}, u32[]{:S(2)}) collective-permute-start(bf16[768,384]{1,0:T(8,128)(2,1)S(1)} %constant_dynamic-slice_fusion.7), channel_id=1, source_target_pairs={{0,1},{1,0},{2,3},{3,2},{4,5},{5,4},{6,7},{7,6},{8,9},{9,8},{10,11... | collective-permute-start | bytes 1769480 | tf_op jit(solution)/shard_map/ppermute | solution.py:834
  39.2 39.3 %collective-permute-start.46 = (bf16[384,576]{1,0:T(8,128)(2,1)S(1)}, bf16[384,576]{1,0:T(8,128)(2,1)S(1)}, u32[]{:S(2)}, u32[]{:S(2)}) collective-permute-start(bf16[384,576]{1,0:T(8,128)(2,1)S(1)} %constant_dynamic-slice_fusion), channel_id=1, source_target_pairs={{0,1},{1,0},{2,3},{3,2},{4,5},{5,4},{6,7},{7,6},{8,9},{9,8},{10,11... | collective-permute-start | bytes 1327112 | tf_op jit(solution)/shard_map/ppermute | solution.py:834
  44.8 13.1 %collective-permute-start.7 = (bf16[1,8,64,384]{3,2,1,0:T(8,128)(2,1)S(1)}, bf16[1,8,64,384]{3,2,1,0:T(8,128)(2,1)S(1)}, u32[]{:S(2)}, u32[]{:S(2)}) collective-permute-start(bf16[1,8,64,384]{3,2,1,0:T(8,128)(2,1)S(1)} %collective-permute-done.6), channel_id=1, source_target_pairs={{0,2},{2,0},{4,6},{6,4},{8,10},{10,8},{12,14},{14,12},{16,18},{18,... | collective-permute-start | bytes 1179656 | tf_op jit(solution)/shard_map/ppermute | solution.py:831
  72.6 7.3 %collective-permute-start.10 = (bf16[88,384]{1,0:T(8,128)(2,1)S(1)}, bf16[88,384]{1,0:T(8,128)(2,1)S(1)}, u32[]{:S(2)}, u32[]{:S(2)}) collective-permute-start(bf16[88,384]{1,0:T(8,128)(2,1)S(1)} %broadcast_select_fusion.66), channel_id=1, source_target_pairs={{0,16},{2,18},{4,20},{6,22},{8,24},{10,26},{12,28},{14,30},{16,0},... | collective-permute-start | bytes 202760 | tf_op jit(solution)/shard_map/ppermute | solution.py:831
  75.5 6.8 %collective-permute-start.9 = (bf16[88,384]{1,0:T(8,128)(2,1)S(1)}, bf16[88,384]{1,0:T(8,128)(2,1)S(1)}, u32[]{:S(2)}, u32[]{:S(2)}) collective-permute-start(bf16[88,384]{1,0:T(8,128)(2,1)S(1)} %broadcast_select_fusion.67), channel_id=1, source_target_pairs={{0,24},{2,26},{4,28},{6,30},{8,16},{10,18},{12,20},{14,22},{16,8},... | collective-permute-start | bytes 202760 | tf_op jit(solution)/shard_map/ppermute | solution.py:831
  78.5 18.7 %collective-permute-start.16 = (bf16[768,384]{1,0:T(8,128)(2,1)S(1)}, bf16[768,384]{1,0:T(8,128)(2,1)S(1)}, u32[]{:S(2)}, u32[]{:S(2)}) collective-permute-start(bf16[768,384]{1,0:T(8,128)(2,1)S(1)} %collective-permute-done.15), channel_id=1, source_target_pairs={{0,2},{2,0},{4,6},{6,4},{8,10},{10,8},{12,14},{14,12},{16,18},{18,... | collective-permute-start | bytes 1769480 | tf_op jit(solution)/shard_map/ppermute | solution.py:831
  85.1 7.4 %collective-permute-start.14 = (bf16[152,768]{1,0:T(8,128)(2,1)S(1)}, bf16[152,768]{1,0:T(8,128)(2,1)S(1)}, u32[]{:S(2)}, u32[]{:S(2)}) collective-permute-start(bf16[152,768]{1,0:T(8,128)(2,1)S(1)} %fusion.50), channel_id=1, source_target_pairs={{0,1},{1,0},{2,3},{3,2},{4,5},{5,4},{6,7},{7,6},{8,9},{9,8},{10,11... | collective-permute-start | bytes 700424 | tf_op jit(solution)/shard_map/ppermute | solution.py:834
  117.4 7.2 %collective-permute-start.19 = (bf16[152,768]{1,0:T(8,128)(2,1)S(1)}, bf16[152,768]{1,0:T(8,128)(2,1)S(1)}, u32[]{:S(2)}, u32[]{:S(2)}) collective-permute-start(bf16[152,768]{1,0:T(8,128)(2,1)S(1)} %slice.1018), channel_id=1, source_target_pairs={{0,1},{1,0},{2,3},{3,2},{4,5},{5,4},{6,7},{7,6},{8,9},{9,8},{10,11... | collective-permute-start | bytes 700424 | tf_op jit(solution)/shard_map/ppermute | solution.py:834
  120.0 17.6 %collective-permute-start.23 = (bf16[768,768]{1,0:T(8,128)(2,1)S(1)}, bf16[768,768]{1,0:T(8,128)(2,1)S(1)}, u32[]{:S(2)}, u32[]{:S(2)}) collective-permute-start(bf16[768,768]{1,0:T(8,128)(2,1)S(1)} %convolution_convert_fusion.2), channel_id=1, source_target_pairs={{0,2},{2,0},{4,6},{6,4},{8,10},{10,8},{12,14},{14,12},{16,18},{18,... | collective-permute-start | bytes 3538952 | tf_op jit(solution)/shard_map/ppermute | solution.py:831
  120.1 10.5 %collective-permute-start.24 = (bf16[152,768]{1,0:T(8,128)(2,1)S(1)}, bf16[152,768]{1,0:T(8,128)(2,1)S(1)}, u32[]{:S(2)}, u32[]{:S(2)}) collective-permute-start(bf16[152,768]{1,0:T(8,128)(2,1)S(1)} %maximum_maximum_fusion), channel_id=1, source_target_pairs={{0,1},{1,0},{2,3},{3,2},{4,5},{5,4},{6,7},{7,6},{8,9},{9,8},{10,11... | collective-permute-start | bytes 700424 | tf_op jit(solution)/shard_map/ppermute | solution.py:834
  134.8 21.0 %collective-permute-start.27 = (bf16[384,1920]{1,0:T(8,128)(2,1)}, bf16[384,1920]{1,0:T(8,128)(2,1)}, u32[]{:S(2)}, u32[]{:S(2)}) collective-permute-start(bf16[384,1920]{1,0:T(8,128)(2,1)} %pad_maximum_fusion.6), channel_id=1, source_target_pairs={{0,2},{2,0},{4,6},{6,4},{8,10},{10,8},{12,14},{14,12},{16,18},{18,... | collective-permute-start | bytes 4423688 | tf_op jit(solution)/shard_map/ppermute | solution.py:831
  134.9 7.8 %collective-permute-start.20 = (bf16[88,384]{1,0:T(8,128)(2,1)S(1)}, bf16[88,384]{1,0:T(8,128)(2,1)S(1)}, u32[]{:S(2)}, u32[]{:S(2)}) collective-permute-start(bf16[88,384]{1,0:T(8,128)(2,1)S(1)} %broadcast_select_fusion.58), channel_id=1, source_target_pairs={{0,8},{2,10},{4,12},{6,14},{8,0},{10,2},{12,4},{14,6},{16,24},{18,... | collective-permute-start | bytes 202760 | tf_op jit(solution)/shard_map/ppermute | solution.py:831
  135.5 7.3 %collective-permute-start.21 = (bf16[88,384]{1,0:T(8,128)(2,1)S(1)}, bf16[88,384]{1,0:T(8,128)(2,1)S(1)}, u32[]{:S(2)}, u32[]{:S(2)}) collective-permute-start(bf16[88,384]{1,0:T(8,128)(2,1)S(1)} %broadcast_select_fusion.57), channel_id=1, source_target_pairs={{0,16},{2,18},{4,20},{6,22},{8,24},{10,26},{12,28},{14,30},{16,0},... | collective-permute-start | bytes 202760 | tf_op jit(solution)/shard_map/ppermute | solution.py:831
  138.0 15.4 %collective-permute-start.26 = (bf16[384,768]{1,0:T(8,128)(2,1)S(1)}, bf16[384,768]{1,0:T(8,128)(2,1)}, u32[]{:S(2)}, u32[]{:S(2)}) collective-permute-start(bf16[384,768]{1,0:T(8,128)(2,1)S(1)} %constant_dynamic-slice_fusion.6), channel_id=1, source_target_pairs={{0,4},{2,6},{4,0},{6,2},{8,12},{10,14},{12,8},{14,10},{16,20},{18,... | collective-permute-start | bytes 1769480 | tf_op jit(solution)/shard_map/ppermute | solution.py:831
  154.7 17.5 %collective-permute-start.28 = (bf16[192,768]{1,0:T(8,128)(2,1)S(1)}, bf16[192,768]{1,0:T(8,128)(2,1)}, u32[]{:S(2)}, u32[]{:S(2)}) collective-permute-start(bf16[192,768]{1,0:T(8,128)(2,1)S(1)} %constant_dynamic-slice_fusion.5), channel_id=1, source_target_pairs={{0,8},{2,10},{4,12},{6,14},{8,0},{10,2},{12,4},{14,6},{16,24},{18,... | collective-permute-start | bytes 884744 | tf_op jit(solution)/shard_map/ppermute | solution.py:831
  157.6 30.1 %collective-permute-start.30 = (bf16[192,1920]{1,0:T(8,128)(2,1)S(1)}, bf16[192,1920]{1,0:T(8,128)(2,1)S(1)}, u32[]{:S(2)}, u32[]{:S(2)}) collective-permute-start(bf16[192,1920]{1,0:T(8,128)(2,1)S(1)} %constant_dynamic-slice_fusion.4), channel_id=1, source_target_pairs={{0,4},{2,6},{4,0},{6,2},{8,12},{10,14},{12,8},{14,10},{16,20},{18,... | collective-permute-start | bytes 2211848 | tf_op jit(solution)/shard_map/ppermute | solution.py:831
  173.3 12.2 %collective-permute-start.29 = (bf16[96,768]{1,0:T(8,128)(2,1)S(1)}, bf16[96,768]{1,0:T(8,128)(2,1)S(1)}, u32[]{:S(2)}, u32[]{:S(2)}) collective-permute-start(bf16[96,768]{1,0:T(8,128)(2,1)S(1)} %constant_dynamic-slice_fusion.3), channel_id=1, source_target_pairs={{0,16},{2,18},{4,20},{6,22},{8,24},{10,26},{12,28},{14,30},{16,0},... | collective-permute-start | bytes 442376 | tf_op jit(solution)/shard_map/ppermute | solution.py:831
  185.6 12.5 %collective-permute-start.31 = (bf16[96,384]{1,0:T(8,128)(2,1)S(1)}, bf16[96,384]{1,0:T(8,128)(2,1)S(1)}, u32[]{:S(2)}, u32[]{:S(2)}) collective-permute-start(bf16[96,384]{1,0:T(8,128)(2,1)S(1)} %get-tuple-element.347), channel_id=1, source_target_pairs={{0,1},{1,0},{2,3},{3,2},{4,5},{5,4},{6,7},{7,6},{8,9},{9,8},{10,11... | collective-permute-start | bytes 221192 | tf_op jit(solution)/shard_map/ppermute | solution.py:834
  188.0 10.2 %collective-permute-start.32 = (bf16[96,1920]{1,0:T(8,128)(2,1)S(1)}, bf16[96,1920]{1,0:T(8,128)(2,1)S(1)}, u32[]{:S(2)}, u32[]{:S(2)}) collective-permute-start(bf16[96,1920]{1,0:T(8,128)(2,1)S(1)} %constant_dynamic-slice_fusion.2), channel_id=1, source_target_pairs={{0,8},{2,10},{4,12},{6,14},{8,0},{10,2},{12,4},{14,6},{16,24},{18,... | collective-permute-start | bytes 1105928 | tf_op jit(solution)/shard_map/ppermute | solution.py:831
  206.7 9.7 %collective-permute-start.33 = (bf16[2,8,64,384]{3,2,1,0:T(8,128)(2,1)}, bf16[2,8,64,384]{3,2,1,0:T(8,128)(2,1)}, u32[]{:S(2)}, u32[]{:S(2)}) collective-permute-start(bf16[2,8,64,384]{3,2,1,0:T(8,128)(2,1)} %get-tuple-element.177), channel_id=1, source_target_pairs={{0,2},{2,0},{4,6},{6,4},{8,10},{10,8},{12,14},{14,12},{16,18},{18,... | collective-permute-start | bytes 2359304 | tf_op jit(solution)/shard_map/ppermute | solution.py:831
  207.4 20.0 %collective-permute-start.36 = (bf16[1,2,96,384]{3,2,1,0:T(8,128)(2,1)S(1)}, bf16[1,2,96,384]{3,2,1,0:T(8,128)(2,1)}, u32[]{:S(2)}, u32[]{:S(2)}) collective-permute-start(bf16[1,2,96,384]{3,2,1,0:T(8,128)(2,1)S(1)} %maximum_bitcast_fusion.1), channel_id=1, source_target_pairs={{0,16},{2,18},{4,20},{6,22},{8,24},{10,26},{12,28},{14,30},{16,0},... | collective-permute-start | bytes 442376 | tf_op jit(solution)/shard_map/ppermute | solution.py:831
  208.9 16.9 %collective-permute-start.35 = (bf16[48,1920]{1,0:T(8,128)(2,1)}, bf16[48,1920]{1,0:T(8,128)(2,1)}, u32[]{:S(2)}, u32[]{:S(2)}) collective-permute-start(bf16[48,1920]{1,0:T(8,128)(2,1)} %constant_dynamic-slice_fusion.1), channel_id=1, source_target_pairs={{0,16},{2,18},{4,20},{6,22},{8,24},{10,26},{12,28},{14,30},{16,0},... | collective-permute-start | bytes 552968 | tf_op jit(solution)/shard_map/ppermute | solution.py:831
  217.8 11.0 %collective-permute-start.34 = (bf16[1,8,64,384]{3,2,1,0:T(8,128)(2,1)S(1)}, bf16[1,8,64,384]{3,2,1,0:T(8,128)(2,1)S(1)}, u32[]{:S(2)}, u32[]{:S(2)}) collective-permute-start(bf16[1,8,64,384]{3,2,1,0:T(8,128)(2,1)S(1)} %get-tuple-element.257), channel_id=1, source_target_pairs={{0,4},{2,6},{4,0},{6,2},{8,12},{10,14},{12,8},{14,10},{16,20},{18,... | collective-permute-start | bytes 1179656 | tf_op jit(solution)/shard_map/ppermute | solution.py:831
  235.0 8.1 %collective-permute-start.42 = (bf16[192,576]{1,0:T(8,128)(2,1)S(1)}, bf16[192,576]{1,0:T(8,128)(2,1)S(1)}, u32[]{:S(2)}, u32[]{:S(2)}) collective-permute-start(bf16[192,576]{1,0:T(8,128)(2,1)S(1)} %dynamic-slice_convert_fusion), channel_id=1, source_target_pairs={{0,4},{2,6},{4,0},{6,2},{8,12},{10,14},{12,8},{14,10},{16,20},{18,... | collective-permute-start | bytes 663560 | tf_op jit(solution)/shard_map/ppermute | solution.py:831
  236.0 12.3 %collective-permute-start.43 = (bf16[1,48,1920]{2,1,0:T(8,128)(2,1)S(1)}, bf16[1,48,1920]{2,1,0:T(8,128)(2,1)S(1)}, u32[]{:S(2)}, u32[]{:S(2)}) collective-permute-start(bf16[1,48,1920]{2,1,0:T(8,128)(2,1)S(1)} %copy-done.35), channel_id=1, source_target_pairs={{0,16},{2,18},{4,20},{6,22},{8,24},{10,26},{12,28},{14,30},{16,0},... | collective-permute-start | bytes 552968 | tf_op jit(solution)/shard_map/ppermute | solution.py:831
  237.3 16.6 %collective-permute-start.44 = (bf16[2,2,96,384]{3,2,1,0:T(8,128)(2,1)S(1)}, bf16[2,2,96,384]{3,2,1,0:T(8,128)(2,1)S(1)}, u32[]{:S(2)}, u32[]{:S(2)}) collective-permute-start(bf16[2,2,96,384]{3,2,1,0:T(8,128)(2,1)S(1)} %copy-done.37), channel_id=1, source_target_pairs={{0,8},{2,10},{4,12},{6,14},{8,0},{10,2},{12,4},{14,6},{16,24},{18,... | collective-permute-start | bytes 884744 | tf_op jit(solution)/shard_map/ppermute | solution.py:831
  237.9 19.4 %collective-permute-start.37 = (bf16[216,384]{1,0:T(8,128)(2,1)S(1)}, bf16[216,384]{1,0:T(8,128)(2,1)S(1)}, u32[]{:S(2)}, u32[]{:S(2)}) collective-permute-start(bf16[216,384]{1,0:T(8,128)(2,1)S(1)} %copy-done.3), channel_id=1, source_target_pairs={{0,8},{2,10},{4,12},{6,14},{8,0},{10,2},{12,4},{14,6},{16,24},{18,... | collective-permute-start | bytes 497672 | tf_op jit(solution)/shard_map/ppermute | solution.py:831
  239.3 20.5 %collective-permute-start.38 = (bf16[216,384]{1,0:T(8,128)(2,1)S(1)}, bf16[216,384]{1,0:T(8,128)(2,1)S(1)}, u32[]{:S(2)}, u32[]{:S(2)}) collective-permute-start(bf16[216,384]{1,0:T(8,128)(2,1)S(1)} %get-tuple-element.185), channel_id=1, source_target_pairs={{0,16},{2,18},{4,20},{6,22},{8,24},{10,26},{12,28},{14,30},{16,0},... | collective-permute-start | bytes 497672 | tf_op jit(solution)/shard_map/ppermute | solution.py:831
  243.1 19.1 %collective-permute-start.39 = (bf16[216,384]{1,0:T(8,128)(2,1)S(1)}, bf16[216,384]{1,0:T(8,128)(2,1)S(1)}, u32[]{:S(2)}, u32[]{:S(2)}) collective-permute-start(bf16[216,384]{1,0:T(8,128)(2,1)S(1)} %get-tuple-element.186), channel_id=1, source_target_pairs={{0,24},{2,26},{4,28},{6,30},{8,16},{10,18},{12,20},{14,22},{16,8},... | collective-permute-start | bytes 497672 | tf_op jit(solution)/shard_map/ppermute | solution.py:831
  248.3 7.1 %collective-permute-start.45 = (bf16[192,576]{1,0:T(8,128)(2,1)S(1)}, bf16[192,576]{1,0:T(8,128)(2,1)S(1)}, u32[]{:S(2)}, u32[]{:S(2)}) collective-permute-start(bf16[192,576]{1,0:T(8,128)(2,1)S(1)} %get-tuple-element.234), channel_id=1, source_target_pairs={{0,1},{1,0},{2,3},{3,2},{4,5},{5,4},{6,7},{7,6},{8,9},{9,8},{10,11... | collective-permute-start | bytes 663560 | tf_op jit(solution)/shard_map/ppermute | solution.py:834
  253.9 12.4 %collective-permute-start.48 = (f32[80,128]{1,0:T(8,128)S(1)}, f32[80,128]{1,0:T(8,128)S(1)}, u32[]{:S(2)}, u32[]{:S(2)}) collective-permute-start(f32[80,128]{1,0:T(8,128)S(1)} %add.370), channel_id=1, source_target_pairs={{0,4},{2,6},{4,0},{6,2},{8,12},{10,14},{12,8},{14,10},{16,20},{18,... | collective-permute-start | bytes 122888 | tf_op jit(solution)/shard_map/ppermute | solution.py:831
  255.5 17.6 %collective-permute-start.49 = (bf16[2,48,1920]{2,1,0:T(8,128)(2,1)S(1)}, bf16[2,48,1920]{2,1,0:T(8,128)(2,1)S(1)}, u32[]{:S(2)}, u32[]{:S(2)}) collective-permute-start(bf16[2,48,1920]{2,1,0:T(8,128)(2,1)S(1)} %constant_dynamic-update-slice_fusion.8), channel_id=1, source_target_pairs={{0,8},{2,10},{4,12},{6,14},{8,0},{10,2},{12,4},{14,6},{16,24},{18,... | collective-permute-start | bytes 1105928 | tf_op jit(solution)/shard_map/ppermute | solution.py:831
  257.3 21.3 %collective-permute-start.52 = (bf16[4,2,96,384]{3,2,1,0:T(8,128)(2,1)S(1)}, bf16[4,2,96,384]{3,2,1,0:T(8,128)(2,1)S(1)}, u32[]{:S(2)}, u32[]{:S(2)}) collective-permute-start(bf16[4,2,96,384]{3,2,1,0:T(8,128)(2,1)S(1)} %constant_dynamic-update-slice_fusion.10), channel_id=1, source_target_pairs={{0,4},{2,6},{4,0},{6,2},{8,12},{10,14},{12,8},{14,10},{16,20},{18,... | collective-permute-start | bytes 1769480 | tf_op jit(solution)/shard_map/ppermute | solution.py:831
  263.1 12.4 %collective-permute-start.50 = (bf16[192,576]{1,0:T(8,128)(2,1)S(1)}, bf16[192,576]{1,0:T(8,128)(2,1)S(1)}, u32[]{:S(2)}, u32[]{:S(2)}) collective-permute-start(bf16[192,576]{1,0:T(8,128)(2,1)S(1)} %add_convert_fusion.7), channel_id=1, source_target_pairs={{0,16},{2,18},{4,20},{6,22},{8,24},{10,26},{12,28},{14,30},{16,0},... | collective-permute-start | bytes 663560 | tf_op jit(solution)/shard_map/ppermute | solution.py:831
  266.3 9.3 %collective-permute-start.51 = (f32[80,128]{1,0:T(8,128)S(1)}, f32[80,128]{1,0:T(8,128)S(1)}, u32[]{:S(2)}, u32[]{:S(2)}) collective-permute-start(f32[80,128]{1,0:T(8,128)S(1)} %add.377), channel_id=1, source_target_pairs={{0,8},{2,10},{4,12},{6,14},{8,0},{10,2},{12,4},{14,6},{16,24},{18,... | collective-permute-start | bytes 122888 | tf_op jit(solution)/shard_map/ppermute | solution.py:831
  273.1 17.1 %collective-permute-start.55 = (bf16[4,48,1920]{2,1,0:T(8,128)(2,1)S(1)}, bf16[4,48,1920]{2,1,0:T(8,128)(2,1)S(1)}, u32[]{:S(2)}, u32[]{:S(2)}) collective-permute-start(bf16[4,48,1920]{2,1,0:T(8,128)(2,1)S(1)} %constant_dynamic-update-slice_fusion.12), channel_id=1, source_target_pairs={{0,4},{2,6},{4,0},{6,2},{8,12},{10,14},{12,8},{14,10},{16,20},{18,... | collective-permute-start | bytes 2211848 | tf_op jit(solution)/shard_map/ppermute | solution.py:831
  290.4 16.1 %collective-permute-start.60 = (bf16[8,2,96,384]{3,2,1,0:T(8,128)(2,1)S(1)}, bf16[8,2,96,384]{3,2,1,0:T(8,128)(2,1)}, u32[]{:S(2)}, u32[]{:S(2)}) collective-permute-start(bf16[8,2,96,384]{3,2,1,0:T(8,128)(2,1)S(1)} %constant_dynamic-update-slice_fusion.14.near_ref), channel_id=1, source_target_pairs={{0,2},{2,0},{4,6},{6,4},{8,10},{10,8},{12,14},{14,12},{16,18},{18,... | collective-permute-start | bytes 3538952 | tf_op jit(solution)/shard_map/ppermute | solution.py:831
  290.9 13.2 %collective-permute-start.58 = (bf16[1,2,192,576]{3,2,1,0:T(8,128)(2,1)S(1)}, bf16[1,2,192,576]{3,2,1,0:T(8,128)(2,1)S(1)}, u32[]{:S(2)}, u32[]{:S(2)}) collective-permute-start(bf16[1,2,192,576]{3,2,1,0:T(8,128)(2,1)S(1)} %maximum_bitcast_fusion), channel_id=1, source_target_pairs={{0,4},{2,6},{4,0},{6,2},{8,12},{10,14},{12,8},{14,10},{16,20},{18,... | collective-permute-start | bytes 1327112 | tf_op jit(solution)/shard_map/ppermute | solution.py:831
  293.2 8.5 %collective-permute-start.57 = (f32[80,128]{1,0:T(8,128)S(1)}, f32[80,128]{1,0:T(8,128)S(1)}, u32[]{:S(2)}, u32[]{:S(2)}) collective-permute-start(f32[80,128]{1,0:T(8,128)S(1)} %add.379), channel_id=1, source_target_pairs={{0,1},{1,0},{2,3},{3,2},{4,5},{5,4},{6,7},{7,6},{8,9},{9,8},{10,11... | collective-permute-start | bytes 122888 | tf_op jit(solution)/shard_map/ppermute | solution.py:834
  305.0 9.5 %collective-permute-start.59 = (bf16[2,2,192,576]{3,2,1,0:T(8,128)(2,1)}, bf16[2,2,192,576]{3,2,1,0:T(8,128)(2,1)}, u32[]{:S(2)}, u32[]{:S(2)}) collective-permute-start(bf16[2,2,192,576]{3,2,1,0:T(8,128)(2,1)} %constant_dynamic-update-slice_fusion.18.near_ref), channel_id=1, source_target_pairs={{0,2},{2,0},{4,6},{6,4},{8,10},{10,8},{12,14},{14,12},{16,18},{18,... | collective-permute-start | bytes 2654216 | tf_op jit(solution)/shard_map/ppermute | solution.py:831
  (74 other events, 467.0 us)

commit v2 on v1

--- a/solution.py
+++ b/solution.py
@@ -133,7 +133,7 @@
             TILE // GROUP,
             bias_group,
             tuple(jnp.full((8, 128), NEGATIVE, F32) for _ in range(chunks * heads)),
-            unroll=2,
+            unroll=8,
         )
         for chunk in range(chunks):
             lanes = slice(offset + chunk * 128, offset + chunk * 128 + 128)

time: 323 us -> 322 us (level)
  Pallas kernels: 89.8 us -> 85.8 us
    pallas_call x2, Pallas kernels: 25.5 us -> 22 us  [attention_forward(): pl.pallas_call(functools.partial(forward_kernel, call, count, heads), gri...]
  transfers between devices with their start and end apart: 61 -> 61, of which waited for: 26 -> 26; matrix products, arithmetic and copies ran while one was open for 21% -> 22% of each run, Pallas kernels for 23% -> 22%
where the time goes in v2:
time: 322 us; the launch traced here: 316 us
  Pallas kernels  85.8 us (27%)
  waiting for transfers between devices  76.5 us (24%)
  starting transfers between devices  63.4 us (20%)
  other arithmetic  41.8 us (13%)
  local copies, waits for them, and re-layouts  29.1 us (9%)
  matrix products  16.8 us (5%)
    ppermute x47, waiting for transfers between devices, swap(): return lax.ppermute(value, 'ctx', [(i, i ^ bit) for i in range(ctx)])  59.3 us
    ppermute x47, starting transfers between devices, swap(): return lax.ppermute(value, 'ctx', [(i, i ^ bit) for i in range(ctx)])  46.8 us
    pallas_call x4, Pallas kernels, attention_backward(): pl.pallas_call(functools.partial(backward_kernel, branch, heads), grid=(t...  41.1 us
    pallas_call x2, Pallas kernels, attention_forward(): pl.pallas_call(functools.partial(forward_kernel, call, count, heads), gri...  22 us
    ppermute x14, waiting for transfers between devices, swap_side(): return lax.ppermute(value, 'wt', [(0, 1), (1, 0)])  17.3 us
    ppermute x14, starting transfers between devices, swap_side(): return lax.ppermute(value, 'wt', [(0, 1), (1, 0)])  16.6 us
    pallas_call x2, Pallas kernels, widen_rows(): pl.pallas_call(functools.partial(widen_kernel, group), grid_spec=pltpu.Pr...  10.7 us
    unnamed x139, local copies, waits for them, and re-layouts  7.97 us
  transfers between devices with their start and end apart: 61, of which 26 were waited for; matrix products, arithmetic and copies ran while one was open for 22% of the time, Pallas kernels for 22%

profile of v2, /device:TPU:0, one launch (start us, length us, event | category | flops | bytes accessed | tf_op | source)
XLA Modules:
  0.0 316.1 jit_solution(14366434987855600218)
XLA Ops:
  0.7 1.8 pad_maximum_fusion.30
  2.5 4.0 %collective-permute-start.1 = (bf16[152,768]{1,0:T(8,128)(2,1)}, bf16[152,768]{1,0:T(8,128)(2,1)}, u32[]{:S(2)}, u32[]{:S(2)}) collective-permute-start(bf16[152,768]{1,0:T(8,128)(2,1)} %pad_maximum_fusion.30), channel_id=1, source_target_pairs={{0,16},{2,18},{4,20},{6,22},{8,24},{10,26},{12,28},{14,30},{16,0},... | collective-permute-start | bytes 700424 | tf_op jit(solution)/shard_map/ppermute | solution.py:831
  11.1 2.0 slice_select_fusion.7
  26.7 2.5 collective-permute-done.3
  29.2 2.0 collective-permute-done.4
  40.4 4.5 %collective-permute-done.6 = bf16[1,8,64,384]{3,2,1,0:T(8,128)(2,1)S(1)} collective-permute-done((bf16[1,8,64,384]{3,2,1,0:T(8,128)(2,1)S(1)}, bf16[1,8,64,384]{3,2,1,0:T(8,128)(2,1)S(1)}, u32[]{:S(2)}, u32[]{:S(2)}) %collective-permute-start.6) | collective-permute-done | bytes 393248 | tf_op jit(solution)/shard_map/ppermute | solution.py:831
  45.3 11.1 %attention_forward.2 = (f32[3,2048,640]{2,1,0:T(8,128)}, bf16[2048,640]{1,0:T(8,128)(2,1)S(1)}, bf16[2048,640]{1,0:T(8,128)(2,1)S(1)}, f32[8,8,640]{2,1,0:T(8,12...) custom-call(s32[32]{0:T(128)S(1)} %reshape.332.refs_0_, ...), custom_call_target="tpu_custom_call" | custom-call | flops 15032385536 | bytes 12582912 | tf_op jit(solution)/shard_map/attention_forward/pallas_call | solution.py:243
  56.5 10.9 %attention_forward.3 = (f32[3,2048,640]{2,1,0:T(8,128)}, bf16[2048,640]{1,0:T(8,128)(2,1)S(1)}, bf16[2048,640]{1,0:T(8,128)(2,1)S(1)}, f32[8,8,640]{2,1,0:T(8,12...) custom-call(s32[32]{0:T(128)S(1)} %reshape.332.refs_0_, ...), custom_call_target="tpu_custom_call", output_to_operand_aliasing={{0}: (6, {}), {1}: (7, {}), {2}: (8, {}), {3}: (9, {})} | custom-call | flops 15032385536 | bytes 12582912 | tf_op jit(solution)/shard_map/attention_forward/pallas_call | solution.py:243
  69.0 2.8 collective-permute-start.10
  76.4 2.4 collective-permute-done.9
  85.0 4.0 %collective-permute-done.14 = bf16[152,768]{1,0:T(8,128)(2,1)S(1)} collective-permute-done((bf16[152,768]{1,0:T(8,128)(2,1)S(1)}, bf16[152,768]{1,0:T(8,128)(2,1)S(1)}, u32[]{:S(2)}, u32[]{:S(2)}) %collective-permute-start.14) | collective-permute-done | bytes 233504 | tf_op jit(solution)/shard_map/ppermute | solution.py:834
  89.0 4.6 %multiply_convert_fusion = (bf16[304,1536]{1,0:T(8,128)(2,1)S(1)}, f32[304,1536]{1,0:T(8,128)S(1)}, f32[304,1536]{1,0:T(8,128)S(1)}) fusion(f32[1536]{0:T(1024)S(1)} %copy-done.51, bf16[768,1536]{1,0:T(8,128)(2,1)S(1)} %copy-done, bf16[152,768]{1,0:T(8,128)(2,1)S(1)} %collective-permute-done.14, bf16[152,768]{1,0:T(8,128)(2,1)S(1)} %fusion.50), kind=kOutput, calls=%fused_computation.10 | convolution fusion | flops 748978176 | bytes 7501824 | tf_op jit(solution)/shard_map/dot_general | solution.py:38
  95.1 1.8 collective-permute-start.17
  98.3 3.6 %collective-permute-done.17 = bf16[152,768]{1,0:T(8,128)(2,1)S(1)} collective-permute-done((bf16[152,768]{1,0:T(8,128)(2,1)S(1)}, bf16[152,768]{1,0:T(8,128)(2,1)S(1)}, u32[]{:S(2)}, u32[]{:S(2)}) %collective-permute-start.17) | collective-permute-done | bytes 233504 | tf_op jit(solution)/shard_map/ppermute | solution.py:834
  105.0 1.7 collective-permute-start.18
  108.1 3.0 collective-permute-done.18
  111.0 1.8 convert_reduce_fusion
  113.8 1.8 collective-permute-start.19
  119.3 1.7 collective-permute-done.19
  124.4 2.5 collective-permute-start.25
  127.2 2.4 collective-permute-done.25
  131.9 2.1 collective-permute-start.21
  136.1 1.9 collective-permute-start.22
  140.5 2.0 collective-permute-done.22.refs_3_
  142.4 1.9 arrange_rows.1.refs_6_
  144.4 5.4 %collective-permute-done.26 = bf16[384,768]{1,0:T(8,128)(2,1)} collective-permute-done((bf16[384,768]{1,0:T(8,128)(2,1)S(1)}, bf16[384,768]{1,0:T(8,128)(2,1)}, u32[]{:S(2)}, u32[]{:S(2)}) %collective-permute-start.26) | collective-permute-done | bytes 589856 | tf_op jit(solution)/shard_map/ppermute | solution.py:831
  152.2 1.7 add_convert_fusion
  155.6 13.1 %attention_backward.4 = (f32[192,640]{1,0:T(8,128)}, f32[128,192]{1,0:T(8,128)}, f32[2,8,64,384]{3,2,1,0:T(8,128)}, bf16[2,8,64,384]{3,2,1,0:T(8,128)(2,1)}) custom-call(f32[3,2048,640]{2,1,0:T(8,128)} %get-tuple-element.139.refs_0_, bf16[2048,640]{1,0:T(8,128)(2,1)} %copy-done.7, bf16[2048,640]{1,0:T(8,128)(2,1)} %copy-done.8, f32[8,8,640]{2,1,0:T(8,128)} %copy-done.10, ...), custom_call_target="tpu_custom_call" | custom-call | flops 8589934592 | bytes 6291456 | tf_op jit(solution)/shard_map/attention_backward/pallas_call | solution.py:438
  171.2 10.8 %attention_backward.5 = (f32[192,640]{1,0:T(8,128)}, f32[128,192]{1,0:T(8,128)}, f32[2,8,64,384]{3,2,1,0:T(8,128)}, bf16[2,8,64,384]{3,2,1,0:T(8,128)(2,1)}) custom-call(f32[3,2048,640]{2,1,0:T(8,128)} %get-tuple-element.139.refs_0_, bf16[2048,640]{1,0:T(8,128)(2,1)} %copy-done.7, ...), custom_call_target="tpu_custom_call", output_to_operand_aliasing={{2}: (11, {}), {3}: (12, {})} | custom-call | flops 8589934592 | bytes 6291456 | tf_op jit(solution)/shard_map/attention_backward/pallas_call | solution.py:438
  182.1 2.1 collective-permute-start.31
  184.9 9.6 %attention_backward.6 = (f32[192,640]{1,0:T(8,128)}, f32[128,192]{1,0:T(8,128)}, f32[2,8,64,384]{3,2,1,0:T(8,128)}, bf16[2,8,64,384]{3,2,1,0:T(8,128)(2,1)}) custom-call(f32[3,2048,640]{2,1,0:T(8,128)} %get-tuple-element.139.refs_0_, bf16[2048,640]{1,0:T(8,128)(2,1)} %copy-done.7, ...), custom_call_target="tpu_custom_call", output_to_operand_aliasing={{2}: (11, {}), {3}: (12, {})} | custom-call | flops 8589934592 | bytes 6291456 | tf_op jit(solution)/shard_map/attention_backward/pallas_call | solution.py:438
  195.4 7.7 %attention_backward.7 = (f32[192,640]{1,0:T(8,128)}, f32[128,192]{1,0:T(8,128)}, f32[2,8,64,384]{3,2,1,0:T(8,128)}, bf16[2,8,64,384]{3,2,1,0:T(8,128)(2,1)}) custom-call(f32[3,2048,640]{2,1,0:T(8,128)} %get-tuple-element.139.refs_0_, bf16[2048,640]{1,0:T(8,128)(2,1)} %copy-done.7, ...), custom_call_target="tpu_custom_call", output_to_operand_aliasing={{2}: (11, {}), {3}: (12, {})} | custom-call | flops 8589934592 | bytes 6291456 | tf_op jit(solution)/shard_map/attention_backward/pallas_call | solution.py:438
  214.8 7.3 %collective-permute-done.35 = bf16[48,1920]{1,0:T(8,128)(2,1)} collective-permute-done((bf16[48,1920]{1,0:T(8,128)(2,1)}, bf16[48,1920]{1,0:T(8,128)(2,1)}, u32[]{:S(2)}, u32[]{:S(2)}) %collective-permute-start.35) | collective-permute-done | bytes 184352 | tf_op jit(solution)/shard_map/ppermute | solution.py:831
  225.5 2.1 finish_heads.1
  237.5 2.0 collective-permute-done.42
  240.8 3.9 %collective-permute-done.43 = bf16[1,48,1920]{2,1,0:T(8,128)(2,1)S(1)} collective-permute-done((bf16[1,48,1920]{2,1,0:T(8,128)(2,1)S(1)}, bf16[1,48,1920]{2,1,0:T(8,128)(2,1)S(1)}, u32[]{:S(2)}, u32[]{:S(2)}) %collective-permute-start.43) | collective-permute-done | bytes 184352 | tf_op jit(solution)/shard_map/ppermute | solution.py:831
  244.8 5.5 %collective-permute-done.44 = bf16[2,2,96,384]{3,2,1,0:T(8,128)(2,1)S(1)} collective-permute-done((bf16[2,2,96,384]{3,2,1,0:T(8,128)(2,1)S(1)}, bf16[2,2,96,384]{3,2,1,0:T(8,128)(2,1)S(1)}, u32[]{:S(2)}, u32[]{:S(2)}) %collective-permute-start.44) | collective-permute-done | bytes 294944 | tf_op jit(solution)/shard_map/ppermute | solution.py:831
  252.0 1.8 collective-permute-done.37
  253.8 2.4 collective-permute-start.52
  256.2 2.4 collective-permute-done.39
  262.8 2.8 collective-permute-start.51
  265.6 3.9 %collective-permute-done.49 = bf16[2,48,1920]{2,1,0:T(8,128)(2,1)S(1)} collective-permute-done((bf16[2,48,1920]{2,1,0:T(8,128)(2,1)S(1)}, bf16[2,48,1920]{2,1,0:T(8,128)(2,1)S(1)}, u32[]{:S(2)}, u32[]{:S(2)}) %collective-permute-start.49) | collective-permute-done | bytes 368672 | tf_op jit(solution)/shard_map/ppermute | solution.py:831
  272.1 2.8 collective-permute-start.54
  275.0 3.7 %collective-permute-done.53 = bf16[1,192,576]{2,1,0:T(8,128)(2,1)S(1)} collective-permute-done((bf16[1,192,576]{2,1,0:T(8,128)(2,1)S(1)}, bf16[1,192,576]{2,1,0:T(8,128)(2,1)S(1)}, u32[]{:S(2)}, u32[]{:S(2)}) %collective-permute-start.53) | collective-permute-done | bytes 221216 | tf_op jit(solution)/shard_map/ppermute | solution.py:831
  278.8 7.7 %collective-permute-done.55 = bf16[4,48,1920]{2,1,0:T(8,128)(2,1)S(1)} collective-permute-done((bf16[4,48,1920]{2,1,0:T(8,128)(2,1)S(1)}, bf16[4,48,1920]{2,1,0:T(8,128)(2,1)S(1)}, u32[]{:S(2)}, u32[]{:S(2)}) %collective-permute-start.55) | collective-permute-done | bytes 737312 | tf_op jit(solution)/shard_map/ppermute | solution.py:831
  292.6 5.5 %widen_rows.2 = (f32[768,1536]{1,0:T(8,128)}, f32[768,384]{1,0:T(8,128)}) custom-call(s32[2]{0:T(128)S(1)} %pad_add_fusion.8.order_ref, bf16[8,48,1920]{2,1,0:T(8,128)(2,1)S(1)} %constant_dynamic-update-slice_fusion.16.near_ref, bf16[8,48,1920]{2,1,0:T(8,128)(2,1)} %collective-permute-done.56.far_ref), custom_call_target="tpu_custom_call" | custom-call | bytes 8847360 | tf_op jit(solution)/shard_map/widen_rows/pallas_call | solution.py:557
  302.9 5.2 %widen_rows.3 = f32[2,1536,384]{2,1,0:T(8,128)} custom-call(s32[2]{0:T(128)S(1)} %pad_add_fusion.8.order_ref, bf16[8,2,96,384]{3,2,1,0:T(8,128)(2,1)S(1)} %constant_dynamic-update-slice_fusion.14.near_ref, bf16[8,2,96,384]{3,2,1,0:T(8,128)(2,1)} %collective-permute-done.60.far_ref), custom_call_target="tpu_custom_call" | custom-call | bytes 7077888 | tf_op jit(solution)/shard_map/widen_rows/pallas_call | solution.py:557
  310.8 5.0 %widen_heads.1 = (f32[768,384]{1,0:T(8,128)}, f32[768,384]{1,0:T(8,128)}, f32[768,384]{1,0:T(8,128)}) custom-call(s32[2]{0:T(128)} %pad_add_fusion.7.order_ref, bf16[2,2,192,576]{3,2,1,0:T(8,128)(2,1)} %constant_dynamic-update-slice_fusion.18.near_ref, bf16[2,2,192,576]{3,2,1,0:T(8,128)(2,1)} %collective-permute-done.59.far_ref), custom_call_target="tpu_custom_call" | custom-call | bytes 5308416 | tf_op jit(solution)/shard_map/widen_heads/pallas_call | solution.py:605
  (452 shorter events, 118.2 us)
Async XLA Ops:
  2.5 22.5 %collective-permute-start.1 = (bf16[152,768]{1,0:T(8,128)(2,1)}, bf16[152,768]{1,0:T(8,128)(2,1)}, u32[]{:S(2)}, u32[]{:S(2)}) collective-permute-start(bf16[152,768]{1,0:T(8,128)(2,1)} %pad_maximum_fusion.30), channel_id=1, source_target_pairs={{0,16},{2,18},{4,20},{6,22},{8,24},{10,26},{12,28},{14,30},{16,0},... | collective-permute-start | bytes 700424 | tf_op jit(solution)/shard_map/ppermute | solution.py:831
  6.5 18.5 %collective-permute-start = (bf16[152,768]{1,0:T(8,128)(2,1)}, bf16[152,768]{1,0:T(8,128)(2,1)}, u32[]{:S(2)}, u32[]{:S(2)}) collective-permute-start(bf16[152,768]{1,0:T(8,128)(2,1)} %pad_maximum_fusion.30), channel_id=1, source_target_pairs={{0,24},{2,26},{4,28},{6,30},{8,16},{10,18},{12,20},{14,22},{16,8},... | collective-permute-start | bytes 700424 | tf_op jit(solution)/shard_map/ppermute | solution.py:831
  7.9 17.2 %collective-permute-start.2 = (bf16[152,768]{1,0:T(8,128)(2,1)}, bf16[152,768]{1,0:T(8,128)(2,1)}, u32[]{:S(2)}, u32[]{:S(2)}) collective-permute-start(bf16[152,768]{1,0:T(8,128)(2,1)} %pad_maximum_fusion.30), channel_id=1, source_target_pairs={{0,8},{2,10},{4,12},{6,14},{8,0},{10,2},{12,4},{14,6},{16,24},{18,... | collective-permute-start | bytes 700424 | tf_op jit(solution)/shard_map/ppermute | solution.py:831
  9.6 11.5 %collective-permute-start.5 = (bf16[32,384]{1,0:T(8,128)(2,1)}, bf16[32,384]{1,0:T(8,128)(2,1)}, u32[]{:S(2)}, u32[]{:S(2)}) collective-permute-start(bf16[32,384]{1,0:T(8,128)(2,1)} %pack_vectors.1.own_ref), channel_id=1, source_target_pairs={{0,1},{1,0},{2,3},{3,2},{4,5},{5,4},{6,7},{7,6},{8,9},{9,8},{10,11... | collective-permute-start | bytes 73736 | tf_op jit(solution)/shard_map/ppermute | solution.py:834
  16.8 12.4 %collective-permute-start.3 = (bf16[384,576]{1,0:T(8,128)(2,1)}, bf16[384,576]{1,0:T(8,128)(2,1)}, u32[]{:S(2)}, u32[]{:S(2)}) collective-permute-start(bf16[384,576]{1,0:T(8,128)(2,1)} %constant_dynamic-slice_fusion.11), channel_id=1, source_target_pairs={{0,1},{1,0},{2,3},{3,2},{4,5},{5,4},{6,7},{7,6},{8,9},{9,8},{10,11... | collective-permute-start | bytes 1327112 | tf_op jit(solution)/shard_map/ppermute | solution.py:834
  33.6 11.2 %collective-permute-start.6 = (bf16[1,8,64,384]{3,2,1,0:T(8,128)(2,1)S(1)}, bf16[1,8,64,384]{3,2,1,0:T(8,128)(2,1)S(1)}, u32[]{:S(2)}, u32[]{:S(2)}) collective-permute-start(bf16[1,8,64,384]{3,2,1,0:T(8,128)(2,1)S(1)} %bitcast.103), channel_id=1, source_target_pairs={{0,4},{2,6},{4,0},{6,2},{8,12},{10,14},{12,8},{14,10},{16,20},{18,... | collective-permute-start | bytes 1179656 | tf_op jit(solution)/shard_map/ppermute | solution.py:831
  35.2 9.7 %collective-permute-start.8 = (bf16[1,8,64,384]{3,2,1,0:T(8,128)(2,1)S(1)}, bf16[1,8,64,384]{3,2,1,0:T(8,128)(2,1)S(1)}, u32[]{:S(2)}, u32[]{:S(2)}) collective-permute-start(bf16[1,8,64,384]{3,2,1,0:T(8,128)(2,1)S(1)} %bitcast.104), channel_id=1, source_target_pairs={{0,2},{2,0},{4,6},{6,4},{8,10},{10,8},{12,14},{14,12},{16,18},{18,... | collective-permute-start | bytes 1179656 | tf_op jit(solution)/shard_map/ppermute | solution.py:831
  36.8 36.5 %collective-permute-start.12 = (bf16[384,384]{1,0:T(8,128)(2,1)S(1)}, bf16[384,384]{1,0:T(8,128)(2,1)S(1)}, u32[]{:S(2)}, u32[]{:S(2)}) collective-permute-start(bf16[384,384]{1,0:T(8,128)(2,1)S(1)} %constant_dynamic-slice_fusion.8), channel_id=1, source_target_pairs={{0,1},{1,0},{2,3},{3,2},{4,5},{5,4},{6,7},{7,6},{8,9},{9,8},{10,11... | collective-permute-start | bytes 884744 | tf_op jit(solution)/shard_map/ppermute | solution.py:834
  38.2 36.7 %collective-permute-start.15 = (bf16[768,384]{1,0:T(8,128)(2,1)S(1)}, bf16[768,384]{1,0:T(8,128)(2,1)S(1)}, u32[]{:S(2)}, u32[]{:S(2)}) collective-permute-start(bf16[768,384]{1,0:T(8,128)(2,1)S(1)} %constant_dynamic-slice_fusion.7), channel_id=1, source_target_pairs={{0,1},{1,0},{2,3},{3,2},{4,5},{5,4},{6,7},{7,6},{8,9},{9,8},{10,11... | collective-permute-start | bytes 1769480 | tf_op jit(solution)/shard_map/ppermute | solution.py:834
  39.2 35.7 %collective-permute-start.46 = (bf16[384,576]{1,0:T(8,128)(2,1)S(1)}, bf16[384,576]{1,0:T(8,128)(2,1)S(1)}, u32[]{:S(2)}, u32[]{:S(2)}) collective-permute-start(bf16[384,576]{1,0:T(8,128)(2,1)S(1)} %constant_dynamic-slice_fusion), channel_id=1, source_target_pairs={{0,1},{1,0},{2,3},{3,2},{4,5},{5,4},{6,7},{7,6},{8,9},{9,8},{10,11... | collective-permute-start | bytes 1327112 | tf_op jit(solution)/shard_map/ppermute | solution.py:834
  44.8 11.5 %collective-permute-start.7 = (bf16[1,8,64,384]{3,2,1,0:T(8,128)(2,1)S(1)}, bf16[1,8,64,384]{3,2,1,0:T(8,128)(2,1)S(1)}, u32[]{:S(2)}, u32[]{:S(2)}) collective-permute-start(bf16[1,8,64,384]{3,2,1,0:T(8,128)(2,1)S(1)} %collective-permute-done.6), channel_id=1, source_target_pairs={{0,2},{2,0},{4,6},{6,4},{8,10},{10,8},{12,14},{14,12},{16,18},{18,... | collective-permute-start | bytes 1179656 | tf_op jit(solution)/shard_map/ppermute | solution.py:831
  69.0 7.3 %collective-permute-start.10 = (bf16[88,384]{1,0:T(8,128)(2,1)S(1)}, bf16[88,384]{1,0:T(8,128)(2,1)S(1)}, u32[]{:S(2)}, u32[]{:S(2)}) collective-permute-start(bf16[88,384]{1,0:T(8,128)(2,1)S(1)} %broadcast_select_fusion.66), channel_id=1, source_target_pairs={{0,16},{2,18},{4,20},{6,22},{8,24},{10,26},{12,28},{14,30},{16,0},... | collective-permute-start | bytes 202760 | tf_op jit(solution)/shard_map/ppermute | solution.py:831
  72.0 6.8 %collective-permute-start.9 = (bf16[88,384]{1,0:T(8,128)(2,1)S(1)}, bf16[88,384]{1,0:T(8,128)(2,1)S(1)}, u32[]{:S(2)}, u32[]{:S(2)}) collective-permute-start(bf16[88,384]{1,0:T(8,128)(2,1)S(1)} %broadcast_select_fusion.67), channel_id=1, source_target_pairs={{0,24},{2,26},{4,28},{6,30},{8,16},{10,18},{12,20},{14,22},{16,8},... | collective-permute-start | bytes 202760 | tf_op jit(solution)/shard_map/ppermute | solution.py:831
  74.9 18.7 %collective-permute-start.16 = (bf16[768,384]{1,0:T(8,128)(2,1)S(1)}, bf16[768,384]{1,0:T(8,128)(2,1)S(1)}, u32[]{:S(2)}, u32[]{:S(2)}) collective-permute-start(bf16[768,384]{1,0:T(8,128)(2,1)S(1)} %collective-permute-done.15), channel_id=1, source_target_pairs={{0,2},{2,0},{4,6},{6,4},{8,10},{10,8},{12,14},{14,12},{16,18},{18,... | collective-permute-start | bytes 1769480 | tf_op jit(solution)/shard_map/ppermute | solution.py:831
  81.6 7.4 %collective-permute-start.14 = (bf16[152,768]{1,0:T(8,128)(2,1)S(1)}, bf16[152,768]{1,0:T(8,128)(2,1)S(1)}, u32[]{:S(2)}, u32[]{:S(2)}) collective-permute-start(bf16[152,768]{1,0:T(8,128)(2,1)S(1)} %fusion.50), channel_id=1, source_target_pairs={{0,1},{1,0},{2,3},{3,2},{4,5},{5,4},{6,7},{7,6},{8,9},{9,8},{10,11... | collective-permute-start | bytes 700424 | tf_op jit(solution)/shard_map/ppermute | solution.py:834
  113.8 7.2 %collective-permute-start.19 = (bf16[152,768]{1,0:T(8,128)(2,1)S(1)}, bf16[152,768]{1,0:T(8,128)(2,1)S(1)}, u32[]{:S(2)}, u32[]{:S(2)}) collective-permute-start(bf16[152,768]{1,0:T(8,128)(2,1)S(1)} %slice.1018), channel_id=1, source_target_pairs={{0,1},{1,0},{2,3},{3,2},{4,5},{5,4},{6,7},{7,6},{8,9},{9,8},{10,11... | collective-permute-start | bytes 700424 | tf_op jit(solution)/shard_map/ppermute | solution.py:834
  116.4 17.6 %collective-permute-start.23 = (bf16[768,768]{1,0:T(8,128)(2,1)S(1)}, bf16[768,768]{1,0:T(8,128)(2,1)S(1)}, u32[]{:S(2)}, u32[]{:S(2)}) collective-permute-start(bf16[768,768]{1,0:T(8,128)(2,1)S(1)} %convolution_convert_fusion.2), channel_id=1, source_target_pairs={{0,2},{2,0},{4,6},{6,4},{8,10},{10,8},{12,14},{14,12},{16,18},{18,... | collective-permute-start | bytes 3538952 | tf_op jit(solution)/shard_map/ppermute | solution.py:831
  116.5 10.5 %collective-permute-start.24 = (bf16[152,768]{1,0:T(8,128)(2,1)S(1)}, bf16[152,768]{1,0:T(8,128)(2,1)S(1)}, u32[]{:S(2)}, u32[]{:S(2)}) collective-permute-start(bf16[152,768]{1,0:T(8,128)(2,1)S(1)} %maximum_maximum_fusion), channel_id=1, source_target_pairs={{0,1},{1,0},{2,3},{3,2},{4,5},{5,4},{6,7},{7,6},{8,9},{9,8},{10,11... | collective-permute-start | bytes 700424 | tf_op jit(solution)/shard_map/ppermute | solution.py:834
  131.3 20.9 %collective-permute-start.27 = (bf16[384,1920]{1,0:T(8,128)(2,1)}, bf16[384,1920]{1,0:T(8,128)(2,1)}, u32[]{:S(2)}, u32[]{:S(2)}) collective-permute-start(bf16[384,1920]{1,0:T(8,128)(2,1)} %pad_maximum_fusion.6), channel_id=1, source_target_pairs={{0,2},{2,0},{4,6},{6,4},{8,10},{10,8},{12,14},{14,12},{16,18},{18,... | collective-permute-start | bytes 4423688 | tf_op jit(solution)/shard_map/ppermute | solution.py:831
  131.4 7.8 %collective-permute-start.20 = (bf16[88,384]{1,0:T(8,128)(2,1)S(1)}, bf16[88,384]{1,0:T(8,128)(2,1)S(1)}, u32[]{:S(2)}, u32[]{:S(2)}) collective-permute-start(bf16[88,384]{1,0:T(8,128)(2,1)S(1)} %broadcast_select_fusion.58), channel_id=1, source_target_pairs={{0,8},{2,10},{4,12},{6,14},{8,0},{10,2},{12,4},{14,6},{16,24},{18,... | collective-permute-start | bytes 202760 | tf_op jit(solution)/shard_map/ppermute | solution.py:831
  131.9 7.3 %collective-permute-start.21 = (bf16[88,384]{1,0:T(8,128)(2,1)S(1)}, bf16[88,384]{1,0:T(8,128)(2,1)S(1)}, u32[]{:S(2)}, u32[]{:S(2)}) collective-permute-start(bf16[88,384]{1,0:T(8,128)(2,1)S(1)} %broadcast_select_fusion.57), channel_id=1, source_target_pairs={{0,16},{2,18},{4,20},{6,22},{8,24},{10,26},{12,28},{14,30},{16,0},... | collective-permute-start | bytes 202760 | tf_op jit(solution)/shard_map/ppermute | solution.py:831
  134.4 15.4 %collective-permute-start.26 = (bf16[384,768]{1,0:T(8,128)(2,1)S(1)}, bf16[384,768]{1,0:T(8,128)(2,1)}, u32[]{:S(2)}, u32[]{:S(2)}) collective-permute-start(bf16[384,768]{1,0:T(8,128)(2,1)S(1)} %constant_dynamic-slice_fusion.6), channel_id=1, source_target_pairs={{0,4},{2,6},{4,0},{6,2},{8,12},{10,14},{12,8},{14,10},{16,20},{18,... | collective-permute-start | bytes 1769480 | tf_op jit(solution)/shard_map/ppermute | solution.py:831
  151.2 17.5 %collective-permute-start.28 = (bf16[192,768]{1,0:T(8,128)(2,1)S(1)}, bf16[192,768]{1,0:T(8,128)(2,1)}, u32[]{:S(2)}, u32[]{:S(2)}) collective-permute-start(bf16[192,768]{1,0:T(8,128)(2,1)S(1)} %constant_dynamic-slice_fusion.5), channel_id=1, source_target_pairs={{0,8},{2,10},{4,12},{6,14},{8,0},{10,2},{12,4},{14,6},{16,24},{18,... | collective-permute-start | bytes 884744 | tf_op jit(solution)/shard_map/ppermute | solution.py:831
  154.0 30.1 %collective-permute-start.30 = (bf16[192,1920]{1,0:T(8,128)(2,1)S(1)}, bf16[192,1920]{1,0:T(8,128)(2,1)S(1)}, u32[]{:S(2)}, u32[]{:S(2)}) collective-permute-start(bf16[192,1920]{1,0:T(8,128)(2,1)S(1)} %constant_dynamic-slice_fusion.4), channel_id=1, source_target_pairs={{0,4},{2,6},{4,0},{6,2},{8,12},{10,14},{12,8},{14,10},{16,20},{18,... | collective-permute-start | bytes 2211848 | tf_op jit(solution)/shard_map/ppermute | solution.py:831
  169.8 12.2 %collective-permute-start.29 = (bf16[96,768]{1,0:T(8,128)(2,1)S(1)}, bf16[96,768]{1,0:T(8,128)(2,1)S(1)}, u32[]{:S(2)}, u32[]{:S(2)}) collective-permute-start(bf16[96,768]{1,0:T(8,128)(2,1)S(1)} %constant_dynamic-slice_fusion.3), channel_id=1, source_target_pairs={{0,16},{2,18},{4,20},{6,22},{8,24},{10,26},{12,28},{14,30},{16,0},... | collective-permute-start | bytes 442376 | tf_op jit(solution)/shard_map/ppermute | solution.py:831
  182.1 12.5 %collective-permute-start.31 = (bf16[96,384]{1,0:T(8,128)(2,1)S(1)}, bf16[96,384]{1,0:T(8,128)(2,1)S(1)}, u32[]{:S(2)}, u32[]{:S(2)}) collective-permute-start(bf16[96,384]{1,0:T(8,128)(2,1)S(1)} %get-tuple-element.347), channel_id=1, source_target_pairs={{0,1},{1,0},{2,3},{3,2},{4,5},{5,4},{6,7},{7,6},{8,9},{9,8},{10,11... | collective-permute-start | bytes 221192 | tf_op jit(solution)/shard_map/ppermute | solution.py:834
  184.4 10.2 %collective-permute-start.32 = (bf16[96,1920]{1,0:T(8,128)(2,1)S(1)}, bf16[96,1920]{1,0:T(8,128)(2,1)S(1)}, u32[]{:S(2)}, u32[]{:S(2)}) collective-permute-start(bf16[96,1920]{1,0:T(8,128)(2,1)S(1)} %constant_dynamic-slice_fusion.2), channel_id=1, source_target_pairs={{0,8},{2,10},{4,12},{6,14},{8,0},{10,2},{12,4},{14,6},{16,24},{18,... | collective-permute-start | bytes 1105928 | tf_op jit(solution)/shard_map/ppermute | solution.py:831
  203.1 9.7 %collective-permute-start.33 = (bf16[2,8,64,384]{3,2,1,0:T(8,128)(2,1)}, bf16[2,8,64,384]{3,2,1,0:T(8,128)(2,1)}, u32[]{:S(2)}, u32[]{:S(2)}) collective-permute-start(bf16[2,8,64,384]{3,2,1,0:T(8,128)(2,1)} %get-tuple-element.177), channel_id=1, source_target_pairs={{0,2},{2,0},{4,6},{6,4},{8,10},{10,8},{12,14},{14,12},{16,18},{18,... | collective-permute-start | bytes 2359304 | tf_op jit(solution)/shard_map/ppermute | solution.py:831
  203.8 20.0 %collective-permute-start.36 = (bf16[1,2,96,384]{3,2,1,0:T(8,128)(2,1)S(1)}, bf16[1,2,96,384]{3,2,1,0:T(8,128)(2,1)}, u32[]{:S(2)}, u32[]{:S(2)}) collective-permute-start(bf16[1,2,96,384]{3,2,1,0:T(8,128)(2,1)S(1)} %maximum_bitcast_fusion.1), channel_id=1, source_target_pairs={{0,16},{2,18},{4,20},{6,22},{8,24},{10,26},{12,28},{14,30},{16,0},... | collective-permute-start | bytes 442376 | tf_op jit(solution)/shard_map/ppermute | solution.py:831
  205.3 16.9 %collective-permute-start.35 = (bf16[48,1920]{1,0:T(8,128)(2,1)}, bf16[48,1920]{1,0:T(8,128)(2,1)}, u32[]{:S(2)}, u32[]{:S(2)}) collective-permute-start(bf16[48,1920]{1,0:T(8,128)(2,1)} %constant_dynamic-slice_fusion.1), channel_id=1, source_target_pairs={{0,16},{2,18},{4,20},{6,22},{8,24},{10,26},{12,28},{14,30},{16,0},... | collective-permute-start | bytes 552968 | tf_op jit(solution)/shard_map/ppermute | solution.py:831
  214.2 11.0 %collective-permute-start.34 = (bf16[1,8,64,384]{3,2,1,0:T(8,128)(2,1)S(1)}, bf16[1,8,64,384]{3,2,1,0:T(8,128)(2,1)S(1)}, u32[]{:S(2)}, u32[]{:S(2)}) collective-permute-start(bf16[1,8,64,384]{3,2,1,0:T(8,128)(2,1)S(1)} %get-tuple-element.257), channel_id=1, source_target_pairs={{0,4},{2,6},{4,0},{6,2},{8,12},{10,14},{12,8},{14,10},{16,20},{18,... | collective-permute-start | bytes 1179656 | tf_op jit(solution)/shard_map/ppermute | solution.py:831
  231.4 8.1 %collective-permute-start.42 = (bf16[192,576]{1,0:T(8,128)(2,1)S(1)}, bf16[192,576]{1,0:T(8,128)(2,1)S(1)}, u32[]{:S(2)}, u32[]{:S(2)}) collective-permute-start(bf16[192,576]{1,0:T(8,128)(2,1)S(1)} %dynamic-slice_convert_fusion), channel_id=1, source_target_pairs={{0,4},{2,6},{4,0},{6,2},{8,12},{10,14},{12,8},{14,10},{16,20},{18,... | collective-permute-start | bytes 663560 | tf_op jit(solution)/shard_map/ppermute | solution.py:831
  232.4 12.3 %collective-permute-start.43 = (bf16[1,48,1920]{2,1,0:T(8,128)(2,1)S(1)}, bf16[1,48,1920]{2,1,0:T(8,128)(2,1)S(1)}, u32[]{:S(2)}, u32[]{:S(2)}) collective-permute-start(bf16[1,48,1920]{2,1,0:T(8,128)(2,1)S(1)} %copy-done.35), channel_id=1, source_target_pairs={{0,16},{2,18},{4,20},{6,22},{8,24},{10,26},{12,28},{14,30},{16,0},... | collective-permute-start | bytes 552968 | tf_op jit(solution)/shard_map/ppermute | solution.py:831
  233.7 16.6 %collective-permute-start.44 = (bf16[2,2,96,384]{3,2,1,0:T(8,128)(2,1)S(1)}, bf16[2,2,96,384]{3,2,1,0:T(8,128)(2,1)S(1)}, u32[]{:S(2)}, u32[]{:S(2)}) collective-permute-start(bf16[2,2,96,384]{3,2,1,0:T(8,128)(2,1)S(1)} %copy-done.37), channel_id=1, source_target_pairs={{0,8},{2,10},{4,12},{6,14},{8,0},{10,2},{12,4},{14,6},{16,24},{18,... | collective-permute-start | bytes 884744 | tf_op jit(solution)/shard_map/ppermute | solution.py:831
  234.3 19.5 %collective-permute-start.37 = (bf16[216,384]{1,0:T(8,128)(2,1)S(1)}, bf16[216,384]{1,0:T(8,128)(2,1)S(1)}, u32[]{:S(2)}, u32[]{:S(2)}) collective-permute-start(bf16[216,384]{1,0:T(8,128)(2,1)S(1)} %copy-done.3), channel_id=1, source_target_pairs={{0,8},{2,10},{4,12},{6,14},{8,0},{10,2},{12,4},{14,6},{16,24},{18,... | collective-permute-start | bytes 497672 | tf_op jit(solution)/shard_map/ppermute | solution.py:831
  235.7 20.5 %collective-permute-start.38 = (bf16[216,384]{1,0:T(8,128)(2,1)S(1)}, bf16[216,384]{1,0:T(8,128)(2,1)S(1)}, u32[]{:S(2)}, u32[]{:S(2)}) collective-permute-start(bf16[216,384]{1,0:T(8,128)(2,1)S(1)} %get-tuple-element.185), channel_id=1, source_target_pairs={{0,16},{2,18},{4,20},{6,22},{8,24},{10,26},{12,28},{14,30},{16,0},... | collective-permute-start | bytes 497672 | tf_op jit(solution)/shard_map/ppermute | solution.py:831
  239.5 19.2 %collective-permute-start.39 = (bf16[216,384]{1,0:T(8,128)(2,1)S(1)}, bf16[216,384]{1,0:T(8,128)(2,1)S(1)}, u32[]{:S(2)}, u32[]{:S(2)}) collective-permute-start(bf16[216,384]{1,0:T(8,128)(2,1)S(1)} %get-tuple-element.186), channel_id=1, source_target_pairs={{0,24},{2,26},{4,28},{6,30},{8,16},{10,18},{12,20},{14,22},{16,8},... | collective-permute-start | bytes 497672 | tf_op jit(solution)/shard_map/ppermute | solution.py:831
  244.7 7.1 %collective-permute-start.45 = (bf16[192,576]{1,0:T(8,128)(2,1)S(1)}, bf16[192,576]{1,0:T(8,128)(2,1)S(1)}, u32[]{:S(2)}, u32[]{:S(2)}) collective-permute-start(bf16[192,576]{1,0:T(8,128)(2,1)S(1)} %get-tuple-element.234), channel_id=1, source_target_pairs={{0,1},{1,0},{2,3},{3,2},{4,5},{5,4},{6,7},{7,6},{8,9},{9,8},{10,11... | collective-permute-start | bytes 663560 | tf_op jit(solution)/shard_map/ppermute | solution.py:834
  250.3 12.4 %collective-permute-start.48 = (f32[80,128]{1,0:T(8,128)S(1)}, f32[80,128]{1,0:T(8,128)S(1)}, u32[]{:S(2)}, u32[]{:S(2)}) collective-permute-start(f32[80,128]{1,0:T(8,128)S(1)} %add.370), channel_id=1, source_target_pairs={{0,4},{2,6},{4,0},{6,2},{8,12},{10,14},{12,8},{14,10},{16,20},{18,... | collective-permute-start | bytes 122888 | tf_op jit(solution)/shard_map/ppermute | solution.py:831
  251.9 17.6 %collective-permute-start.49 = (bf16[2,48,1920]{2,1,0:T(8,128)(2,1)S(1)}, bf16[2,48,1920]{2,1,0:T(8,128)(2,1)S(1)}, u32[]{:S(2)}, u32[]{:S(2)}) collective-permute-start(bf16[2,48,1920]{2,1,0:T(8,128)(2,1)S(1)} %constant_dynamic-update-slice_fusion.8), channel_id=1, source_target_pairs={{0,8},{2,10},{4,12},{6,14},{8,0},{10,2},{12,4},{14,6},{16,24},{18,... | collective-permute-start | bytes 1105928 | tf_op jit(solution)/shard_map/ppermute | solution.py:831
  253.8 21.1 %collective-permute-start.52 = (bf16[4,2,96,384]{3,2,1,0:T(8,128)(2,1)S(1)}, bf16[4,2,96,384]{3,2,1,0:T(8,128)(2,1)S(1)}, u32[]{:S(2)}, u32[]{:S(2)}) collective-permute-start(bf16[4,2,96,384]{3,2,1,0:T(8,128)(2,1)S(1)} %constant_dynamic-update-slice_fusion.10), channel_id=1, source_target_pairs={{0,4},{2,6},{4,0},{6,2},{8,12},{10,14},{12,8},{14,10},{16,20},{18,... | collective-permute-start | bytes 1769480 | tf_op jit(solution)/shard_map/ppermute | solution.py:831
  259.5 12.4 %collective-permute-start.50 = (bf16[192,576]{1,0:T(8,128)(2,1)S(1)}, bf16[192,576]{1,0:T(8,128)(2,1)S(1)}, u32[]{:S(2)}, u32[]{:S(2)}) collective-permute-start(bf16[192,576]{1,0:T(8,128)(2,1)S(1)} %add_convert_fusion.7), channel_id=1, source_target_pairs={{0,16},{2,18},{4,20},{6,22},{8,24},{10,26},{12,28},{14,30},{16,0},... | collective-permute-start | bytes 663560 | tf_op jit(solution)/shard_map/ppermute | solution.py:831
  262.8 9.3 %collective-permute-start.51 = (f32[80,128]{1,0:T(8,128)S(1)}, f32[80,128]{1,0:T(8,128)S(1)}, u32[]{:S(2)}, u32[]{:S(2)}) collective-permute-start(f32[80,128]{1,0:T(8,128)S(1)} %add.377), channel_id=1, source_target_pairs={{0,8},{2,10},{4,12},{6,14},{8,0},{10,2},{12,4},{14,6},{16,24},{18,... | collective-permute-start | bytes 122888 | tf_op jit(solution)/shard_map/ppermute | solution.py:831
  269.5 17.1 %collective-permute-start.55 = (bf16[4,48,1920]{2,1,0:T(8,128)(2,1)S(1)}, bf16[4,48,1920]{2,1,0:T(8,128)(2,1)S(1)}, u32[]{:S(2)}, u32[]{:S(2)}) collective-permute-start(bf16[4,48,1920]{2,1,0:T(8,128)(2,1)S(1)} %constant_dynamic-update-slice_fusion.12), channel_id=1, source_target_pairs={{0,4},{2,6},{4,0},{6,2},{8,12},{10,14},{12,8},{14,10},{16,20},{18,... | collective-permute-start | bytes 2211848 | tf_op jit(solution)/shard_map/ppermute | solution.py:831
  286.7 16.1 %collective-permute-start.60 = (bf16[8,2,96,384]{3,2,1,0:T(8,128)(2,1)S(1)}, bf16[8,2,96,384]{3,2,1,0:T(8,128)(2,1)}, u32[]{:S(2)}, u32[]{:S(2)}) collective-permute-start(bf16[8,2,96,384]{3,2,1,0:T(8,128)(2,1)S(1)} %constant_dynamic-update-slice_fusion.14.near_ref), channel_id=1, source_target_pairs={{0,2},{2,0},{4,6},{6,4},{8,10},{10,8},{12,14},{14,12},{16,18},{18,... | collective-permute-start | bytes 3538952 | tf_op jit(solution)/shard_map/ppermute | solution.py:831
  287.3 13.2 %collective-permute-start.58 = (bf16[1,2,192,576]{3,2,1,0:T(8,128)(2,1)S(1)}, bf16[1,2,192,576]{3,2,1,0:T(8,128)(2,1)S(1)}, u32[]{:S(2)}, u32[]{:S(2)}) collective-permute-start(bf16[1,2,192,576]{3,2,1,0:T(8,128)(2,1)S(1)} %maximum_bitcast_fusion), channel_id=1, source_target_pairs={{0,4},{2,6},{4,0},{6,2},{8,12},{10,14},{12,8},{14,10},{16,20},{18,... | collective-permute-start | bytes 1327112 | tf_op jit(solution)/shard_map/ppermute | solution.py:831
  289.6 8.5 %collective-permute-start.57 = (f32[80,128]{1,0:T(8,128)S(1)}, f32[80,128]{1,0:T(8,128)S(1)}, u32[]{:S(2)}, u32[]{:S(2)}) collective-permute-start(f32[80,128]{1,0:T(8,128)S(1)} %add.379), channel_id=1, source_target_pairs={{0,1},{1,0},{2,3},{3,2},{4,5},{5,4},{6,7},{7,6},{8,9},{9,8},{10,11... | collective-permute-start | bytes 122888 | tf_op jit(solution)/shard_map/ppermute | solution.py:834
  301.4 9.5 %collective-permute-start.59 = (bf16[2,2,192,576]{3,2,1,0:T(8,128)(2,1)}, bf16[2,2,192,576]{3,2,1,0:T(8,128)(2,1)}, u32[]{:S(2)}, u32[]{:S(2)}) collective-permute-start(bf16[2,2,192,576]{3,2,1,0:T(8,128)(2,1)} %constant_dynamic-update-slice_fusion.18.near_ref), channel_id=1, source_target_pairs={{0,2},{2,0},{4,6},{6,4},{8,10},{10,8},{12,14},{14,12},{16,18},{18,... | collective-permute-start | bytes 2654216 | tf_op jit(solution)/shard_map/ppermute | solution.py:831
  (74 other events, 462.5 us)

commit v3 on v2

--- a/solution.py
+++ b/solution.py
@@ -133,7 +133,7 @@
             TILE // GROUP,
             bias_group,
             tuple(jnp.full((8, 128), NEGATIVE, F32) for _ in range(chunks * heads)),
-            unroll=8,
+            unroll=4,
         )
         for chunk in range(chunks):
             lanes = slice(offset + chunk * 128, offset + chunk * 128 + 128)
@@ -468,7 +468,7 @@
             dimension_semantics=("arbitrary",), vmem_limit_bytes=58 << 20
         ),
         cost_estimate=pl.CostEstimate(
-            flops=8 << 30, bytes_accessed=6 << 20, transcendentals=1 << 18
+            flops=5 << 30, bytes_accessed=6 << 20, transcendentals=1 << 18
         ),
         name="attention_backward",
     )(exps, buckets, lows, maxima, totals, query256, grad256, mixed_t, keys_values, *carried)

time: 322 us -> 317 us (0.984)
  local copies, waits for them, and re-layouts: 29.1 us -> 23 us
    ppermute x47, waiting for transfers between devices: 59.3 us -> 63.4 us  [swap(): return lax.ppermute(value, 'ctx', [(i, i ^ bit) for i in range(ctx)])]
    unnamed x139 -> x131, local copies, waits for them, and re-layouts: 7.97 us -> 6.25 us
  transfers between devices with their start and end apart: 61 -> 61, of which waited for: 26 -> 25; matrix products, arithmetic and copies ran while one was open for 22% -> 20% of each run, Pallas kernels for 22% -> 23%
where the time goes in v3:
time: 317 us; the launch traced here: 313 us
  Pallas kernels  87.1 us (27%)
  waiting for transfers between devices  79.4 us (25%)
  starting transfers between devices  64.4 us (20%)
  other arithmetic  39.5 us (12%)
  local copies, waits for them, and re-layouts  23 us (7%)
  matrix products  17.4 us (5%)
    ppermute x47, waiting for transfers between devices, swap(): return lax.ppermute(value, 'ctx', [(i, i ^ bit) for i in range(ctx)])  63.4 us
    ppermute x47, starting transfers between devices, swap(): return lax.ppermute(value, 'ctx', [(i, i ^ bit) for i in range(ctx)])  46.8 us
    pallas_call x4, Pallas kernels, attention_backward(): pl.pallas_call(functools.partial(backward_kernel, branch, heads), grid=(t...  41.1 us
    pallas_call x2, Pallas kernels, attention_forward(): pl.pallas_call(functools.partial(forward_kernel, call, count, heads), gri...  22.9 us
    ppermute x14, starting transfers between devices, swap_side(): return lax.ppermute(value, 'wt', [(0, 1), (1, 0)])  17.6 us
    ppermute x14, waiting for transfers between devices, swap_side(): return lax.ppermute(value, 'wt', [(0, 1), (1, 0)])  16 us
    pallas_call x2, Pallas kernels, widen_rows(): pl.pallas_call(functools.partial(widen_kernel, group), grid_spec=pltpu.Pr...  10.7 us
    dot_general x5, matrix products, dot(): return jnp.dot(left, right, preferred_element_type=F32)  7.08 us
  transfers between devices with their start and end apart: 61, of which 25 were waited for; matrix products, arithmetic and copies ran while one was open for 20% of the time, Pallas kernels for 23%

profile of v3, /device:TPU:0, one launch (start us, length us, event | category | flops | bytes accessed | tf_op | source)
XLA Modules:
  0.0 313.5 jit_solution(12951449098708785384)
XLA Ops:
  0.7 1.8 pad_maximum_fusion.30
  2.5 4.0 %collective-permute-start.1 = (bf16[152,768]{1,0:T(8,128)(2,1)}, bf16[152,768]{1,0:T(8,128)(2,1)}, u32[]{:S(2)}, u32[]{:S(2)}) collective-permute-start(bf16[152,768]{1,0:T(8,128)(2,1)} %pad_maximum_fusion.30), channel_id=1, source_target_pairs={{0,16},{2,18},{4,20},{6,22},{8,24},{10,26},{12,28},{14,30},{16,0},... | collective-permute-start | bytes 700424 | tf_op jit(solution)/shard_map/ppermute | solution.py:831
  21.6 2.0 unpack_vectors.1
  29.1 2.0 collective-permute-done.4
  40.2 4.5 %collective-permute-done.6 = bf16[1,8,64,384]{3,2,1,0:T(8,128)(2,1)S(1)} collective-permute-done((bf16[1,8,64,384]{3,2,1,0:T(8,128)(2,1)S(1)}, bf16[1,8,64,384]{3,2,1,0:T(8,128)(2,1)S(1)}, u32[]{:S(2)}, u32[]{:S(2)}) %collective-permute-start.6) | collective-permute-done | bytes 393248 | tf_op jit(solution)/shard_map/ppermute | solution.py:831
  45.2 11.3 %attention_forward.2 = (f32[3,2048,640]{2,1,0:T(8,128)}, bf16[2048,640]{1,0:T(8,128)(2,1)S(1)}, bf16[2048,640]{1,0:T(8,128)(2,1)S(1)}, f32[8,8,640]{2,1,0:T(8,12...) custom-call(s32[32]{0:T(128)S(1)} %reshape.332.refs_0_, ...), custom_call_target="tpu_custom_call" | custom-call | flops 15032385536 | bytes 12582912 | tf_op jit(solution)/shard_map/attention_forward/pallas_call | solution.py:243
  56.6 11.6 %attention_forward.3 = (f32[3,2048,640]{2,1,0:T(8,128)}, bf16[2048,640]{1,0:T(8,128)(2,1)S(1)}, bf16[2048,640]{1,0:T(8,128)(2,1)S(1)}, f32[8,8,640]{2,1,0:T(8,12...) custom-call(s32[32]{0:T(128)S(1)} %reshape.332.refs_0_, ...), custom_call_target="tpu_custom_call", output_to_operand_aliasing={{0}: (6, {}), {1}: (7, {}), {2}: (8, {}), {3}: (9, {})} | custom-call | flops 15032385536 | bytes 12582912 | tf_op jit(solution)/shard_map/attention_forward/pallas_call | solution.py:243
  69.8 3.0 collective-permute-start.10
  77.3 2.5 collective-permute-done.9
  85.9 4.0 %collective-permute-done.14 = bf16[152,768]{1,0:T(8,128)(2,1)S(1)} collective-permute-done((bf16[152,768]{1,0:T(8,128)(2,1)S(1)}, bf16[152,768]{1,0:T(8,128)(2,1)S(1)}, u32[]{:S(2)}, u32[]{:S(2)}) %collective-permute-start.14) | collective-permute-done | bytes 233504 | tf_op jit(solution)/shard_map/ppermute | solution.py:834
  89.9 4.6 %multiply_convert_fusion = (bf16[304,1536]{1,0:T(8,128)(2,1)S(1)}, f32[304,1536]{1,0:T(8,128)S(1)}, f32[304,1536]{1,0:T(8,128)S(1)}) fusion(f32[1536]{0:T(1024)S(1)} %convert_element_type.227, bf16[768,1536]{1,0:T(8,128)(2,1)S(1)} %copy-done, bf16[152,768]{1,0:T(8,128)(2,1)S(1)} %collective-permute-done.14, bf16[152,768]{1,0:T(8,128)(2,1)S(1)} %fusion.50), kind=kOutput, calls=%fused_computation.10 | convolution fusion | flops 748978176 | bytes 7501824 | tf_op jit(solution)/shard_map/dot_general | solution.py:38
  96.1 1.8 collective-permute-start.17
  99.3 3.6 %collective-permute-done.17 = bf16[152,768]{1,0:T(8,128)(2,1)S(1)} collective-permute-done((bf16[152,768]{1,0:T(8,128)(2,1)S(1)}, bf16[152,768]{1,0:T(8,128)(2,1)S(1)}, u32[]{:S(2)}, u32[]{:S(2)}) %collective-permute-start.17) | collective-permute-done | bytes 233504 | tf_op jit(solution)/shard_map/ppermute | solution.py:834
  105.9 1.7 collective-permute-start.18
  109.0 2.9 collective-permute-done.18
  112.0 2.4 convert_reduce_fusion
  115.4 1.8 collective-permute-start.19
  125.1 2.5 collective-permute-start.25
  128.0 2.4 collective-permute-done.25
  132.5 2.1 collective-permute-start.21
  137.4 2.1 collective-permute-start.22
  140.8 2.8 collective-permute-done.22.refs_3_
  144.2 1.9 arrange_rows.1.refs_6_
  146.1 5.2 %collective-permute-done.26 = bf16[384,768]{1,0:T(8,128)(2,1)} collective-permute-done((bf16[384,768]{1,0:T(8,128)(2,1)}, bf16[384,768]{1,0:T(8,128)(2,1)}, u32[]{:S(2)}, u32[]{:S(2)}) %collective-permute-start.26) | collective-permute-done | bytes 589856 | tf_op jit(solution)/shard_map/ppermute | solution.py:831
  156.7 13.1 %attention_backward.4 = (f32[192,640]{1,0:T(8,128)}, f32[128,192]{1,0:T(8,128)}, f32[2,8,64,384]{3,2,1,0:T(8,128)}, bf16[2,8,64,384]{3,2,1,0:T(8,128)(2,1)}) custom-call(f32[3,2048,640]{2,1,0:T(8,128)} %get-tuple-element.139.refs_0_, bf16[2048,640]{1,0:T(8,128)(2,1)} %copy-done.2, bf16[2048,640]{1,0:T(8,128)(2,1)} %copy-done.3, f32[8,8,640]{2,1,0:T(8,128)} %copy-done.6, ...), custom_call_target="tpu_custom_call" | custom-call | flops 5368709120 | bytes 6291456 | tf_op jit(solution)/shard_map/attention_backward/pallas_call | solution.py:438
  169.9 1.9 collective-permute-start.29
  171.8 10.8 %attention_backward.5 = (f32[192,640]{1,0:T(8,128)}, f32[128,192]{1,0:T(8,128)}, f32[2,8,64,384]{3,2,1,0:T(8,128)}, bf16[2,8,64,384]{3,2,1,0:T(8,128)(2,1)}) custom-call(f32[3,2048,640]{2,1,0:T(8,128)} %get-tuple-element.139.refs_0_, bf16[2048,640]{1,0:T(8,128)(2,1)} %copy-done.2, ...), custom_call_target="tpu_custom_call", output_to_operand_aliasing={{2}: (11, {}), {3}: (12, {})} | custom-call | flops 5368709120 | bytes 6291456 | tf_op jit(solution)/shard_map/attention_backward/pallas_call | solution.py:438
  182.7 2.1 collective-permute-start.31
  185.4 9.6 %attention_backward.6 = (f32[192,640]{1,0:T(8,128)}, f32[128,192]{1,0:T(8,128)}, f32[2,8,64,384]{3,2,1,0:T(8,128)}, bf16[2,8,64,384]{3,2,1,0:T(8,128)(2,1)}) custom-call(f32[3,2048,640]{2,1,0:T(8,128)} %get-tuple-element.139.refs_0_, bf16[2048,640]{1,0:T(8,128)(2,1)} %copy-done.2, ...), custom_call_target="tpu_custom_call", output_to_operand_aliasing={{2}: (11, {}), {3}: (12, {})} | custom-call | flops 5368709120 | bytes 6291456 | tf_op jit(solution)/shard_map/attention_backward/pallas_call | solution.py:438
  195.9 7.7 %attention_backward.7 = (f32[192,640]{1,0:T(8,128)}, f32[128,192]{1,0:T(8,128)}, f32[2,8,64,384]{3,2,1,0:T(8,128)}, bf16[2,8,64,384]{3,2,1,0:T(8,128)(2,1)}) custom-call(f32[3,2048,640]{2,1,0:T(8,128)} %get-tuple-element.139.refs_0_, bf16[2048,640]{1,0:T(8,128)(2,1)} %copy-done.2, ...), custom_call_target="tpu_custom_call", output_to_operand_aliasing={{2}: (11, {}), {3}: (12, {})} | custom-call | flops 5368709120 | bytes 6291456 | tf_op jit(solution)/shard_map/attention_backward/pallas_call | solution.py:438
  203.7 1.8 collective-permute-start.36
  212.1 9.9 %collective-permute-done.35 = bf16[48,1920]{1,0:T(8,128)(2,1)} collective-permute-done((bf16[48,1920]{1,0:T(8,128)(2,1)}, bf16[48,1920]{1,0:T(8,128)(2,1)}, u32[]{:S(2)}, u32[]{:S(2)}) %collective-permute-start.35) | collective-permute-done | bytes 184352 | tf_op jit(solution)/shard_map/ppermute | solution.py:831
  224.1 2.1 finish_heads.1
  230.6 1.9 collective-permute-start.44
  232.6 2.7 collective-permute-start.38
  235.4 2.1 collective-permute-done.42
  239.1 2.3 collective-permute-done.43
  241.5 6.4 %collective-permute-done.44 = bf16[2,2,96,384]{3,2,1,0:T(8,128)(2,1)S(1)} collective-permute-done((bf16[2,2,96,384]{3,2,1,0:T(8,128)(2,1)S(1)}, bf16[2,2,96,384]{3,2,1,0:T(8,128)(2,1)S(1)}, u32[]{:S(2)}, u32[]{:S(2)}) %collective-permute-start.44) | collective-permute-done | bytes 294944 | tf_op jit(solution)/shard_map/ppermute | solution.py:831
  252.6 2.9 collective-permute-done.39
  260.2 2.5 collective-permute-start.51
  262.8 3.7 %collective-permute-done.49 = bf16[2,48,1920]{2,1,0:T(8,128)(2,1)S(1)} collective-permute-done((bf16[2,48,1920]{2,1,0:T(8,128)(2,1)S(1)}, bf16[2,48,1920]{2,1,0:T(8,128)(2,1)S(1)}, u32[]{:S(2)}, u32[]{:S(2)}) %collective-permute-start.49) | collective-permute-done | bytes 368672 | tf_op jit(solution)/shard_map/ppermute | solution.py:831
  268.8 2.9 collective-permute-start.54
  272.0 3.6 %collective-permute-done.53 = bf16[1,192,576]{2,1,0:T(8,128)(2,1)S(1)} collective-permute-done((bf16[1,192,576]{2,1,0:T(8,128)(2,1)S(1)}, bf16[1,192,576]{2,1,0:T(8,128)(2,1)S(1)}, u32[]{:S(2)}, u32[]{:S(2)}) %collective-permute-start.53) | collective-permute-done | bytes 221216 | tf_op jit(solution)/shard_map/ppermute | solution.py:831
  275.7 8.3 %collective-permute-done.55 = bf16[4,48,1920]{2,1,0:T(8,128)(2,1)S(1)} collective-permute-done((bf16[4,48,1920]{2,1,0:T(8,128)(2,1)S(1)}, bf16[4,48,1920]{2,1,0:T(8,128)(2,1)S(1)}, u32[]{:S(2)}, u32[]{:S(2)}) %collective-permute-start.55) | collective-permute-done | bytes 737312 | tf_op jit(solution)/shard_map/ppermute | solution.py:831
  289.0 5.5 %widen_rows.2 = (f32[768,1536]{1,0:T(8,128)}, f32[768,384]{1,0:T(8,128)}) custom-call(s32[2]{0:T(128)S(1)} %pad_add_fusion.8.order_ref, bf16[8,48,1920]{2,1,0:T(8,128)(2,1)S(1)} %constant_dynamic-update-slice_fusion.16.near_ref, bf16[8,48,1920]{2,1,0:T(8,128)(2,1)} %collective-permute-done.56.far_ref), custom_call_target="tpu_custom_call" | custom-call | bytes 8847360 | tf_op jit(solution)/shard_map/widen_rows/pallas_call | solution.py:557
  295.4 2.6 collective-permute-done.58
  300.3 5.2 %widen_rows.3 = f32[2,1536,384]{2,1,0:T(8,128)} custom-call(s32[2]{0:T(128)S(1)} %pad_add_fusion.8.order_ref, bf16[8,2,96,384]{3,2,1,0:T(8,128)(2,1)S(1)} %constant_dynamic-update-slice_fusion.14.near_ref, bf16[8,2,96,384]{3,2,1,0:T(8,128)(2,1)} %collective-permute-done.60.far_ref), custom_call_target="tpu_custom_call" | custom-call | bytes 7077888 | tf_op jit(solution)/shard_map/widen_rows/pallas_call | solution.py:557
  308.3 5.0 %widen_heads.1 = (f32[768,384]{1,0:T(8,128)}, f32[768,384]{1,0:T(8,128)}, f32[768,384]{1,0:T(8,128)}) custom-call(s32[2]{0:T(128)} %pad_add_fusion.7.order_ref, bf16[2,2,192,576]{3,2,1,0:T(8,128)(2,1)} %constant_dynamic-update-slice_fusion.18.near_ref, bf16[2,2,192,576]{3,2,1,0:T(8,128)(2,1)} %collective-permute-done.59.far_ref), custom_call_target="tpu_custom_call" | custom-call | bytes 5308416 | tf_op jit(solution)/shard_map/widen_heads/pallas_call | solution.py:605
  (444 shorter events, 109.7 us)
Async XLA Ops:
  2.5 23.5 %collective-permute-start.1 = (bf16[152,768]{1,0:T(8,128)(2,1)}, bf16[152,768]{1,0:T(8,128)(2,1)}, u32[]{:S(2)}, u32[]{:S(2)}) collective-permute-start(bf16[152,768]{1,0:T(8,128)(2,1)} %pad_maximum_fusion.30), channel_id=1, source_target_pairs={{0,16},{2,18},{4,20},{6,22},{8,24},{10,26},{12,28},{14,30},{16,0},... | collective-permute-start | bytes 700424 | tf_op jit(solution)/shard_map/ppermute | solution.py:831
  6.5 19.5 %collective-permute-start = (bf16[152,768]{1,0:T(8,128)(2,1)}, bf16[152,768]{1,0:T(8,128)(2,1)}, u32[]{:S(2)}, u32[]{:S(2)}) collective-permute-start(bf16[152,768]{1,0:T(8,128)(2,1)} %pad_maximum_fusion.30), channel_id=1, source_target_pairs={{0,24},{2,26},{4,28},{6,30},{8,16},{10,18},{12,20},{14,22},{16,8},... | collective-permute-start | bytes 700424 | tf_op jit(solution)/shard_map/ppermute | solution.py:831
  7.9 18.1 %collective-permute-start.2 = (bf16[152,768]{1,0:T(8,128)(2,1)}, bf16[152,768]{1,0:T(8,128)(2,1)}, u32[]{:S(2)}, u32[]{:S(2)}) collective-permute-start(bf16[152,768]{1,0:T(8,128)(2,1)} %pad_maximum_fusion.30), channel_id=1, source_target_pairs={{0,8},{2,10},{4,12},{6,14},{8,0},{10,2},{12,4},{14,6},{16,24},{18,... | collective-permute-start | bytes 700424 | tf_op jit(solution)/shard_map/ppermute | solution.py:831
  9.6 11.4 %collective-permute-start.5 = (bf16[32,384]{1,0:T(8,128)(2,1)}, bf16[32,384]{1,0:T(8,128)(2,1)S(1)}, u32[]{:S(2)}, u32[]{:S(2)}) collective-permute-start(bf16[32,384]{1,0:T(8,128)(2,1)} %pack_vectors.1.own_ref), channel_id=1, source_target_pairs={{0,1},{1,0},{2,3},{3,2},{4,5},{5,4},{6,7},{7,6},{8,9},{9,8},{10,11... | collective-permute-start | bytes 73736 | tf_op jit(solution)/shard_map/ppermute | solution.py:834
  16.6 12.4 %collective-permute-start.3 = (bf16[384,576]{1,0:T(8,128)(2,1)}, bf16[384,576]{1,0:T(8,128)(2,1)}, u32[]{:S(2)}, u32[]{:S(2)}) collective-permute-start(bf16[384,576]{1,0:T(8,128)(2,1)} %constant_dynamic-slice_fusion.11), channel_id=1, source_target_pairs={{0,1},{1,0},{2,3},{3,2},{4,5},{5,4},{6,7},{7,6},{8,9},{9,8},{10,11... | collective-permute-start | bytes 1327112 | tf_op jit(solution)/shard_map/ppermute | solution.py:834
  33.5 11.2 %collective-permute-start.6 = (bf16[1,8,64,384]{3,2,1,0:T(8,128)(2,1)S(1)}, bf16[1,8,64,384]{3,2,1,0:T(8,128)(2,1)S(1)}, u32[]{:S(2)}, u32[]{:S(2)}) collective-permute-start(bf16[1,8,64,384]{3,2,1,0:T(8,128)(2,1)S(1)} %bitcast.103), channel_id=1, source_target_pairs={{0,4},{2,6},{4,0},{6,2},{8,12},{10,14},{12,8},{14,10},{16,20},{18,... | collective-permute-start | bytes 1179656 | tf_op jit(solution)/shard_map/ppermute | solution.py:831
  35.0 9.7 %collective-permute-start.8 = (bf16[1,8,64,384]{3,2,1,0:T(8,128)(2,1)S(1)}, bf16[1,8,64,384]{3,2,1,0:T(8,128)(2,1)S(1)}, u32[]{:S(2)}, u32[]{:S(2)}) collective-permute-start(bf16[1,8,64,384]{3,2,1,0:T(8,128)(2,1)S(1)} %bitcast.104), channel_id=1, source_target_pairs={{0,2},{2,0},{4,6},{6,4},{8,10},{10,8},{12,14},{14,12},{16,18},{18,... | collective-permute-start | bytes 1179656 | tf_op jit(solution)/shard_map/ppermute | solution.py:831
  36.7 37.4 %collective-permute-start.12 = (bf16[384,384]{1,0:T(8,128)(2,1)S(1)}, bf16[384,384]{1,0:T(8,128)(2,1)S(1)}, u32[]{:S(2)}, u32[]{:S(2)}) collective-permute-start(bf16[384,384]{1,0:T(8,128)(2,1)S(1)} %constant_dynamic-slice_fusion.8), channel_id=1, source_target_pairs={{0,1},{1,0},{2,3},{3,2},{4,5},{5,4},{6,7},{7,6},{8,9},{9,8},{10,11... | collective-permute-start | bytes 884744 | tf_op jit(solution)/shard_map/ppermute | solution.py:834
  38.0 37.5 %collective-permute-start.15 = (bf16[768,384]{1,0:T(8,128)(2,1)S(1)}, bf16[768,384]{1,0:T(8,128)(2,1)S(1)}, u32[]{:S(2)}, u32[]{:S(2)}) collective-permute-start(bf16[768,384]{1,0:T(8,128)(2,1)S(1)} %constant_dynamic-slice_fusion.7), channel_id=1, source_target_pairs={{0,1},{1,0},{2,3},{3,2},{4,5},{5,4},{6,7},{7,6},{8,9},{9,8},{10,11... | collective-permute-start | bytes 1769480 | tf_op jit(solution)/shard_map/ppermute | solution.py:834
  39.0 36.6 %collective-permute-start.46 = (bf16[384,576]{1,0:T(8,128)(2,1)S(1)}, bf16[384,576]{1,0:T(8,128)(2,1)S(1)}, u32[]{:S(2)}, u32[]{:S(2)}) collective-permute-start(bf16[384,576]{1,0:T(8,128)(2,1)S(1)} %constant_dynamic-slice_fusion), channel_id=1, source_target_pairs={{0,1},{1,0},{2,3},{3,2},{4,5},{5,4},{6,7},{7,6},{8,9},{9,8},{10,11... | collective-permute-start | bytes 1327112 | tf_op jit(solution)/shard_map/ppermute | solution.py:834
  44.7 11.8 %collective-permute-start.7 = (bf16[1,8,64,384]{3,2,1,0:T(8,128)(2,1)S(1)}, bf16[1,8,64,384]{3,2,1,0:T(8,128)(2,1)S(1)}, u32[]{:S(2)}, u32[]{:S(2)}) collective-permute-start(bf16[1,8,64,384]{3,2,1,0:T(8,128)(2,1)S(1)} %collective-permute-done.6), channel_id=1, source_target_pairs={{0,2},{2,0},{4,6},{6,4},{8,10},{10,8},{12,14},{14,12},{16,18},{18,... | collective-permute-start | bytes 1179656 | tf_op jit(solution)/shard_map/ppermute | solution.py:831
  69.8 7.5 %collective-permute-start.10 = (bf16[88,384]{1,0:T(8,128)(2,1)S(1)}, bf16[88,384]{1,0:T(8,128)(2,1)S(1)}, u32[]{:S(2)}, u32[]{:S(2)}) collective-permute-start(bf16[88,384]{1,0:T(8,128)(2,1)S(1)} %broadcast_select_fusion.66), channel_id=1, source_target_pairs={{0,16},{2,18},{4,20},{6,22},{8,24},{10,26},{12,28},{14,30},{16,0},... | collective-permute-start | bytes 202760 | tf_op jit(solution)/shard_map/ppermute | solution.py:831
  72.9 6.8 %collective-permute-start.9 = (bf16[88,384]{1,0:T(8,128)(2,1)S(1)}, bf16[88,384]{1,0:T(8,128)(2,1)S(1)}, u32[]{:S(2)}, u32[]{:S(2)}) collective-permute-start(bf16[88,384]{1,0:T(8,128)(2,1)S(1)} %broadcast_select_fusion.67), channel_id=1, source_target_pairs={{0,24},{2,26},{4,28},{6,30},{8,16},{10,18},{12,20},{14,22},{16,8},... | collective-permute-start | bytes 202760 | tf_op jit(solution)/shard_map/ppermute | solution.py:831
  75.7 18.9 %collective-permute-start.16 = (bf16[768,384]{1,0:T(8,128)(2,1)S(1)}, bf16[768,384]{1,0:T(8,128)(2,1)S(1)}, u32[]{:S(2)}, u32[]{:S(2)}) collective-permute-start(bf16[768,384]{1,0:T(8,128)(2,1)S(1)} %collective-permute-done.15), channel_id=1, source_target_pairs={{0,2},{2,0},{4,6},{6,4},{8,10},{10,8},{12,14},{14,12},{16,18},{18,... | collective-permute-start | bytes 1769480 | tf_op jit(solution)/shard_map/ppermute | solution.py:831
  77.3 6.9 %collective-permute-start.47 = (bf16[384,576]{1,0:T(8,128)(2,1)S(1)}, bf16[384,576]{1,0:T(8,128)(2,1)S(1)}, u32[]{:S(2)}, u32[]{:S(2)}) collective-permute-start(bf16[384,576]{1,0:T(8,128)(2,1)S(1)} %collective-permute-done.46), channel_id=1, source_target_pairs={{0,2},{2,0},{4,6},{6,4},{8,10},{10,8},{12,14},{14,12},{16,18},{18,... | collective-permute-start | bytes 1327112 | tf_op jit(solution)/shard_map/ppermute | solution.py:831
  82.5 7.4 %collective-permute-start.14 = (bf16[152,768]{1,0:T(8,128)(2,1)S(1)}, bf16[152,768]{1,0:T(8,128)(2,1)S(1)}, u32[]{:S(2)}, u32[]{:S(2)}) collective-permute-start(bf16[152,768]{1,0:T(8,128)(2,1)S(1)} %fusion.50), channel_id=1, source_target_pairs={{0,1},{1,0},{2,3},{3,2},{4,5},{5,4},{6,7},{7,6},{8,9},{9,8},{10,11... | collective-permute-start | bytes 700424 | tf_op jit(solution)/shard_map/ppermute | solution.py:834
  115.4 7.2 %collective-permute-start.19 = (bf16[152,768]{1,0:T(8,128)(2,1)S(1)}, bf16[152,768]{1,0:T(8,128)(2,1)S(1)}, u32[]{:S(2)}, u32[]{:S(2)}) collective-permute-start(bf16[152,768]{1,0:T(8,128)(2,1)S(1)} %slice.1018), channel_id=1, source_target_pairs={{0,1},{1,0},{2,3},{3,2},{4,5},{5,4},{6,7},{7,6},{8,9},{9,8},{10,11... | collective-permute-start | bytes 700424 | tf_op jit(solution)/shard_map/ppermute | solution.py:834
  118.0 16.6 %collective-permute-start.23 = (bf16[768,768]{1,0:T(8,128)(2,1)S(1)}, bf16[768,768]{1,0:T(8,128)(2,1)S(1)}, u32[]{:S(2)}, u32[]{:S(2)}) collective-permute-start(bf16[768,768]{1,0:T(8,128)(2,1)S(1)} %convolution_convert_fusion.2), channel_id=1, source_target_pairs={{0,2},{2,0},{4,6},{6,4},{8,10},{10,8},{12,14},{14,12},{16,18},{18,... | collective-permute-start | bytes 3538952 | tf_op jit(solution)/shard_map/ppermute | solution.py:831
  118.1 9.7 %collective-permute-start.24 = (bf16[152,768]{1,0:T(8,128)(2,1)S(1)}, bf16[152,768]{1,0:T(8,128)(2,1)S(1)}, u32[]{:S(2)}, u32[]{:S(2)}) collective-permute-start(bf16[152,768]{1,0:T(8,128)(2,1)S(1)} %maximum_maximum_fusion), channel_id=1, source_target_pairs={{0,1},{1,0},{2,3},{3,2},{4,5},{5,4},{6,7},{7,6},{8,9},{9,8},{10,11... | collective-permute-start | bytes 700424 | tf_op jit(solution)/shard_map/ppermute | solution.py:834
  132.0 21.4 %collective-permute-start.27 = (bf16[384,1920]{1,0:T(8,128)(2,1)}, bf16[384,1920]{1,0:T(8,128)(2,1)}, u32[]{:S(2)}, u32[]{:S(2)}) collective-permute-start(bf16[384,1920]{1,0:T(8,128)(2,1)} %pad_maximum_fusion.6), channel_id=1, source_target_pairs={{0,2},{2,0},{4,6},{6,4},{8,10},{10,8},{12,14},{14,12},{16,18},{18,... | collective-permute-start | bytes 4423688 | tf_op jit(solution)/shard_map/ppermute | solution.py:831
  132.2 8.6 %collective-permute-start.20 = (bf16[88,384]{1,0:T(8,128)(2,1)S(1)}, bf16[88,384]{1,0:T(8,128)(2,1)S(1)}, u32[]{:S(2)}, u32[]{:S(2)}) collective-permute-start(bf16[88,384]{1,0:T(8,128)(2,1)S(1)} %broadcast_select_fusion.58), channel_id=1, source_target_pairs={{0,8},{2,10},{4,12},{6,14},{8,0},{10,2},{12,4},{14,6},{16,24},{18,... | collective-permute-start | bytes 202760 | tf_op jit(solution)/shard_map/ppermute | solution.py:831
  132.5 8.2 %collective-permute-start.21 = (bf16[88,384]{1,0:T(8,128)(2,1)S(1)}, bf16[88,384]{1,0:T(8,128)(2,1)S(1)}, u32[]{:S(2)}, u32[]{:S(2)}) collective-permute-start(bf16[88,384]{1,0:T(8,128)(2,1)S(1)} %broadcast_select_fusion.57), channel_id=1, source_target_pairs={{0,16},{2,18},{4,20},{6,22},{8,24},{10,26},{12,28},{14,30},{16,0},... | collective-permute-start | bytes 202760 | tf_op jit(solution)/shard_map/ppermute | solution.py:831
  135.8 15.5 %collective-permute-start.26 = (bf16[384,768]{1,0:T(8,128)(2,1)}, bf16[384,768]{1,0:T(8,128)(2,1)}, u32[]{:S(2)}, u32[]{:S(2)}) collective-permute-start(bf16[384,768]{1,0:T(8,128)(2,1)} %constant_dynamic-slice_fusion.6), channel_id=1, source_target_pairs={{0,4},{2,6},{4,0},{6,2},{8,12},{10,14},{12,8},{14,10},{16,20},{18,... | collective-permute-start | bytes 1769480 | tf_op jit(solution)/shard_map/ppermute | solution.py:831
  152.5 17.3 %collective-permute-start.28 = (bf16[192,768]{1,0:T(8,128)(2,1)S(1)}, bf16[192,768]{1,0:T(8,128)(2,1)S(1)}, u32[]{:S(2)}, u32[]{:S(2)}) collective-permute-start(bf16[192,768]{1,0:T(8,128)(2,1)S(1)} %constant_dynamic-slice_fusion.5), channel_id=1, source_target_pairs={{0,8},{2,10},{4,12},{6,14},{8,0},{10,2},{12,4},{14,6},{16,24},{18,... | collective-permute-start | bytes 884744 | tf_op jit(solution)/shard_map/ppermute | solution.py:831
  155.2 29.6 %collective-permute-start.30 = (bf16[192,1920]{1,0:T(8,128)(2,1)S(1)}, bf16[192,1920]{1,0:T(8,128)(2,1)S(1)}, u32[]{:S(2)}, u32[]{:S(2)}) collective-permute-start(bf16[192,1920]{1,0:T(8,128)(2,1)S(1)} %constant_dynamic-slice_fusion.4), channel_id=1, source_target_pairs={{0,4},{2,6},{4,0},{6,2},{8,12},{10,14},{12,8},{14,10},{16,20},{18,... | collective-permute-start | bytes 2211848 | tf_op jit(solution)/shard_map/ppermute | solution.py:831
  169.9 12.7 %collective-permute-start.29 = (bf16[96,768]{1,0:T(8,128)(2,1)S(1)}, bf16[96,768]{1,0:T(8,128)(2,1)S(1)}, u32[]{:S(2)}, u32[]{:S(2)}) collective-permute-start(bf16[96,768]{1,0:T(8,128)(2,1)S(1)} %constant_dynamic-slice_fusion.3), channel_id=1, source_target_pairs={{0,16},{2,18},{4,20},{6,22},{8,24},{10,26},{12,28},{14,30},{16,0},... | collective-permute-start | bytes 442376 | tf_op jit(solution)/shard_map/ppermute | solution.py:831
  182.7 12.3 %collective-permute-start.31 = (bf16[96,384]{1,0:T(8,128)(2,1)S(1)}, bf16[96,384]{1,0:T(8,128)(2,1)S(1)}, u32[]{:S(2)}, u32[]{:S(2)}) collective-permute-start(bf16[96,384]{1,0:T(8,128)(2,1)S(1)} %get-tuple-element.347), channel_id=1, source_target_pairs={{0,1},{1,0},{2,3},{3,2},{4,5},{5,4},{6,7},{7,6},{8,9},{9,8},{10,11... | collective-permute-start | bytes 221192 | tf_op jit(solution)/shard_map/ppermute | solution.py:834
  185.0 10.0 %collective-permute-start.32 = (bf16[96,1920]{1,0:T(8,128)(2,1)S(1)}, bf16[96,1920]{1,0:T(8,128)(2,1)S(1)}, u32[]{:S(2)}, u32[]{:S(2)}) collective-permute-start(bf16[96,1920]{1,0:T(8,128)(2,1)S(1)} %constant_dynamic-slice_fusion.2), channel_id=1, source_target_pairs={{0,8},{2,10},{4,12},{6,14},{8,0},{10,2},{12,4},{14,6},{16,24},{18,... | collective-permute-start | bytes 1105928 | tf_op jit(solution)/shard_map/ppermute | solution.py:831
  203.7 19.3 %collective-permute-start.36 = (bf16[1,2,96,384]{3,2,1,0:T(8,128)(2,1)S(1)}, bf16[1,2,96,384]{3,2,1,0:T(8,128)(2,1)}, u32[]{:S(2)}, u32[]{:S(2)}) collective-permute-start(bf16[1,2,96,384]{3,2,1,0:T(8,128)(2,1)S(1)} %maximum_bitcast_fusion.1), channel_id=1, source_target_pairs={{0,16},{2,18},{4,20},{6,22},{8,24},{10,26},{12,28},{14,30},{16,0},... | collective-permute-start | bytes 442376 | tf_op jit(solution)/shard_map/ppermute | solution.py:831
  205.5 16.5 %collective-permute-start.35 = (bf16[48,1920]{1,0:T(8,128)(2,1)}, bf16[48,1920]{1,0:T(8,128)(2,1)}, u32[]{:S(2)}, u32[]{:S(2)}) collective-permute-start(bf16[48,1920]{1,0:T(8,128)(2,1)} %constant_dynamic-slice_fusion.1), channel_id=1, source_target_pairs={{0,16},{2,18},{4,20},{6,22},{8,24},{10,26},{12,28},{14,30},{16,0},... | collective-permute-start | bytes 552968 | tf_op jit(solution)/shard_map/ppermute | solution.py:831
  211.5 12.5 %collective-permute-start.34 = (bf16[1,8,64,384]{3,2,1,0:T(8,128)(2,1)S(1)}, bf16[1,8,64,384]{3,2,1,0:T(8,128)(2,1)S(1)}, u32[]{:S(2)}, u32[]{:S(2)}) collective-permute-start(bf16[1,8,64,384]{3,2,1,0:T(8,128)(2,1)S(1)} %get-tuple-element.257), channel_id=1, source_target_pairs={{0,4},{2,6},{4,0},{6,2},{8,12},{10,14},{12,8},{14,10},{16,20},{18,... | collective-permute-start | bytes 1179656 | tf_op jit(solution)/shard_map/ppermute | solution.py:831
  229.4 8.1 %collective-permute-start.42 = (bf16[192,576]{1,0:T(8,128)(2,1)S(1)}, bf16[192,576]{1,0:T(8,128)(2,1)S(1)}, u32[]{:S(2)}, u32[]{:S(2)}) collective-permute-start(bf16[192,576]{1,0:T(8,128)(2,1)S(1)} %dynamic-slice_convert_fusion), channel_id=1, source_target_pairs={{0,4},{2,6},{4,0},{6,2},{8,12},{10,14},{12,8},{14,10},{16,20},{18,... | collective-permute-start | bytes 663560 | tf_op jit(solution)/shard_map/ppermute | solution.py:831
  230.3 11.1 %collective-permute-start.43 = (bf16[1,48,1920]{2,1,0:T(8,128)(2,1)S(1)}, bf16[1,48,1920]{2,1,0:T(8,128)(2,1)S(1)}, u32[]{:S(2)}, u32[]{:S(2)}) collective-permute-start(bf16[1,48,1920]{2,1,0:T(8,128)(2,1)S(1)} %fusion.95), channel_id=1, source_target_pairs={{0,16},{2,18},{4,20},{6,22},{8,24},{10,26},{12,28},{14,30},{16,0},... | collective-permute-start | bytes 552968 | tf_op jit(solution)/shard_map/ppermute | solution.py:831
  230.6 17.4 %collective-permute-start.44 = (bf16[2,2,96,384]{3,2,1,0:T(8,128)(2,1)S(1)}, bf16[2,2,96,384]{3,2,1,0:T(8,128)(2,1)S(1)}, u32[]{:S(2)}, u32[]{:S(2)}) collective-permute-start(bf16[2,2,96,384]{3,2,1,0:T(8,128)(2,1)S(1)} %copy-done.28), channel_id=1, source_target_pairs={{0,8},{2,10},{4,12},{6,14},{8,0},{10,2},{12,4},{14,6},{16,24},{18,... | collective-permute-start | bytes 884744 | tf_op jit(solution)/shard_map/ppermute | solution.py:831
  232.5 18.8 %collective-permute-start.37 = (bf16[216,384]{1,0:T(8,128)(2,1)S(1)}, bf16[216,384]{1,0:T(8,128)(2,1)S(1)}, u32[]{:S(2)}, u32[]{:S(2)}) collective-permute-start(bf16[216,384]{1,0:T(8,128)(2,1)S(1)} %get-tuple-element.184), channel_id=1, source_target_pairs={{0,8},{2,10},{4,12},{6,14},{8,0},{10,2},{12,4},{14,6},{16,24},{18,... | collective-permute-start | bytes 497672 | tf_op jit(solution)/shard_map/ppermute | solution.py:831
  232.6 20.0 %collective-permute-start.38 = (bf16[216,384]{1,0:T(8,128)(2,1)S(1)}, bf16[216,384]{1,0:T(8,128)(2,1)S(1)}, u32[]{:S(2)}, u32[]{:S(2)}) collective-permute-start(bf16[216,384]{1,0:T(8,128)(2,1)S(1)} %get-tuple-element.185), channel_id=1, source_target_pairs={{0,16},{2,18},{4,20},{6,22},{8,24},{10,26},{12,28},{14,30},{16,0},... | collective-permute-start | bytes 497672 | tf_op jit(solution)/shard_map/ppermute | solution.py:831
  237.4 18.0 %collective-permute-start.39 = (bf16[216,384]{1,0:T(8,128)(2,1)S(1)}, bf16[216,384]{1,0:T(8,128)(2,1)S(1)}, u32[]{:S(2)}, u32[]{:S(2)}) collective-permute-start(bf16[216,384]{1,0:T(8,128)(2,1)S(1)} %get-tuple-element.186), channel_id=1, source_target_pairs={{0,24},{2,26},{4,28},{6,30},{8,16},{10,18},{12,20},{14,22},{16,8},... | collective-permute-start | bytes 497672 | tf_op jit(solution)/shard_map/ppermute | solution.py:831
  241.4 8.2 %collective-permute-start.45 = (bf16[192,576]{1,0:T(8,128)(2,1)S(1)}, bf16[192,576]{1,0:T(8,128)(2,1)S(1)}, u32[]{:S(2)}, u32[]{:S(2)}) collective-permute-start(bf16[192,576]{1,0:T(8,128)(2,1)S(1)} %get-tuple-element.234), channel_id=1, source_target_pairs={{0,1},{1,0},{2,3},{3,2},{4,5},{5,4},{6,7},{7,6},{8,9},{9,8},{10,11... | collective-permute-start | bytes 663560 | tf_op jit(solution)/shard_map/ppermute | solution.py:834
  247.9 12.3 %collective-permute-start.48 = (f32[80,128]{1,0:T(8,128)S(1)}, f32[80,128]{1,0:T(8,128)S(1)}, u32[]{:S(2)}, u32[]{:S(2)}) collective-permute-start(f32[80,128]{1,0:T(8,128)S(1)} %add.370), channel_id=1, source_target_pairs={{0,4},{2,6},{4,0},{6,2},{8,12},{10,14},{12,8},{14,10},{16,20},{18,... | collective-permute-start | bytes 122888 | tf_op jit(solution)/shard_map/ppermute | solution.py:831
  249.6 16.9 %collective-permute-start.49 = (bf16[2,48,1920]{2,1,0:T(8,128)(2,1)S(1)}, bf16[2,48,1920]{2,1,0:T(8,128)(2,1)S(1)}, u32[]{:S(2)}, u32[]{:S(2)}) collective-permute-start(bf16[2,48,1920]{2,1,0:T(8,128)(2,1)S(1)} %constant_dynamic-update-slice_fusion.8), channel_id=1, source_target_pairs={{0,8},{2,10},{4,12},{6,14},{8,0},{10,2},{12,4},{14,6},{16,24},{18,... | collective-permute-start | bytes 1105928 | tf_op jit(solution)/shard_map/ppermute | solution.py:831
  251.3 20.5 %collective-permute-start.52 = (bf16[4,2,96,384]{3,2,1,0:T(8,128)(2,1)S(1)}, bf16[4,2,96,384]{3,2,1,0:T(8,128)(2,1)S(1)}, u32[]{:S(2)}, u32[]{:S(2)}) collective-permute-start(bf16[4,2,96,384]{3,2,1,0:T(8,128)(2,1)S(1)} %constant_dynamic-update-slice_fusion.10), channel_id=1, source_target_pairs={{0,4},{2,6},{4,0},{6,2},{8,12},{10,14},{12,8},{14,10},{16,20},{18,... | collective-permute-start | bytes 1769480 | tf_op jit(solution)/shard_map/ppermute | solution.py:831
  256.3 12.4 %collective-permute-start.50 = (bf16[192,576]{1,0:T(8,128)(2,1)S(1)}, bf16[192,576]{1,0:T(8,128)(2,1)S(1)}, u32[]{:S(2)}, u32[]{:S(2)}) collective-permute-start(bf16[192,576]{1,0:T(8,128)(2,1)S(1)} %add_convert_fusion.7), channel_id=1, source_target_pairs={{0,16},{2,18},{4,20},{6,22},{8,24},{10,26},{12,28},{14,30},{16,0},... | collective-permute-start | bytes 663560 | tf_op jit(solution)/shard_map/ppermute | solution.py:831
  260.2 8.6 %collective-permute-start.51 = (f32[80,128]{1,0:T(8,128)S(1)}, f32[80,128]{1,0:T(8,128)S(1)}, u32[]{:S(2)}, u32[]{:S(2)}) collective-permute-start(f32[80,128]{1,0:T(8,128)S(1)} %add.377), channel_id=1, source_target_pairs={{0,8},{2,10},{4,12},{6,14},{8,0},{10,2},{12,4},{14,6},{16,24},{18,... | collective-permute-start | bytes 122888 | tf_op jit(solution)/shard_map/ppermute | solution.py:831
  266.5 17.5 %collective-permute-start.55 = (bf16[4,48,1920]{2,1,0:T(8,128)(2,1)S(1)}, bf16[4,48,1920]{2,1,0:T(8,128)(2,1)S(1)}, u32[]{:S(2)}, u32[]{:S(2)}) collective-permute-start(bf16[4,48,1920]{2,1,0:T(8,128)(2,1)S(1)} %constant_dynamic-update-slice_fusion.12), channel_id=1, source_target_pairs={{0,4},{2,6},{4,0},{6,2},{8,12},{10,14},{12,8},{14,10},{16,20},{18,... | collective-permute-start | bytes 2211848 | tf_op jit(solution)/shard_map/ppermute | solution.py:831
  284.2 16.1 %collective-permute-start.60 = (bf16[8,2,96,384]{3,2,1,0:T(8,128)(2,1)S(1)}, bf16[8,2,96,384]{3,2,1,0:T(8,128)(2,1)}, u32[]{:S(2)}, u32[]{:S(2)}) collective-permute-start(bf16[8,2,96,384]{3,2,1,0:T(8,128)(2,1)S(1)} %constant_dynamic-update-slice_fusion.14.near_ref), channel_id=1, source_target_pairs={{0,2},{2,0},{4,6},{6,4},{8,10},{10,8},{12,14},{14,12},{16,18},{18,... | collective-permute-start | bytes 3538952 | tf_op jit(solution)/shard_map/ppermute | solution.py:831
  284.8 13.2 %collective-permute-start.58 = (bf16[1,2,192,576]{3,2,1,0:T(8,128)(2,1)S(1)}, bf16[1,2,192,576]{3,2,1,0:T(8,128)(2,1)S(1)}, u32[]{:S(2)}, u32[]{:S(2)}) collective-permute-start(bf16[1,2,192,576]{3,2,1,0:T(8,128)(2,1)S(1)} %maximum_bitcast_fusion), channel_id=1, source_target_pairs={{0,4},{2,6},{4,0},{6,2},{8,12},{10,14},{12,8},{14,10},{16,20},{18,... | collective-permute-start | bytes 1327112 | tf_op jit(solution)/shard_map/ppermute | solution.py:831
  286.8 7.7 %collective-permute-start.57 = (f32[80,128]{1,0:T(8,128)S(1)}, f32[80,128]{1,0:T(8,128)S(1)}, u32[]{:S(2)}, u32[]{:S(2)}) collective-permute-start(f32[80,128]{1,0:T(8,128)S(1)} %add.379), channel_id=1, source_target_pairs={{0,1},{1,0},{2,3},{3,2},{4,5},{5,4},{6,7},{7,6},{8,9},{9,8},{10,11... | collective-permute-start | bytes 122888 | tf_op jit(solution)/shard_map/ppermute | solution.py:834
  298.8 9.5 %collective-permute-start.59 = (bf16[2,2,192,576]{3,2,1,0:T(8,128)(2,1)}, bf16[2,2,192,576]{3,2,1,0:T(8,128)(2,1)}, u32[]{:S(2)}, u32[]{:S(2)}) collective-permute-start(bf16[2,2,192,576]{3,2,1,0:T(8,128)(2,1)} %constant_dynamic-update-slice_fusion.18.near_ref), channel_id=1, source_target_pairs={{0,2},{2,0},{4,6},{6,4},{8,10},{10,8},{12,14},{14,12},{16,18},{18,... | collective-permute-start | bytes 2654216 | tf_op jit(solution)/shard_map/ppermute | solution.py:831
  (70 other events, 452.1 us)
